TPU v7x, 256 devices: a whole 4x4x8 slice. The times are simulated.
256 devices in a mesh: dp: 16 (over x, z_hi), slab: 16 (over z_lo, y, core).
Axes of the slice: x: 4, y: 4, z: 8 (z_hi: 4, z_lo: 2; z = z_hi * 2 + z_lo), core: 2. Of those that a mesh axis runs over, the one named last changes fastest.
Arguments:
- field: bfloat16 [16, 64, 64, 4096], P('dp', None, 'slab'), may hold values from -6 to 6
- cotangent: bfloat16 [16, 64, 64, 4096], P('dp', None, 'slab'), may hold values from -6 to 6
- spectral_weight: bfloat16 [16, 256, 64, 128], P(None, 'slab'), may hold values from -0.375 to 0.375
- point_weight: bfloat16 [64, 64], replicated, may hold values from -0.75 to 0.75
- bias: float32 [64], replicated, may hold values from -3 to 3
Outputs:
- input_grad: bfloat16 [16, 64, 64, 4096], P('dp', None, 'slab')
- spectral_grad: float32 [16, 256, 64, 128], P('dp', 'slab')
- point_grad: float32 [64, 64], replicated
- bias_grad: float32 [64], replicated
All inputs are finite; a program needn't handle non-finite values.
Results may differ from a plain program's by a relative error of at most 0.015.
Values may be sent and summed in bfloat16 or wider, within the bound.
No kernel may reach another device: no remote copies, remote signals or barrier semaphores. Data moves between devices by JAX's collectives and lax.ppermute only.
A program may use at most 64 MiB of HBM per device.

v0:
```python
import functools
import math

import jax
import jax.numpy as jnp
import numpy as np
from jax import lax
from jax.experimental import pallas as pl
from jax.experimental.pallas import tpu as pltpu
from jax.sharding import PartitionSpec as P

C = 64
N = 64
XL = 4
S = 16
L = 16
CELLS = 4096
ROWS = C * XL
Q = 512
F32 = jnp.float32
BF16 = jnp.bfloat16


def mm(a, b):
    return jnp.dot(a, b, preferred_element_type=F32)


def nt(a, b):
    return lax.dot_general(a, b, (((1,), (1,)), ((), ())), preferred_element_type=F32)


def tn(a, b):
    return lax.dot_general(a, b, (((0,), (0,)), ((), ())), preferred_element_type=F32)


def waves(count, size):
    return np.array([i if i < count // 2 else size - count + i for i in range(count)])


def phase_tables():
    y = np.arange(CELLS) // N
    k = waves(S, N)
    ang = 2.0 * np.pi * ((k[:, None] * y[None, :]) % N) / N
    ang = ang[:, None, :] + np.array([0.0, np.pi / 2])[None, :, None]
    ang = ang.reshape(2 * S, CELLS)
    z = np.arange(128) % N
    angz = 2.0 * np.pi * ((np.arange(L)[:, None] * z[None, :]) % N) / N
    f = np.float32
    return (
        (np.cos(ang) / N).astype(f),
        (np.sin(ang) / N).astype(f),
        np.cos(angz).astype(f),
        np.sin(angz).astype(f),
    )


def x_tables():
    ang = 2.0 * np.pi * ((np.arange(N)[:, None] * waves(16, N)[None, :]) % N) / N
    return np.cos(ang) / 8.0, np.sin(ang) / 8.0


def constants():
    cos, sin = x_tables()
    perm = np.zeros((ROWS, ROWS))
    for c in range(C):
        for x in range(XL):
            perm[c * XL + x, x * C + c] = 1
    order = np.zeros((128, 128))
    for j in range(S):
        for x in range(XL):
            for a in range(2):
                order[j * 8 + x * 2 + a, x * 32 + j * 2 + a] = 1
    fx = np.zeros((64, 128))
    fo = np.zeros((64, 128))
    iv = np.zeros((128, 64))
    ia = np.zeros((128, 64))
    for i in range(16):
        for h in range(2):
            for x in range(N):
                c, s = cos[x, i], sin[x, i]
                re, im = i * 4 + h * 2, i * 4 + h * 2 + 1
                fx[re, 2 * x : 2 * x + 2] = (c, s)
                fx[im, 2 * x : 2 * x + 2] = (-s, c)
                fo[re, 2 * x : 2 * x + 2] = (-s, c)
                fo[im, 2 * x : 2 * x + 2] = (-c, -s)
                vre, vim = (re, im) if h == 0 else (im, re)
                iv[2 * x, vre], iv[2 * x, vim] = c, -s
                iv[2 * x + 1, vre], iv[2 * x + 1, vim] = s, c
                ia[2 * x, re], ia[2 * x, im] = c, -s
                ia[2 * x + 1, re], ia[2 * x + 1, im] = s, c
    ext = np.zeros((128, 128))
    for s in range(S):
        for r in range(4):
            ext[s * 8 + r, s * 4 + r] = 1
            ext[s * 8 + 4 + r, 64 + s * 4 + r] = 1
    gather = np.zeros((2, 128, 128))
    for i in range(16):
        for h in range(2):
            for q in range(4):
                gather[h, i * 8 + h * 4 + q, (q // 2) * 64 + i * 4 + q % 2] = 1
    pick = np.zeros((6, 32, 128))
    for b in range(16):
        for h in range(2):
            base = b * 8 + h * 4
            pick[h * 3, b * 2, base] = 1
            pick[h * 3, b * 2 + 1, base + 1] = 1
            pick[h * 3 + 1, b * 2, base + 2] = 1
            pick[h * 3 + 1, b * 2 + 1, base + 3] = 1
            pick[h * 3 + 2, b * 2, base + 3] = 1
            pick[h * 3 + 2, b * 2 + 1, base + 2] = -1
    bf = lambda v: jnp.asarray(np.asarray(v, np.float32), BF16)
    return {
        "perm": bf(perm),
        "order": bf(order),
        "order_t": bf(order.T),
        "fx": bf(fx),
        "fo": bf(fo),
        "iv": bf(iv),
        "ia": bf(ia),
        "ext": bf(ext),
        "ext_t": bf(ext.T),
        "gather": bf(gather),
        "pick": bf(pick),
    }


def lanes(shape):
    return lax.broadcasted_iota(jnp.int32, shape, 1)


def subl(shape):
    return lax.broadcasted_iota(jnp.int32, shape, 0)


def low_half(shape):
    return (lanes(shape) & 64) == 0


def half_turn(v):
    return pltpu.roll(v, 64, 1)


def pack_spectra(acc, perm, order, z_ref):
    s = mm(acc.astype(BF16), perm)
    low = low_half((32, 128))
    for u in range(L // 2):
        for t in range(2):
            a = s[u * 64 : u * 64 + 32, t * 128 : t * 128 + 128]
            b = s[u * 64 + 32 : u * 64 + 64, t * 128 : t * 128 + 128]
            even = jnp.where(low, a, half_turn(b))
            odd = jnp.where(low, half_turn(a), b)
            z_ref[t * 64 : t * 64 + 32, u * 128 : u * 128 + 128] = even.astype(BF16)
            z_ref[t * 64 + 32 : t * 64 + 64, u * 128 : u * 128 + 128] = odd.astype(BF16)
    return mm(order, z_ref[...]).astype(BF16)


def unpack_back(arrived, perm, order_t, b_ref, doubled):
    z = mm(order_t, arrived)
    low = low_half((32, 128))
    for u in range(L // 2):
        for t in range(2):
            a = z[t * 64 : t * 64 + 32, u * 128 : u * 128 + 128]
            b = z[t * 64 + 32 : t * 64 + 64, u * 128 : u * 128 + 128]
            first = jnp.where(low, a, half_turn(b))
            second = jnp.where(low, half_turn(a), b)
            if doubled:
                first = first * (1.0 if u == 0 else 2.0)
                second = second * 2.0
            b_ref[u * 64 : u * 64 + 32, t * 128 : t * 128 + 128] = first.astype(BF16)
            b_ref[u * 64 + 32 : u * 64 + 64, t * 128 : t * 128 + 128] = second.astype(BF16)
    return nt(perm, b_ref[...]).astype(BF16)


def split(v):
    hi = v.astype(BF16)
    lo = (v - hi.astype(F32)).astype(BF16)
    return jnp.where(low_half(v.shape), hi.astype(F32), lo.astype(F32)).astype(BF16)


def spread_weight(w, transposed):
    e = (subl((ROWS, C)) // XL == lanes((ROWS, C))).astype(BF16)
    left = tn(w, e.T) if False else mm(e, w)
    full = nt(left.astype(BF16), e)
    same = (subl((ROWS, ROWS)) & 3) == (lanes((ROWS, ROWS)) & 3)
    return jnp.where(same, full, 0.0).astype(BF16)


STEPS = 8
CHUNK = CELLS // STEPS


def spectra_kernel(f_ref, ca_ref, sa_ref, cb_ref, sb_ref, perm_ref, order_ref, out_ref, t_ref, acc_ref, z_ref):
    step = pl.program_id(0)
    for g in range(CHUNK // 128):
        cols = slice(g * 128, g * 128 + 128)
        ca, sa = ca_ref[:, cols], sa_ref[:, cols]
        for l in range(L):
            cb, sb = cb_ref[l : l + 1, :], sb_ref[l : l + 1, :]
            t_ref[l * 32 : l * 32 + 32, cols] = (ca * cb - sa * sb).astype(BF16)
    part = nt(t_ref[...], f_ref[...])

    @pl.when(step == 0)
    def _():
        acc_ref[...] = part

    @pl.when(step > 0)
    def _():
        acc_ref[...] += part

    @pl.when(step == STEPS - 1)
    def _():
        out_ref[...] = pack_spectra(acc_ref[...], perm_ref[...], order_ref[...], z_ref)


def mix_kernel(r_ref, w_ref, fx_ref, iv_ref, out_ref, m_ref, mask_ref, v_ref):
    u = pl.program_id(0)

    @pl.when(u == 0)
    def _():
        m = mm(fx_ref[...], r_ref[...])
        m_ref[...] = m.astype(BF16)
        shape = m.shape
        keep = ((lanes(shape) >> 6) & 1) == ((subl(shape) >> 1) & 1)
        mask_ref[...] = jnp.where(keep, m, 0.0)

    cols = pl.ds(pl.multiple_of(u * 128, 128), 128)
    row, lane = subl((8, 128)), lanes((8, 128))
    top = row < 4
    even = (row & 1) == 0
    sign = jnp.where(lane < 64, -1.0, 1.0)
    keep = (lane >> 6) == ((row >> 1) & 1)
    for t in range(8):
        left = mask_ref[8 * t : 8 * t + 8, cols].astype(BF16)
        right = jnp.concatenate(
            [w_ref[2 * t].reshape(128, 128), w_ref[2 * t + 1].reshape(128, 128)], axis=1
        )
        o = mm(left, right)
        res = jnp.where(top, o[:, :128], o[:, 128:])
        turned = half_turn(res)
        above = pltpu.roll(turned, 7, 0)
        below = pltpu.roll(turned, 1, 0)
        v = jnp.where(even, res + sign * above, below - sign * res)
        v_ref[8 * t : 8 * t + 8, cols] = jnp.where(keep, v, 0.0)

    @pl.when(u == L // 2 - 1)
    def _():
        out_ref[...] = mm(iv_ref[...], v_ref[...].astype(BF16)).astype(BF16)


def slope(v):
    a = jnp.abs(v)
    e = jnp.exp(v * v * -0.5)
    t = 1.0 / (1.0 + (0.3275911 / math.sqrt(2.0)) * a)
    poly = t * (
        0.5 * 0.254829592
        + t
        * (
            0.5 * -0.284496736
            + t * (0.5 * 1.421413741 + t * (0.5 * -1.453152027 + t * (0.5 * 1.061405429)))
        )
    )
    tail = poly * e
    return jnp.where(v < 0, tail, 1.0 - tail) + v * e * (1.0 / math.sqrt(2.0 * math.pi))


def delta_kernel(
    r_ref, f_ref, ct_ref, t_ref, w_ref, bias_ref, perm_ref, order_ref, order_t_ref, ext_ref,
    out_ref, d_ref, b_ref, lw_ref, pre_ref, s_ref, g_ref, bs_ref, bt_ref, z_ref,
):
    step = pl.program_id(0)

    @pl.when(step == 0)
    def _():
        b_ref[...] = unpack_back(r_ref[...], perm_ref[...], order_t_ref[...], bt_ref, True)
        lw_ref[...] = spread_weight(w_ref[...], False)
        s_ref[...] = jnp.zeros_like(s_ref)
        g_ref[...] = jnp.zeros_like(g_ref)
        bs_ref[...] = jnp.zeros_like(bs_ref)

    pre_ref[...] = mm(b_ref[...], t_ref[...]) + mm(lw_ref[...], f_ref[...])
    for r in range(0, ROWS, 16):
        rows = slice(r, r + 16)
        v = pre_ref[rows, :] + bias_ref[rows, :]
        d = (ct_ref[rows, :].astype(F32) * slope(v)).astype(BF16)
        d_ref[rows, :] = d
        df = d.astype(F32)
        part = df[:, :128]
        for g in range(1, CHUNK // 128):
            part = part + df[:, g * 128 : g * 128 + 128]
        bs_ref[rows, :] += part
    s_ref[...] += nt(t_ref[...], d_ref[...])
    g_ref[...] += nt(d_ref[...], f_ref[...])

    @pl.when(step == STEPS - 1)
    def _():
        doubled = jnp.where(subl((Q, ROWS)) < 32, 1.0, 2.0)
        out_ref[:, :1024] = pack_spectra(s_ref[...] * doubled, perm_ref[...], order_ref[...], z_ref)
        same = (subl((ROWS, ROWS)) & 3) == (lanes((ROWS, ROWS)) & 3)
        g = jnp.where(same, g_ref[...], 0.0)
        e = (subl((C, ROWS)) == lanes((C, ROWS)) // XL).astype(F32)
        e2 = ((subl((ROWS, 128)) // XL) == (lanes((ROWS, 128)) & 63)).astype(F32)
        hi = functools.partial(jnp.dot, precision=lax.Precision.HIGHEST, preferred_element_type=F32)
        wg = hi(hi(e, g), e2)
        bg = jnp.sum(hi(e, bs_ref[...]), axis=1, keepdims=True)
        both = jnp.concatenate([wg, jnp.broadcast_to(bg, (C, 128))], axis=0)
        out_ref[:, 1024:] = mm(ext_ref[...], split(both)).astype(BF16)


def total_of(ext):
    shape = (8, 128)
    pick = ((lanes(shape) & 7) == subl(shape)).astype(BF16)
    v = mm(pick, ext)
    return v + half_turn(v)


def spread_total(v):
    return jnp.concatenate([split(v).astype(F32)] * S, axis=0).astype(BF16)


def grad_modes_kernel(r_ref, m_ref, fx_ref, fo_ref, gather_ref, left_ref, dp_ref):
    r = r_ref[:, :1024]
    a = mm(fx_ref[...], r)
    b = mm(fo_ref[...], r)
    row = subl((64, 128))
    first = ((row >> 1) & 1) == 0
    low = low_half((64, 128))
    for u in range(8):
        cols = slice(u * 128, u * 128 + 128)
        au, bu = a[:, cols], b[:, cols]
        left_ref[:, cols] = jnp.where(
            first, jnp.where(low, au, half_turn(bu)), jnp.where(low, half_turn(au), bu)
        ).astype(BF16)
    both = jnp.concatenate([m_ref[...], a.astype(BF16)], axis=0)
    dp_ref[:, :512] = (
        mm(gather_ref[0], both[:, :512]) + mm(gather_ref[1], both[:, 512:])
    ).astype(BF16)
    dp_ref[:, 512:] = spread_total(total_of(r_ref[:, 1024:]))


def adjoint_kernel(left_ref, w_ref, out_ref):
    row, lane = subl((8, 128)), lanes((8, 128))
    top = row < 4
    keep = (lane >> 6) == ((row >> 1) & 1)
    for t in range(8):
        right = jnp.concatenate(
            [w_ref[2 * t].reshape(128, 128), w_ref[2 * t + 1].reshape(128, 128)], axis=0
        )
        o = nt(left_ref[8 * t : 8 * t + 8, :], right)
        res = jnp.where(top, o[:, :128], o[:, 128:])
        out_ref[8 * t : 8 * t + 8, :] = jnp.where(keep, res, 0.0).astype(BF16)


def adjoint_back_kernel(v_ref, dp_ref, ia_ref, out_ref):
    out_ref[:, :1024] = mm(ia_ref[...], v_ref[...]).astype(BF16)
    out_ref[:, 1024:] = spread_total(total_of(dp_ref[:, 512:]))


def weight_grad_kernel(dp_ref, pick_ref, out_ref):
    low = low_half((32, 128))
    data = dp_ref[:, :512]
    for h in range(2):
        m = mm(pick_ref[h * 3], data)
        g1 = mm(pick_ref[h * 3 + 1], data)
        g2 = mm(pick_ref[h * 3 + 2], data)
        for v in range(4):
            cols = slice(v * 128, v * 128 + 128)
            a, b = g1[:, cols], g2[:, cols]
            right = jnp.concatenate(
                [jnp.where(low, a, half_turn(b)), jnp.where(low, half_turn(a), b)], axis=1
            )
            o = tn(m[:, cols].astype(BF16), right.astype(BF16)) * 0.25
            l = h * 8 + v * 2
            out_ref[l] = o[:64, :128]
            out_ref[l + 1] = o[64:, 128:]


def input_grad_kernel(
    r_ref, d_ref, t_ref, w_ref, perm_ref, order_t_ref, ext_t_ref,
    out_ref, pg_ref, b_ref, lw_ref, bt_ref,
):
    step = pl.program_id(0)

    @pl.when(step == 0)
    def _():
        b_ref[...] = unpack_back(r_ref[:, :1024], perm_ref[...], order_t_ref[...], bt_ref, False)
        lw = spread_weight(w_ref[...], False).astype(F32)
        lw_ref[...] = lw.T.astype(BF16)
        v = mm(ext_t_ref[...], r_ref[:, 1024:])
        pg_ref[...] = (v + half_turn(v)) * (1.0 / 2048.0)

    out_ref[...] = (mm(b_ref[...], t_ref[...]) + mm(lw_ref[...], d_ref[...])).astype(BF16)


def whole(shape):
    return pl.BlockSpec(shape, lambda *_: (0,) * len(shape))


def chunked(rows):
    return pl.BlockSpec((rows, CHUNK), lambda i: (0, i))


def sds(shape, dtype=BF16):
    return jax.ShapeDtypeStruct(shape, dtype)


def exchange(v, axis):
    width = v.shape[1]
    out = lax.all_to_all(v.reshape(S, 8, width), axis, split_axis=0, concat_axis=0, tiled=True)
    return out.reshape(128, width)


def body(field, cotangent, spectral_weight, point_weight, bias):
    k = constants()
    ca, sa, cb, sb = (jnp.asarray(v) for v in phase_tables())
    field2 = field.reshape(ROWS, CELLS)
    cot2 = cotangent.reshape(ROWS, CELLS)
    bias_rows = jnp.broadcast_to(bias[:, None], (C, XL)).reshape(ROWS, 1)
    w_spec = pl.BlockSpec((16, 2, 64, 128), lambda u: (0, u, 0, 0))

    spectra, table = pl.pallas_call(
        spectra_kernel,
        grid=(STEPS,),
        in_specs=[chunked(ROWS), chunked(32), chunked(32), whole((L, 128)), whole((L, 128)),
                  whole((ROWS, ROWS)), whole((128, 128))],
        out_specs=[whole((128, 1024)), chunked(Q)],
        out_shape=[sds((128, 1024)), sds((Q, CELLS))],
        scratch_shapes=[pltpu.VMEM((Q, ROWS), F32), pltpu.VMEM((128, 1024), BF16)],
        name="spectra",
    )(field2, ca, sa, cb, sb, k["perm"], k["order"])
    arrived = exchange(spectra, "slab")

    back, modes = pl.pallas_call(
        mix_kernel,
        grid=(L // 2,),
        in_specs=[whole((128, 1024)), w_spec, whole((64, 128)), whole((128, 64))],
        out_specs=[whole((128, 1024)), whole((64, 1024))],
        out_shape=[sds((128, 1024)), sds((64, 1024))],
        scratch_shapes=[pltpu.VMEM((64, 1024), F32), pltpu.VMEM((64, 1024), F32)],
        name="mix",
    )(arrived, spectral_weight, k["fx"], k["iv"])
    arrived = exchange(back, "slab")

    grad_spectra, delta = pl.pallas_call(
        delta_kernel,
        grid=(STEPS,),
        in_specs=[whole((128, 1024)), chunked(ROWS), chunked(ROWS), chunked(Q), whole((C, C)),
                  whole((ROWS, 1)), whole((ROWS, ROWS)), whole((128, 128)), whole((128, 128)),
                  whole((128, 128))],
        out_specs=[whole((128, 1152)), chunked(ROWS)],
        out_shape=[sds((128, 1152)), sds((ROWS, CELLS))],
        scratch_shapes=[
            pltpu.VMEM((ROWS, Q), BF16),
            pltpu.VMEM((ROWS, ROWS), BF16),
            pltpu.VMEM((ROWS, CHUNK), F32),
            pltpu.VMEM((Q, ROWS), F32),
            pltpu.VMEM((ROWS, ROWS), F32),
            pltpu.VMEM((ROWS, 128), F32),
            pltpu.VMEM((Q, ROWS), BF16),
            pltpu.VMEM((128, 1024), BF16),
        ],
        name="delta",
    )(arrived, field2, cot2, table, point_weight, bias_rows, k["perm"], k["order"], k["order_t"],
      k["ext"])
    arrived = exchange(grad_spectra, "slab")

    left, shared = pl.pallas_call(
        grad_modes_kernel,
        out_shape=[sds((64, 1024)), sds((128, 640))],
        name="grad_modes",
    )(arrived, modes, k["fx"], k["fo"], k["gather"])
    shared = exchange(shared, "dp")

    adjoint = pl.pallas_call(
        adjoint_kernel,
        grid=(L // 2,),
        in_specs=[pl.BlockSpec((64, 128), lambda u: (0, u)), w_spec],
        out_specs=pl.BlockSpec((64, 128), lambda u: (0, u)),
        out_shape=sds((64, 1024)),
        name="adjoint",
    )(left, spectral_weight)
    adjoint_back = pl.pallas_call(
        adjoint_back_kernel,
        out_shape=sds((128, 1152)),
        name="adjoint_back",
    )(adjoint, shared, k["ia"])
    arrived = exchange(adjoint_back, "slab")

    spectral_grad = pl.pallas_call(
        weight_grad_kernel,
        out_shape=sds((L, C, 128), F32),
        name="weight_grad",
    )(shared, k["pick"])

    input_grad, small = pl.pallas_call(
        input_grad_kernel,
        grid=(STEPS,),
        in_specs=[whole((128, 1152)), chunked(ROWS), chunked(Q), whole((C, C)), whole((ROWS, ROWS)),
                  whole((128, 128)), whole((128, 128))],
        out_specs=[chunked(ROWS), whole((128, 128))],
        out_shape=[sds((ROWS, CELLS)), sds((128, 128), F32)],
        scratch_shapes=[
            pltpu.VMEM((ROWS, Q), BF16),
            pltpu.VMEM((ROWS, ROWS), BF16),
            pltpu.VMEM((Q, ROWS), BF16),
        ],
        name="input_grad",
    )(arrived, delta, table, point_weight, k["perm"], k["order_t"], k["ext_t"])
    return (
        input_grad.reshape(field.shape),
        spectral_grad[None],
        small[:C, :C],
        small[C:, 0],
    )


def solution(mesh):
    return jax.shard_map(
        body,
        mesh=mesh,
        in_specs=(
            P("dp", None, "slab", None),
            P("dp", None, "slab", None),
            P(None, "slab", None, None),
            P(),
            P(),
        ),
        out_specs=(P("dp", None, "slab", None), P("dp", "slab", None, None), P(), P()),
        check_vma=False,
    )
```

profile of v0, /device:TPU:1, one launch (start us, length us, event | category | flops | bytes accessed | tf_op | source)
XLA Modules:
  0.0 127.4 jit_solution(9916606528246824860)
XLA Ops:
  0.6 4.0 %reshape.51.f_ref = bf16[256,4096]{1,0:T(8,128)(2,1)} reshape(bf16[1,64,4,4096]{3,2,1,0:T(4,128)(2,1)} %param.20) | data formatting | bytes 4194304 | tf_op jit(solution)/shard_map/reshape | solution.py:415
  4.6 8.6 %spectra.1 = (bf16[128,1024]{1,0:T(8,128)(2,1)}, bf16[512,4096]{1,0:T(8,128)(2,1)}) custom-call(bf16[256,4096]{1,0:T(8,128)(2,1)} %reshape.51.f_ref, f32[32,4096]{1,0:T(8,128)} %constant.41.clone.ca_ref, f32[32,4096]{1,0:T(8,128)} %constant.42.clone.sa_ref, f32[16,128]{1,0:T(8,128)} %constant.43.clone.cb_ref, f32[16,128]{1,0:T(8,128)} %constant.44.clone.sb_ref, ...), custom_call_target="tpu_custom_call" | custom-call | tf_op jit(solution)/shard_map/spectra/pallas_call | solution.py:420
  13.2 14.6 %all_to_all.25 = bf16[16,8,1024]{2,1,0:T(8,128)(2,1)} all-to-all(bf16[16,8,1024]{2,1,0:T(8,128)(2,1)} %bitcast.21), channel_id=1, replica_groups=mesh['dp'=16,'slab'=16] {'slab'}, dimensions={0} | all-to-all | bytes 524288 | tf_op jit(solution)/shard_map/all_to_all | solution.py:408
  27.8 7.0 %mix.1 = (bf16[128,1024]{1,0:T(8,128)(2,1)}, bf16[64,1024]{1,0:T(8,128)(2,1)}) custom-call(bf16[128,1024]{1,0:T(8,128)(2,1)} %bitcast.17, bf16[16,16,64,128]{3,2,1,0:T(8,128)(2,1)} %w_ref.6, bf16[64,128]{1,0:T(8,128)(2,1)} %constant.33.clone.fx_ref, bf16[128,64]{1,0:T(8,128)(2,1)} %constant.35.clone.iv_ref), custom_call_target="tpu_custom_call" | custom-call | tf_op jit(solution)/shard_map/mix/pallas_call | solution.py:432
  34.8 4.2 %all-to-all-start.1 = ((bf16[16,8,1024]{2,1,0:T(8,128)(2,1)}), bf16[16,8,1024]{2,1,0:T(8,128)(2,1)S(1)}, u32[]{:S(2)}, u32[]{:S(2)}) async-start(bf16[16,8,1024]{2,1,0:T(8,128)(2,1)} %bitcast.20), calls=%async_computation.1 | async-start | bytes 524288 | tf_op jit(solution)/shard_map/all_to_all | solution.py:408
  39.1 0.7 reshape.65.bias_ref
  39.9 2.1 %reshape.56.ct_ref = bf16[256,4096]{1,0:T(8,128)(2,1)} reshape(bf16[1,64,4,4096]{3,2,1,0:T(4,128)(2,1)S(1)} %copy-done) | data formatting | bytes 4194304 | tf_op jit(solution)/shard_map/reshape | solution.py:416
  42.0 4.4 %all-to-all-done.1 = bf16[16,8,1024]{2,1,0:T(8,128)(2,1)S(1)} async-done(((bf16[16,8,1024]{2,1,0:T(8,128)(2,1)}), bf16[16,8,1024]{2,1,0:T(8,128)(2,1)S(1)}, u32[]{:S(2)}, u32[]{:S(2)}) %all-to-all-start.1) | async-done | bytes 262176 | tf_op jit(solution)/shard_map/all_to_all | solution.py:408
  46.3 0.7 copy-done.3
  47.1 13.7 %delta.1 = (bf16[128,1152]{1,0:T(8,128)(2,1)}, bf16[256,4096]{1,0:T(8,128)(2,1)}) custom-call(bf16[128,1024]{1,0:T(8,128)(2,1)} %bitcast.16, bf16[256,4096]{1,0:T(8,128)(2,1)} %reshape.51.f_ref, bf16[256,4096]{1,0:T(8,128)(2,1)} %reshape.56.ct_ref, bf16[512,4096]{1,0:T(8,128)(2,1)} %get-tuple-element.16.t_ref, bf16[64,64]{1,0:T(8,128)(2,1)} %w_ref.7, ...), custom_call_target="tpu_custom_call" | custom-call | tf_op jit(solution)/shard_map/delta/pallas_call | solution.py:443
  60.8 12.5 %all_to_all.26 = bf16[16,8,1152]{2,1,0:T(8,128)(2,1)} all-to-all(bf16[16,8,1152]{2,1,0:T(8,128)(2,1)} %bitcast.19), channel_id=1, replica_groups=mesh['dp'=16,'slab'=16] {'slab'}, dimensions={0} | all-to-all | bytes 589824 | tf_op jit(solution)/shard_map/all_to_all | solution.py:408
  73.2 2.2 %grad_modes.1 = (bf16[64,1024]{1,0:T(8,128)(2,1)}, bf16[128,640]{1,0:T(8,128)(2,1)}) custom-call(bf16[128,1152]{1,0:T(8,128)(2,1)} %bitcast.15, bf16[64,1024]{1,0:T(8,128)(2,1)} %get-tuple-element.18.m_ref, bf16[64,128]{1,0:T(8,128)(2,1)} %constant.33.clone.fx_ref, bf16[64,128]{1,0:T(8,128)(2,1)} %constant.34.clone.fo_ref, ...), custom_call_target="tpu_custom_call" | custom-call | tf_op jit(solution)/shard_map/grad_modes/pallas_call | solution.py:466
  75.5 9.8 %all-to-all-start.3 = ((bf16[16,8,640]{2,1,0:T(8,128)(2,1)}), bf16[16,8,640]{2,1,0:T(8,128)(2,1)S(1)}, u32[]{:S(2)}, u32[]{:S(2)}) async-start(bf16[16,8,640]{2,1,0:T(8,128)(2,1)} %bitcast.22), calls=%async_computation.3 | async-start | bytes 327680 | tf_op jit(solution)/shard_map/all_to_all | solution.py:408
  85.3 6.6 %adjoint.1.v_ref = bf16[64,1024]{1,0:T(8,128)(2,1)} custom-call(bf16[64,1024]{1,0:T(8,128)(2,1)} %get-tuple-element.19.left_ref, bf16[16,16,64,128]{3,2,1,0:T(8,128)(2,1)} %w_ref.6), custom_call_target="tpu_custom_call" | custom-call | tf_op jit(solution)/shard_map/adjoint/pallas_call | solution.py:473
  91.9 3.6 %all-to-all-done.3 = bf16[16,8,640]{2,1,0:T(8,128)(2,1)S(1)} async-done(((bf16[16,8,640]{2,1,0:T(8,128)(2,1)}), bf16[16,8,640]{2,1,0:T(8,128)(2,1)S(1)}, u32[]{:S(2)}, u32[]{:S(2)}) %all-to-all-start.3) | async-done | bytes 163872 | tf_op jit(solution)/shard_map/all_to_all | solution.py:408
  96.2 2.0 %adjoint_back.1 = bf16[128,1152]{1,0:T(8,128)(2,1)} custom-call(bf16[64,1024]{1,0:T(8,128)(2,1)} %adjoint.1.v_ref, bf16[128,640]{1,0:T(8,128)(2,1)} %bitcast.11, bf16[128,64]{1,0:T(8,128)(2,1)} %constant.36.clone.ia_ref), custom_call_target="tpu_custom_call" | custom-call | tf_op jit(solution)/shard_map/adjoint_back/pallas_call | solution.py:481
  98.1 5.3 %all-to-all-start.4 = ((bf16[16,8,1152]{2,1,0:T(8,128)(2,1)}), bf16[16,8,1152]{2,1,0:T(8,128)(2,1)S(1)}, u32[]{:S(2)}, u32[]{:S(2)}) async-start(bf16[16,8,1152]{2,1,0:T(8,128)(2,1)} %bitcast.14), calls=%async_computation.4 | async-start | bytes 589824 | tf_op jit(solution)/shard_map/all_to_all | solution.py:408
  103.5 2.5 %weight_grad.1 = f32[16,64,128]{2,1,0:T(8,128)} custom-call(bf16[128,640]{1,0:T(8,128)(2,1)} %bitcast.12, bf16[6,32,128]{2,1,0:T(8,128)(2,1)} %constant.40.clone.pick_ref), custom_call_target="tpu_custom_call" | custom-call | tf_op jit(solution)/shard_map/weight_grad/pallas_call | solution.py:488
  106.0 5.0 %all-to-all-done.4 = bf16[16,8,1152]{2,1,0:T(8,128)(2,1)S(1)} async-done(((bf16[16,8,1152]{2,1,0:T(8,128)(2,1)}), bf16[16,8,1152]{2,1,0:T(8,128)(2,1)S(1)}, u32[]{:S(2)}, u32[]{:S(2)}) %all-to-all-start.4) | async-done | bytes 294944 | tf_op jit(solution)/shard_map/all_to_all | solution.py:408
  111.0 0.7 copy-done.2
  111.7 8.8 %input_grad.1 = (bf16[256,4096]{1,0:T(8,128)(2,1)}, f32[128,128]{1,0:T(8,128)}) custom-call(bf16[128,1152]{1,0:T(8,128)(2,1)} %bitcast.13, bf16[256,4096]{1,0:T(8,128)(2,1)} %get-tuple-element.21.d_ref, bf16[512,4096]{1,0:T(8,128)(2,1)} %get-tuple-element.16.t_ref, bf16[64,64]{1,0:T(8,128)(2,1)} %w_ref.7, bf16[256,256]{1,0:T(8,128)(2,1)} %constant.30.clone.perm_ref, ...), custom_call_target="tpu_custom_call" | custom-call | tf_op jit(solution)/shard_map/input_grad/pallas_call | solution.py:494
  120.5 1.4 %slice_reduce_fusion = f32[64]{0:T(128)} fusion(f32[128,128]{1,0:T(8,128)} %get-tuple-element.23), kind=kLoop, calls=%fused_computation | loop fusion | bytes 512 | tf_op jit(solution)/shard_map/slice | solution.py:512
  121.9 1.4 %slice.6 = f32[64,64]{1,0:T(8,128)} slice(f32[128,128]{1,0:T(8,128)} %get-tuple-element.23), slice={[0:64], [0:64]} | slice | bytes 32768 | tf_op jit(solution)/shard_map/slice | solution.py:511
  123.3 4.1 %reshape.64 = bf16[1,64,4,4096]{3,2,1,0:T(4,128)(2,1)} reshape(bf16[256,4096]{1,0:T(8,128)(2,1)} %get-tuple-element.22) | data formatting | bytes 4194304 | tf_op jit(solution)/shard_map/reshape | solution.py:509
  (9 shorter events, 0.7 us)
Async XLA Ops:
  27.8 11.2 %copy-start.4 = (f32[64]{0:T(128)S(1)}, f32[64]{0:T(128)}, u32[]{:S(2)}) copy-start(f32[64]{0:T(128)} %param.24) | copy-start | bytes 772
  27.8 12.1 %copy-start = (bf16[1,64,4,4096]{3,2,1,0:T(4,128)(2,1)S(1)}, bf16[1,64,4,4096]{3,2,1,0:T(4,128)(2,1)}, u32[]{:S(2)}) copy-start(bf16[1,64,4,4096]{3,2,1,0:T(4,128)(2,1)} %param.21) | copy-start | bytes 6291460
  34.8 11.5 %all-to-all-start.1 = ((bf16[16,8,1024]{2,1,0:T(8,128)(2,1)}), bf16[16,8,1024]{2,1,0:T(8,128)(2,1)S(1)}, u32[]{:S(2)}, u32[]{:S(2)}) async-start(bf16[16,8,1024]{2,1,0:T(8,128)(2,1)} %bitcast.20), calls=%async_computation.1 | async-start | bytes 524288 | tf_op jit(solution)/shard_map/all_to_all | solution.py:408
  46.3 0.7 copy-start.3
  75.5 20.0 %all-to-all-start.3 = ((bf16[16,8,640]{2,1,0:T(8,128)(2,1)}), bf16[16,8,640]{2,1,0:T(8,128)(2,1)S(1)}, u32[]{:S(2)}, u32[]{:S(2)}) async-start(bf16[16,8,640]{2,1,0:T(8,128)(2,1)} %bitcast.22), calls=%async_computation.3 | async-start | bytes 327680 | tf_op jit(solution)/shard_map/all_to_all | solution.py:408
  95.5 0.7 copy-start.1
  98.1 12.9 %all-to-all-start.4 = ((bf16[16,8,1152]{2,1,0:T(8,128)(2,1)}), bf16[16,8,1152]{2,1,0:T(8,128)(2,1)S(1)}, u32[]{:S(2)}, u32[]{:S(2)}) async-start(bf16[16,8,1152]{2,1,0:T(8,128)(2,1)} %bitcast.14), calls=%async_computation.4 | async-start | bytes 589824 | tf_op jit(solution)/shard_map/all_to_all | solution.py:408
  111.0 0.7 copy-start.2
where the time goes:
time: 129 us; the launch traced here: 127 us
  Pallas kernels  51.4 us (40%)
  blocking collectives  27.1 us (21%)
  starting transfers between devices  19.4 us (15%)
  local copies, waits for them, and re-layouts  15.8 us (12%)
  waiting for transfers between devices  13 us (10%)
    all_to_all x2, blocking collectives, exchange(): lax.all_to_all(v.reshape(S, 8, width), axis, split_axis=0, concat_axis=0,...  27.1 us
    all_to_all x3, starting transfers between devices, exchange(): lax.all_to_all(v.reshape(S, 8, width), axis, split_axis=0, concat_axis=0,...  19.4 us
    pallas_call x1, Pallas kernels, body(): pl.pallas_call(delta_kernel, grid=(STEPS,), in_specs=[whole((128, 1024)),...  13.7 us
    all_to_all x3, waiting for transfers between devices, exchange(): lax.all_to_all(v.reshape(S, 8, width), axis, split_axis=0, concat_axis=0,...  13 us
    pallas_call x1, Pallas kernels, body(): pl.pallas_call(input_grad_kernel, grid=(STEPS,), in_specs=[whole((128, 11...  8.8 us
    pallas_call x1, Pallas kernels, body(): pl.pallas_call(spectra_kernel, grid=(STEPS,), in_specs=[chunked(ROWS), ch...  8.61 us
    pallas_call x1, Pallas kernels, body(): pl.pallas_call(mix_kernel, grid=(L // 2,), in_specs=[whole((128, 1024)),...  7 us
    pallas_call x1, Pallas kernels, body(): pl.pallas_call(adjoint_kernel, grid=(L // 2,), in_specs=[pl.BlockSpec((64...  6.61 us
  transfers between devices with their start and end apart: 3, of which 3 were waited for; matrix products, arithmetic and copies ran while one was open for 2% of the time, Pallas kernels for 7%

commit v1 on v0

v1 whole, which is shorter than its diff:
```python
import functools
import math

import jax
import jax.numpy as jnp
import numpy as np
from jax import lax
from jax.experimental import pallas as pl
from jax.experimental.pallas import tpu as pltpu
from jax.sharding import PartitionSpec as P

C = 64
N = 64
XL = 4
S = 16
L = 16
CELLS = 4096
ROWS = C * XL
Q = 512
F32 = jnp.float32
BF16 = jnp.bfloat16


def mm(a, b):
    return jnp.dot(a, b, preferred_element_type=F32)


def nt(a, b):
    return lax.dot_general(a, b, (((1,), (1,)), ((), ())), preferred_element_type=F32)


def tn(a, b):
    return lax.dot_general(a, b, (((0,), (0,)), ((), ())), preferred_element_type=F32)


def waves(count, size):
    return np.array([i if i < count // 2 else size - count + i for i in range(count)])


def phase_tables():
    f = np.float32
    k = np.repeat(waves(S, N), 2)[:, None]
    part = np.tile([0.0, np.pi / 2], S)[:, None]
    unit = 2.0 * np.pi / N
    ang = unit * (k * (np.arange(128) // N)[None, :]) + part
    turn = unit * np.broadcast_to(2 * k, (2 * S, 128))
    angz = unit * ((np.arange(L)[:, None] * (np.arange(128) % N)[None, :]) % N)
    pair = lambda a, scale: np.concatenate([np.cos(a), np.sin(a)]) * scale
    return np.concatenate([pair(ang, 1.0 / N), pair(turn, 1.0), pair(angz, 1.0)]).astype(f)


def x_tables():
    ang = 2.0 * np.pi * ((np.arange(N)[:, None] * waves(16, N)[None, :]) % N) / N
    return np.cos(ang) / 8.0, np.sin(ang) / 8.0


def constants():
    cos, sin = x_tables()
    fx = np.zeros((64, 128))
    fo = np.zeros((64, 128))
    iv = np.zeros((128, 64))
    ia = np.zeros((128, 64))
    for i in range(16):
        for h in range(2):
            for x in range(N):
                c, s = cos[x, i], sin[x, i]
                re, im = i * 4 + h * 2, i * 4 + h * 2 + 1
                fx[re, 2 * x : 2 * x + 2] = (c, s)
                fx[im, 2 * x : 2 * x + 2] = (-s, c)
                fo[re, 2 * x : 2 * x + 2] = (-s, c)
                fo[im, 2 * x : 2 * x + 2] = (-c, -s)
                vre, vim = (re, im) if h == 0 else (im, re)
                iv[2 * x, vre], iv[2 * x, vim] = c, -s
                iv[2 * x + 1, vre], iv[2 * x + 1, vim] = s, c
                ia[2 * x, re], ia[2 * x, im] = c, -s
                ia[2 * x + 1, re], ia[2 * x + 1, im] = s, c
    gather = np.zeros((2, 128, 128))
    for i in range(16):
        for h in range(2):
            for q in range(4):
                gather[h, i * 8 + h * 4 + q, (q // 2) * 64 + i * 4 + q % 2] = 1
    pick = np.zeros((6, 32, 128))
    for b in range(16):
        for h in range(2):
            base = b * 8 + h * 4
            pick[h * 3, b * 2, base] = 1
            pick[h * 3, b * 2 + 1, base + 1] = 1
            pick[h * 3 + 1, b * 2, base + 2] = 1
            pick[h * 3 + 1, b * 2 + 1, base + 3] = 1
            pick[h * 3 + 2, b * 2, base + 3] = 1
            pick[h * 3 + 2, b * 2 + 1, base + 2] = -1
    bf = lambda v: jnp.asarray(np.asarray(v, np.float32), BF16)
    return {
        "fx": bf(fx),
        "fo": bf(fo),
        "iv": bf(iv),
        "ia": bf(ia),
        "gather": bf(gather),
        "pick": bf(pick),
    }


def lanes(shape):
    return lax.broadcasted_iota(jnp.int32, shape, 1)


def subl(shape):
    return lax.broadcasted_iota(jnp.int32, shape, 0)


def low_half(shape):
    return (lanes(shape) & 64) == 0


def half_turn(v):
    return pltpu.roll(v, 64, 1)


def pack_spectra(acc, perm, order, z_ref):
    s = mm(acc.astype(BF16), perm)
    low = low_half((32, 128))
    for u in range(L // 2):
        for t in range(2):
            a = s[u * 64 : u * 64 + 32, t * 128 : t * 128 + 128]
            b = s[u * 64 + 32 : u * 64 + 64, t * 128 : t * 128 + 128]
            even = jnp.where(low, a, half_turn(b))
            odd = jnp.where(low, half_turn(a), b)
            z_ref[t * 64 : t * 64 + 32, u * 128 : u * 128 + 128] = even.astype(BF16)
            z_ref[t * 64 + 32 : t * 64 + 64, u * 128 : u * 128 + 128] = odd.astype(BF16)
    return mm(order, z_ref[...]).astype(BF16)


def unpack_back(arrived, perm, order_t, b_ref, doubled):
    z = mm(order_t, arrived)
    low = low_half((32, 128))
    for u in range(L // 2):
        for t in range(2):
            a = z[t * 64 : t * 64 + 32, u * 128 : u * 128 + 128]
            b = z[t * 64 + 32 : t * 64 + 64, u * 128 : u * 128 + 128]
            first = jnp.where(low, a, half_turn(b))
            second = jnp.where(low, half_turn(a), b)
            if doubled:
                first = first * (1.0 if u == 0 else 2.0)
                second = second * 2.0
            b_ref[u * 64 : u * 64 + 32, t * 128 : t * 128 + 128] = first.astype(BF16)
            b_ref[u * 64 + 32 : u * 64 + 64, t * 128 : t * 128 + 128] = second.astype(BF16)
    return nt(perm, b_ref[...]).astype(BF16)


def split(v):
    hi = v.astype(BF16)
    lo = (v - hi.astype(F32)).astype(BF16)
    return jnp.where(low_half(v.shape), hi.astype(F32), lo.astype(F32)).astype(BF16)


def spread_weight(w):
    e = (subl((ROWS, C)) // XL == lanes((ROWS, C))).astype(BF16)
    left = mm(e, w)
    full = nt(left.astype(BF16), e)
    same = (subl((ROWS, ROWS)) & 3) == (lanes((ROWS, ROWS)) & 3)
    return jnp.where(same, full, 0.0).astype(BF16)


def onehot(match):
    return jnp.where(match, 1.0, 0.0).astype(BF16)


def lane_order():
    r, k = subl((ROWS, ROWS)), lanes((ROWS, ROWS))
    return onehot(((r >> 2) == (k & 63)) & ((r & 3) == (k >> 6)))


def row_order(r, k):
    return onehot(((r >> 3) == ((k >> 1) & 15)) & (((r >> 1) & 3) == (k >> 5)) & ((r & 1) == (k & 1)))


def ext_order(r, k):
    return onehot(((r >> 3) == ((k >> 2) & 15)) & (((r >> 2) & 1) == (k >> 6)) & ((r & 3) == (k & 3)))


SQUARE = (128, 128)

STEPS = 8
CHUNK = CELLS // STEPS
EXACT = functools.partial(
    lax.dot_general, precision=lax.Precision.HIGHEST, preferred_element_type=F32
)
NT = (((1,), (1,)), ((), ()))
NN = (((1,), (0,)), ((), ()))


def at(step):
    return pl.ds(pl.multiple_of(step * CHUNK, CHUNK), CHUNK)


def planes(src, dst, sems, step):
    return pltpu.make_async_copy(src.at[:, :, at(step)], dst.at[:, :, at(step)], sems.at[step])


def columns(src, dst, sems, step):
    return pltpu.make_async_copy(src.at[:, at(step)], dst.at[:, at(step)], sems.at[step])


def modes_pair(src, dst, sems, u):
    return pltpu.make_async_copy(src.at[:, pl.ds(2 * u, 2)], dst.at[:, pl.ds(2 * u, 2)], sems.at[u])


def start_all(copy, src, dst, sems):
    for n in range(STEPS):
        copy(src, dst, sems, n).start()


def wait_all(copy, src, dst, sems):
    for n in range(STEPS):
        copy(src, dst, sems, n).wait()


def spectra_kernel(
    f_hbm, phase_hbm,
    out_ref, t_hbm, flat_hbm,
    f_ref, t_ref, flat_ref, ta_ref, tb_ref, acc_ref, pack_ref, phase_ref, f_sem, t_sem, p_sem, flat_sem,
):
    phases = pltpu.make_async_copy(phase_hbm, phase_ref, p_sem.at[0])
    phases.start()
    start_all(planes, f_hbm, f_ref, f_sem)
    acc_ref[...] = jnp.zeros_like(acc_ref)
    phases.wait()
    cr, sr = phase_ref[64:96, :], phase_ref[96:128, :]

    def make(n, ca, sa, buf_ref):
        for g in range(CHUNK // 128):
            cols = pl.ds(pl.multiple_of(n * CHUNK + g * 128, 128), 128)
            for l in range(L):
                v = (ca * phase_ref[128 + l : 129 + l, :] - sa * phase_ref[144 + l : 145 + l, :]).astype(BF16)
                buf_ref[l * 32 : l * 32 + 32, g * 128 : g * 128 + 128] = v
                t_ref[l * 32 : l * 32 + 32, cols] = v
            ca, sa = ca * cr - sa * sr, sa * cr + ca * sr
        return ca, sa

    def add(n, buf_ref):
        flat = f_ref[:, :, at(n)].reshape(ROWS, CHUNK)
        flat_ref[:, at(n)] = flat
        acc_ref[...] += nt(buf_ref[...], flat)
        columns(flat_ref, flat_hbm, flat_sem, n).start()

    ca, sa = make(0, phase_ref[:32, :], phase_ref[32:64, :], ta_ref)
    columns(t_ref, t_hbm, t_sem, 0).start()

    def step(m, carry):
        n = 2 * m
        planes(f_hbm, f_ref, f_sem, n).wait()
        planes(f_hbm, f_ref, f_sem, n + 1).wait()
        add(n, ta_ref)
        carry = make(n + 1, *carry, tb_ref)
        columns(t_ref, t_hbm, t_sem, n + 1).start()
        add(n + 1, tb_ref)
        carry = make(n + 2, *carry, ta_ref)
        columns(t_ref, t_hbm, t_sem, n + 2).start()
        return carry

    ca, sa = lax.fori_loop(0, STEPS // 2 - 1, step, (ca, sa))
    planes(f_hbm, f_ref, f_sem, STEPS - 2).wait()
    planes(f_hbm, f_ref, f_sem, STEPS - 1).wait()
    add(STEPS - 2, ta_ref)
    make(STEPS - 1, ca, sa, tb_ref)
    columns(t_ref, t_hbm, t_sem, STEPS - 1).start()
    add(STEPS - 1, tb_ref)
    out_ref[...] = pack_spectra(acc_ref[...], lane_order(), row_order(subl(SQUARE), lanes(SQUARE)), pack_ref)
    wait_all(columns, t_ref, t_hbm, t_sem)
    wait_all(columns, flat_ref, flat_hbm, flat_sem)


def mix_kernel(r_ref, w_hbm, fx_ref, iv_ref, out_ref, m_ref, w_ref, mask_ref, v_ref, w_sem):
    start_all(modes_pair, w_hbm, w_ref, w_sem)
    m = mm(fx_ref[...], r_ref[...])
    m_ref[...] = m.astype(BF16)
    shape = m.shape
    own = ((lanes(shape) >> 6) & 1) == ((subl(shape) >> 1) & 1)
    mask_ref[...] = jnp.where(own, m, 0.0)
    row, lane = subl((8, 128)), lanes((8, 128))
    top = row < 4
    even = (row & 1) == 0
    sign = jnp.where(lane < 64, -1.0, 1.0)
    keep = (lane >> 6) == ((row >> 1) & 1)

    def step(u, carry):
        cols = pl.ds(pl.multiple_of(u * 128, 128), 128)
        pair = pl.ds(2 * u, 2)
        modes_pair(w_hbm, w_ref, w_sem, u).wait()
        for t in range(8):
            left = mask_ref[8 * t : 8 * t + 8, cols].astype(BF16)
            right = jnp.concatenate(
                [w_ref[2 * t, pair].reshape(128, 128), w_ref[2 * t + 1, pair].reshape(128, 128)],
                axis=1,
            )
            o = mm(left, right)
            res = jnp.where(top, o[:, :128], o[:, 128:])
            turned = half_turn(res)
            above = pltpu.roll(turned, 7, 0)
            below = pltpu.roll(turned, 1, 0)
            v = jnp.where(even, res + sign * above, below - sign * res)
            v_ref[8 * t : 8 * t + 8, cols] = jnp.where(keep, v, 0.0)
        return carry

    lax.fori_loop(0, L // 2, step, 0)
    out_ref[...] = mm(iv_ref[...], v_ref[...].astype(BF16)).astype(BF16)


def slope(v):
    a = jnp.abs(v)
    e = jnp.exp(v * v * -0.5)
    t = 1.0 / (1.0 + (0.3275911 / math.sqrt(2.0)) * a)
    poly = t * (
        0.5 * 0.254829592
        + t
        * (
            0.5 * -0.284496736
            + t * (0.5 * 1.421413741 + t * (0.5 * -1.453152027 + t * (0.5 * 1.061405429)))
        )
    )
    tail = e * (poly - a * (1.0 / math.sqrt(2.0 * math.pi)))
    return jnp.where(v < 0, tail, 1.0 - tail)


def delta_kernel(
    r_ref, f_hbm, ct_hbm, t_hbm, w_ref, bias_ref,
    out_ref, d_hbm,
    f_ref, ct_ref, t_ref, d_ref, b_ref, lw_ref, shift_ref, pa_ref, pb_ref, da_ref, db_ref,
    s_ref, g_ref, bt_ref, z_ref, f_sem, ct_sem, t_sem, d_sem,
):
    for n in range(STEPS):
        columns(t_hbm, t_ref.at[:Q], t_sem, n).start()
        columns(f_hbm, f_ref, f_sem, n).start()
        columns(ct_hbm, ct_ref, ct_sem, n).start()
    t_ref[Q:, :] = jnp.ones((16, CELLS), BF16)
    b_ref[...] = unpack_back(
        r_ref[...], lane_order(), row_order(lanes(SQUARE), subl(SQUARE)), bt_ref, True
    )
    lw_ref[...] = spread_weight(w_ref[...])
    e = (subl((ROWS, C)) // XL == lanes((ROWS, C))).astype(F32)
    shift_ref[...] = EXACT(e, jnp.broadcast_to(bias_ref[...], (128, C)), NT)
    s_ref[...] = jnp.zeros_like(s_ref)
    g_ref[...] = jnp.zeros_like(g_ref)
    db_ref[...] = jnp.zeros_like(db_ref)

    def arrive(n):
        columns(t_hbm, t_ref.at[:Q], t_sem, n).wait()
        columns(f_hbm, f_ref, f_sem, n).wait()

    def before(n, p_ref, halves=(0, 1)):
        for h in halves:
            cols = pl.ds(pl.multiple_of(n * CHUNK + h * 256, 256), 256)
            p_ref[:, h * 256 : h * 256 + 256] = mm(b_ref[...], t_ref[:Q, cols]) + mm(
                lw_ref[...], f_ref[:, cols]
            )

    def add_spectra(n, own_ref, first, last):
        s_ref[first:last, :] += nt(t_ref[first:last, at(n)], own_ref[...])

    def add_point(n, own_ref):
        g_ref[...] += nt(own_ref[...], f_ref[:, at(n)])

    def bend(n, p_ref, own_ref, blocks):
        for r in blocks:
            rows = slice(r * 16, r * 16 + 16)
            v = p_ref[rows, :] + jnp.concatenate([shift_ref[rows, :]] * (CHUNK // 128), axis=1)
            d = (ct_ref[rows, at(n)].astype(F32) * slope(v)).astype(BF16)
            own_ref[rows, :] = d
            d_ref[rows, at(n)] = d

    def weave(n, p_ref, next_ref, own_ref, past_ref):
        past, later = jnp.maximum(n - 1, 0), jnp.minimum(n + 1, STEPS - 1)
        add_spectra(past, past_ref, 0, 256)
        bend(n, p_ref, own_ref, range(0, 3))
        add_spectra(past, past_ref, 256, Q + 16)
        bend(n, p_ref, own_ref, range(3, 6))
        add_point(past, past_ref)
        bend(n, p_ref, own_ref, range(6, 9))
        before(later, next_ref, (0,))
        bend(n, p_ref, own_ref, range(9, 12))
        before(later, next_ref, (1,))
        bend(n, p_ref, own_ref, range(12, 16))
        columns(d_ref, d_hbm, d_sem, n).start()

    arrive(0)
    before(0, pa_ref)

    def step(m, carry):
        n = 2 * m
        columns(ct_hbm, ct_ref, ct_sem, n).wait()
        columns(ct_hbm, ct_ref, ct_sem, n + 1).wait()
        arrive(n + 1)

        @pl.when(m < STEPS // 2 - 1)
        def _():
            arrive(n + 2)

        weave(n, pa_ref, pb_ref, da_ref, db_ref)
        weave(n + 1, pb_ref, pa_ref, db_ref, da_ref)
        return carry

    lax.fori_loop(0, STEPS // 2, step, 0)
    add_spectra(STEPS - 1, db_ref, 0, Q + 16)
    add_point(STEPS - 1, db_ref)
    doubled = jnp.where(subl((Q, ROWS)) < 32, 1.0, 2.0)
    out_ref[:, :1024] = pack_spectra(
        s_ref[:Q, :] * doubled, lane_order(), row_order(subl(SQUARE), lanes(SQUARE)), z_ref
    )
    same = (subl((ROWS, ROWS)) & 3) == (lanes((ROWS, ROWS)) & 3)
    g = jnp.where(same, g_ref[...], 0.0)
    e = (subl((C, ROWS)) == lanes((C, ROWS)) // XL).astype(F32)
    e2 = ((subl((ROWS, 128)) // XL) == (lanes((ROWS, 128)) & 63)).astype(F32)
    wg = EXACT(EXACT(e, g, NN), e2, NN)
    bg = EXACT(e, jnp.broadcast_to(s_ref[Q : Q + 1, :], (128, ROWS)), NT)
    both = jnp.concatenate([wg, bg], axis=0)
    out_ref[:, 1024:] = mm(ext_order(subl(SQUARE), lanes(SQUARE)), split(both)).astype(BF16)
    wait_all(columns, d_ref, d_hbm, d_sem)


def total_of(ext):
    shape = (8, 128)
    pick = ((lanes(shape) & 7) == subl(shape)).astype(BF16)
    v = mm(pick, ext)
    return v + half_turn(v)


def spread_total(v):
    return jnp.concatenate([split(v).astype(F32)] * S, axis=0).astype(BF16)


def grad_modes_kernel(r_ref, m_ref, fx_ref, fo_ref, gather_ref, left_ref, dp_ref):
    r = r_ref[:, :1024]
    a = mm(fx_ref[...], r)
    b = mm(fo_ref[...], r)
    row = subl((64, 128))
    first = ((row >> 1) & 1) == 0
    low = low_half((64, 128))
    for u in range(8):
        cols = slice(u * 128, u * 128 + 128)
        au, bu = a[:, cols], b[:, cols]
        left_ref[:, cols] = jnp.where(
            first, jnp.where(low, au, half_turn(bu)), jnp.where(low, half_turn(au), bu)
        ).astype(BF16)
    both = jnp.concatenate([m_ref[...], a.astype(BF16)], axis=0)
    dp_ref[:, :512] = (
        mm(gather_ref[0], both[:, :512]) + mm(gather_ref[1], both[:, 512:])
    ).astype(BF16)
    dp_ref[:, 512:] = spread_total(total_of(r_ref[:, 1024:]))


def adjoint_kernel(left_ref, w_hbm, ia_ref, out_ref, w_ref, v_ref, w_sem):
    start_all(modes_pair, w_hbm, w_ref, w_sem)
    row, lane = subl((8, 128)), lanes((8, 128))
    top = row < 4
    keep = (lane >> 6) == ((row >> 1) & 1)

    def step(u, carry):
        cols = pl.ds(pl.multiple_of(u * 128, 128), 128)
        pair = pl.ds(2 * u, 2)
        modes_pair(w_hbm, w_ref, w_sem, u).wait()
        for t in range(8):
            right = jnp.concatenate(
                [w_ref[2 * t, pair].reshape(128, 128), w_ref[2 * t + 1, pair].reshape(128, 128)],
                axis=0,
            )
            o = nt(left_ref[8 * t : 8 * t + 8, cols], right)
            res = jnp.where(top, o[:, :128], o[:, 128:])
            v_ref[8 * t : 8 * t + 8, cols] = jnp.where(keep, res, 0.0)
        return carry

    lax.fori_loop(0, L // 2, step, 0)
    out_ref[...] = mm(ia_ref[...], v_ref[...].astype(BF16)).astype(BF16)


def join_kernel(v_ref, dp_ref, out_ref):
    out_ref[:, :1024] = v_ref[...]
    out_ref[:, 1024:] = spread_total(total_of(dp_ref[:, 512:]))


def weight_grad_kernel(dp_ref, pick_ref, out_ref):
    low = low_half((32, 128))
    data = dp_ref[:, :512]
    for h in range(2):
        m = mm(pick_ref[h * 3], data)
        g1 = mm(pick_ref[h * 3 + 1], data)
        g2 = mm(pick_ref[h * 3 + 2], data)
        for v in range(4):
            cols = slice(v * 128, v * 128 + 128)
            a, b = g1[:, cols], g2[:, cols]
            right = jnp.concatenate(
                [jnp.where(low, a, half_turn(b)), jnp.where(low, half_turn(a), b)], axis=1
            )
            o = tn(m[:, cols].astype(BF16), right.astype(BF16)) * 0.25
            l = h * 8 + v * 2
            out_ref[l] = o[:64, :128]
            out_ref[l + 1] = o[64:, 128:]


def input_grad_kernel(
    r_ref, d_hbm, t_hbm, w_ref,
    out_hbm, pg_hbm, bg_hbm,
    d_ref, t_ref, o_ref, b_ref, lw_ref, bt_ref, pg_ref, bg_ref, d_sem, t_sem, o_sem, g_sem,
):
    for n in range(STEPS):
        columns(t_hbm, t_ref, t_sem, n).start()
        columns(d_hbm, d_ref, d_sem, n).start()
    b_ref[...] = unpack_back(
        r_ref[:, :1024], lane_order(), row_order(lanes(SQUARE), subl(SQUARE)), bt_ref, False
    )
    lw_ref[...] = spread_weight(w_ref[...]).astype(F32).T.astype(BF16)
    v = mm(ext_order(lanes(SQUARE), subl(SQUARE)), r_ref[:, 1024:])
    v = (v + half_turn(v)) * (1.0 / 2048.0)
    pg_ref[...] = v[:C, :C]
    diag = subl((C, C)) == lanes((C, C))
    bg_ref[...] = jnp.sum(jnp.where(diag, v[C:, :C], 0.0), axis=0, keepdims=True)
    small = [
        pltpu.make_async_copy(pg_ref, pg_hbm, g_sem.at[0]),
        pltpu.make_async_copy(bg_ref, bg_hbm, g_sem.at[1]),
    ]
    for copy in small:
        copy.start()

    def step(n, carry):
        columns(t_hbm, t_ref, t_sem, n).wait()
        columns(d_hbm, d_ref, d_sem, n).wait()
        out = mm(b_ref[...], t_ref[:, at(n)]) + mm(lw_ref[...], d_ref[:, at(n)])
        o_ref[:, :, at(n)] = out.astype(BF16).reshape(C, XL, CHUNK)
        planes(o_ref, out_hbm, o_sem, n).start()
        return carry

    lax.fori_loop(0, STEPS, step, 0)
    wait_all(planes, o_ref, out_hbm, o_sem)
    for copy in small:
        copy.wait()


def call(kernel, name, outs, scratch, args, big=(), big_outs=(), sems=0):
    place = lambda n, far: pl.BlockSpec(memory_space=pltpu.HBM if n in far else pltpu.VMEM)
    return pl.pallas_call(
        kernel,
        in_specs=[place(n, big) for n in range(len(args))],
        out_specs=[place(n, big_outs) for n in range(len(outs))],
        out_shape=[
            (pltpu.HBM if n in big_outs else pltpu.VMEM)(shape, dtype)
            for n, (shape, dtype) in enumerate(outs)
        ],
        scratch_shapes=[pltpu.VMEM(shape, dtype) for shape, dtype in scratch]
        + [pltpu.SemaphoreType.DMA((STEPS,))] * sems,
        compiler_params=pltpu.CompilerParams(vmem_limit_bytes=40 << 20),
        name=name,
    )(
        *[
            pltpu.with_memory_space_constraint(a, pltpu.HBM if n in big else pltpu.VMEM)
            for n, a in enumerate(args)
        ]
    )


def exchange(v, axis):
    width = v.shape[1]
    out = lax.all_to_all(v.reshape(S, 8, width), axis, split_axis=0, concat_axis=0, tiled=True)
    return out.reshape(128, width)


def body(field, cotangent, spectral_weight, point_weight, bias):
    k = constants()
    field3 = field.reshape(C, XL, CELLS)
    cot2 = cotangent.reshape(ROWS, CELLS)
    planes_shape = ((C, XL, CELLS), BF16)
    cells_shape = ((ROWS, CELLS), BF16)
    weight_shape = (spectral_weight.shape, BF16)

    spectra, table, flat = call(
        spectra_kernel,
        "spectra",
        [((128, 1024), BF16), ((Q, CELLS), BF16), cells_shape],
        [planes_shape, ((Q, CELLS), BF16), cells_shape, ((Q, CHUNK), BF16), ((Q, CHUNK), BF16),
         ((Q, ROWS), F32), ((128, 1024), BF16), ((160, 128), F32)],
        [field3, jnp.asarray(phase_tables())],
        big=(0, 1), big_outs=(1, 2), sems=4,
    )
    arrived = exchange(spectra, "slab")
    back, modes = call(
        mix_kernel,
        "mix",
        [((128, 1024), BF16), ((64, 1024), BF16)],
        [weight_shape, ((64, 1024), F32), ((64, 1024), F32)],
        [arrived, spectral_weight, k["fx"], k["iv"]],
        big=(1,), sems=1,
    )
    arrived = exchange(back, "slab")
    grad_spectra, delta = call(
        delta_kernel,
        "delta",
        [((128, 1152), BF16), cells_shape],
        [
            cells_shape, cells_shape, ((Q + 16, CELLS), BF16), cells_shape,
            ((ROWS, Q), BF16), ((ROWS, ROWS), BF16), ((ROWS, 128), F32),
            ((ROWS, CHUNK), F32), ((ROWS, CHUNK), F32), ((ROWS, CHUNK), BF16), ((ROWS, CHUNK), BF16),
            ((Q + 16, ROWS), F32), ((ROWS, ROWS), F32), ((Q, ROWS), BF16), ((128, 1024), BF16),
        ],
        [arrived, flat, cot2, table, point_weight, bias.reshape(1, C)],
        big=(1, 2, 3), big_outs=(1,), sems=4,
    )
    arrived = exchange(grad_spectra, "slab")
    left, shared = call(
        grad_modes_kernel,
        "grad_modes",
        [((64, 1024), BF16), ((128, 640), BF16)],
        [],
        [arrived, modes, k["fx"], k["fo"], k["gather"]],
    )
    shared = exchange(shared, "dp")
    (adjoint,) = call(
        adjoint_kernel,
        "adjoint",
        [((128, 1024), BF16)],
        [weight_shape, ((64, 1024), F32)],
        [left, spectral_weight, k["ia"]],
        big=(1,), sems=1,
    )
    (joined,) = call(join_kernel, "join", [((128, 1152), BF16)], [], [adjoint, shared])
    arrived = exchange(joined, "slab")
    (spectral_grad,) = call(
        weight_grad_kernel, "weight_grad", [((L, C, 128), F32)], [], [shared, k["pick"]]
    )
    input_grad, point_grad, bias_grad = call(
        input_grad_kernel,
        "input_grad",
        [planes_shape, ((C, C), F32), ((1, C), F32)],
        [cells_shape, ((Q, CELLS), BF16), planes_shape,
         ((ROWS, Q), BF16), ((ROWS, ROWS), BF16), ((Q, ROWS), BF16), ((C, C), F32), ((1, C), F32)],
        [arrived, delta, table, point_weight],
        big=(1, 2), big_outs=(0, 1, 2), sems=4,
    )
    return (
        input_grad.reshape(field.shape),
        spectral_grad[None],
        point_grad,
        bias_grad.reshape(C),
    )


def solution(mesh):
    return jax.shard_map(
        body,
        mesh=mesh,
        in_specs=(
            P("dp", None, "slab", None),
            P("dp", None, "slab", None),
            P(None, "slab", None, None),
            P(),
            P(),
        ),
        out_specs=(P("dp", None, "slab", None), P("dp", "slab", None, None), P(), P()),
        check_vma=False,
    )
```

time: 129 us -> 99.4 us (0.77)
  Pallas kernels: 51.4 us -> 32.7 us
  local copies, waits for them, and re-layouts: 15.8 us -> 2.95 us
  waiting for transfers between devices: 13 us -> 17.9 us
  blocking collectives: 27.1 us -> 25.2 us
    pallas_call x8, Pallas kernels: 51.4 us -> 32.7 us  [call(): pl.pallas_call(kernel, in_specs=[place(n, big) for n in range(len(args))]...]
    reshape x3 -> x0, local copies, waits for them, and re-layouts: 8.79 us -> none  [the longest x1 4.09 us: body(): input_grad.reshape(field.shape)]
    all_to_all x3, waiting for transfers between devices: 13 us -> 17.9 us  [exchange(): lax.all_to_all(v.reshape(S, 8, width), axis, split_axis=0, concat_axis=0,...]
    slice x2 -> x0, local copies, waits for them, and re-layouts: 2.76 us -> none  [the longest x1 1.38 us: body(): small[C:, 0]]
    all_to_all x2, blocking collectives: 27.1 us -> 25.2 us  [exchange(): lax.all_to_all(v.reshape(S, 8, width), axis, split_axis=0, concat_axis=0,...]
  transfers between devices with their start and end apart: 3 -> 3, of which waited for: 3 -> 3; matrix products, arithmetic and copies ran while one was open for 2% -> 3% of each run, Pallas kernels for 7% -> 4%
where the time goes in v1:
time: 99.4 us; the launch traced here: 98.9 us
  Pallas kernels  32.7 us (33%)
  blocking collectives  25.2 us (25%)
  starting transfers between devices  19.5 us (20%)
  waiting for transfers between devices  17.9 us (18%)
  local copies, waits for them, and re-layouts  2.95 us (3%)
    pallas_call x8, Pallas kernels, call(): pl.pallas_call(kernel, in_specs=[place(n, big) for n in range(len(args))]...  32.7 us
    all_to_all x2, blocking collectives, exchange(): lax.all_to_all(v.reshape(S, 8, width), axis, split_axis=0, concat_axis=0,...  25.2 us
    all_to_all x3, starting transfers between devices, exchange(): lax.all_to_all(v.reshape(S, 8, width), axis, split_axis=0, concat_axis=0,...  19.5 us
    all_to_all x3, waiting for transfers between devices, exchange(): lax.all_to_all(v.reshape(S, 8, width), axis, split_axis=0, concat_axis=0,...  17.9 us
    reshape x1, local copies, waits for them, and re-layouts, body(): cot2 = cotangent.reshape(ROWS, CELLS)  2.1 us
  transfers between devices with their start and end apart: 3, of which 3 were waited for; matrix products, arithmetic and copies ran while one was open for 3% of the time, Pallas kernels for 4%

profile of v1, /device:TPU:1, one launch (start us, length us, event | category | flops | bytes accessed | tf_op | source)
XLA Modules:
  0.0 98.9 jit_solution(7816388634609074634)
XLA Ops:
  0.6 0.0 copy-start.1
  0.6 0.0 copy-start.5
  0.7 6.2 %spectra.1 = (bf16[128,1024]{1,0:T(8,128)(2,1)S(1)}, bf16[512,4096]{1,0:T(8,128)(2,1)}, bf16[256,4096]{1,0:T(8,128)(2,1)}) custom-call(bf16[64,4,4096]{2,1,0:T(4,128)(2,1)} %bitcast.25, f32[160,128]{1,0:T(8,128)} %constant.20.clone.phase_hbm), custom_call_target="tpu_custom_call" | custom-call | tf_op jit(solution)/shard_map/spectra/pallas_call | solution.py:539
  6.9 14.3 %all_to_all.25 = bf16[16,8,1024]{2,1,0:T(8,128)(2,1)S(1)} all-to-all(bf16[16,8,1024]{2,1,0:T(8,128)(2,1)S(1)} %bitcast.23), channel_id=1, replica_groups=mesh['dp'=16,'slab'=16] {'slab'}, dimensions={0} | all-to-all | bytes 524288 | tf_op jit(solution)/shard_map/all_to_all | solution.py:561
  21.2 4.3 %mix.1 = (bf16[128,1024]{1,0:T(8,128)(2,1)}, bf16[64,1024]{1,0:T(8,128)(2,1)S(1)}) custom-call(bf16[128,1024]{1,0:T(8,128)(2,1)S(1)} %bitcast.21, bf16[16,16,64,128]{3,2,1,0:T(8,128)(2,1)} %w_hbm.3, bf16[64,128]{1,0:T(8,128)(2,1)S(1)} %copy-done.1, bf16[128,64]{1,0:T(8,128)(2,1)S(1)} %copy-done.5), custom_call_target="tpu_custom_call" | custom-call | tf_op jit(solution)/shard_map/mix/pallas_call | solution.py:539
  25.5 4.3 %all-to-all-start.1 = ((bf16[16,8,1024]{2,1,0:T(8,128)(2,1)}), bf16[16,8,1024]{2,1,0:T(8,128)(2,1)S(1)}, u32[]{:S(2)}, u32[]{:S(2)}) async-start(bf16[16,8,1024]{2,1,0:T(8,128)(2,1)} %bitcast.3), calls=%async_computation.1 | async-start | bytes 524288 | tf_op jit(solution)/shard_map/all_to_all | solution.py:561
  29.8 0.0 copy-start
  29.8 0.0 copy-start.7
  29.8 2.1 %reshape.58.ct_hbm = bf16[256,4096]{1,0:T(8,128)(2,1)} reshape(bf16[1,64,4,4096]{3,2,1,0:T(4,128)(2,1)S(1)} %copy-done.8) | data formatting | bytes 4194304 | tf_op jit(solution)/shard_map/reshape | solution.py:568
  31.9 5.1 %all-to-all-done.1 = bf16[16,8,1024]{2,1,0:T(8,128)(2,1)S(1)} async-done(((bf16[16,8,1024]{2,1,0:T(8,128)(2,1)}), bf16[16,8,1024]{2,1,0:T(8,128)(2,1)S(1)}, u32[]{:S(2)}, u32[]{:S(2)}) %all-to-all-start.1) | async-done | bytes 262176 | tf_op jit(solution)/shard_map/all_to_all | solution.py:561
  37.0 0.0 copy-start.4
  37.0 10.5 %delta.1 = (bf16[128,1152]{1,0:T(8,128)(2,1)S(1)}, bf16[256,4096]{1,0:T(8,128)(2,1)}) custom-call(bf16[128,1024]{1,0:T(8,128)(2,1)S(1)} %bitcast.20, bf16[256,4096]{1,0:T(8,128)(2,1)} %get-tuple-element.18.f_hbm, bf16[256,4096]{1,0:T(8,128)(2,1)} %reshape.58.ct_hbm, bf16[512,4096]{1,0:T(8,128)(2,1)} %get-tuple-element.19.t_hbm, bf16[64,64]{1,0:T(8,128)(2,1)S(1)} %copy-done, ...), custom_call_target="tpu_custom_call" | custom-call | tf_op jit(solution)/shard_map/delta/pallas_call | solution.py:539
  47.5 10.9 %all_to_all.26 = bf16[16,8,1152]{2,1,0:T(8,128)(2,1)S(1)} all-to-all(bf16[16,8,1152]{2,1,0:T(8,128)(2,1)S(1)} %bitcast.22), channel_id=1, replica_groups=mesh['dp'=16,'slab'=16] {'slab'}, dimensions={0} | all-to-all | bytes 589824 | tf_op jit(solution)/shard_map/all_to_all | solution.py:561
  58.4 1.1 %grad_modes.1 = (bf16[64,1024]{1,0:T(8,128)(2,1)S(1)}, bf16[128,640]{1,0:T(8,128)(2,1)}) custom-call(bf16[128,1152]{1,0:T(8,128)(2,1)S(1)} %bitcast.19, bf16[64,1024]{1,0:T(8,128)(2,1)S(1)} %get-tuple-element.21.m_ref, bf16[64,128]{1,0:T(8,128)(2,1)S(1)} %copy-done.1, bf16[64,128]{1,0:T(8,128)(2,1)S(1)} %copy-done.6, bf16[2,128,128]{2,1,0:T(8,128)(2,1)S(1)} %copy-done.2), custom_call_target="tpu_custom_call" | custom-call | tf_op jit(solution)/shard_map/grad_modes/pallas_call | solution.py:539
  59.6 9.9 %all-to-all-start.3 = ((bf16[16,8,640]{2,1,0:T(8,128)(2,1)}), bf16[16,8,640]{2,1,0:T(8,128)(2,1)S(1)}, u32[]{:S(2)}, u32[]{:S(2)}) async-start(bf16[16,8,640]{2,1,0:T(8,128)(2,1)} %bitcast.8), calls=%async_computation.3 | async-start | bytes 327680 | tf_op jit(solution)/shard_map/all_to_all | solution.py:561
  69.4 0.0 copy-start.3
  69.5 3.4 %adjoint.1.v_ref = bf16[128,1024]{1,0:T(8,128)(2,1)S(1)} custom-call(bf16[64,1024]{1,0:T(8,128)(2,1)S(1)} %get-tuple-element.22.left_ref, bf16[16,16,64,128]{3,2,1,0:T(8,128)(2,1)} %w_hbm.3, bf16[128,64]{1,0:T(8,128)(2,1)S(1)} %copy-done.4), custom_call_target="tpu_custom_call" | custom-call | tf_op jit(solution)/shard_map/adjoint/pallas_call | solution.py:539
  72.8 6.8 %all-to-all-done.3 = bf16[16,8,640]{2,1,0:T(8,128)(2,1)S(1)} async-done(((bf16[16,8,640]{2,1,0:T(8,128)(2,1)}), bf16[16,8,640]{2,1,0:T(8,128)(2,1)S(1)}, u32[]{:S(2)}, u32[]{:S(2)}) %all-to-all-start.3) | async-done | bytes 163872 | tf_op jit(solution)/shard_map/all_to_all | solution.py:561
  79.6 0.9 join.1
  80.5 5.3 %all-to-all-start.4 = ((bf16[16,8,1152]{2,1,0:T(8,128)(2,1)}), bf16[16,8,1152]{2,1,0:T(8,128)(2,1)S(1)}, u32[]{:S(2)}, u32[]{:S(2)}) async-start(bf16[16,8,1152]{2,1,0:T(8,128)(2,1)} %bitcast.10), calls=%async_computation.4 | async-start | bytes 589824 | tf_op jit(solution)/shard_map/all_to_all | solution.py:561
  85.9 0.8 weight_grad.1
  86.7 0.8 copy.16
  87.5 5.9 %all-to-all-done.4 = bf16[16,8,1152]{2,1,0:T(8,128)(2,1)S(1)} async-done(((bf16[16,8,1152]{2,1,0:T(8,128)(2,1)}), bf16[16,8,1152]{2,1,0:T(8,128)(2,1)S(1)}, u32[]{:S(2)}, u32[]{:S(2)}) %all-to-all-start.4) | async-done | bytes 294944 | tf_op jit(solution)/shard_map/all_to_all | solution.py:561
  93.4 5.5 %input_grad.1 = (bf16[64,4,4096]{2,1,0:T(4,128)(2,1)}, f32[64,64]{1,0:T(8,128)}, f32[1,64]{1,0:T(1,128)}) custom-call(bf16[128,1152]{1,0:T(8,128)(2,1)S(1)} %bitcast.18, bf16[256,4096]{1,0:T(8,128)(2,1)} %get-tuple-element.24.d_hbm, bf16[512,4096]{1,0:T(8,128)(2,1)} %get-tuple-element.19.t_hbm, bf16[64,64]{1,0:T(8,128)(2,1)S(1)} %copy-done), custom_call_target="tpu_custom_call" | custom-call | tf_op jit(solution)/shard_map/input_grad/pallas_call | solution.py:539
  (12 shorter events, 0.0 us)
Async XLA Ops:
  0.6 20.6 %copy-start.1 = (bf16[64,128]{1,0:T(8,128)(2,1)S(1)}, bf16[64,128]{1,0:T(8,128)(2,1)}, u32[]{:S(2)}) copy-start(bf16[64,128]{1,0:T(8,128)(2,1)} %constant.14.clone.fx_ref) | copy-start | bytes 49156
  0.6 20.6 %copy-start.5 = (bf16[128,64]{1,0:T(8,128)(2,1)S(1)}, bf16[128,64]{1,0:T(8,128)(2,1)}, u32[]{:S(2)}) copy-start(bf16[128,64]{1,0:T(8,128)(2,1)} %constant.16.clone.iv_ref) | copy-start | bytes 49156
  21.2 8.5 %copy-start.8 = (bf16[1,64,4,4096]{3,2,1,0:T(4,128)(2,1)S(1)}, bf16[1,64,4,4096]{3,2,1,0:T(4,128)(2,1)}, u32[]{:S(2)}) copy-start(bf16[1,64,4,4096]{3,2,1,0:T(4,128)(2,1)} %param.13) | copy-start | bytes 6291460
  25.5 11.5 %all-to-all-start.1 = ((bf16[16,8,1024]{2,1,0:T(8,128)(2,1)}), bf16[16,8,1024]{2,1,0:T(8,128)(2,1)S(1)}, u32[]{:S(2)}, u32[]{:S(2)}) async-start(bf16[16,8,1024]{2,1,0:T(8,128)(2,1)} %bitcast.3), calls=%async_computation.1 | async-start | bytes 524288 | tf_op jit(solution)/shard_map/all_to_all | solution.py:561
  29.8 7.3 %copy-start = (bf16[64,64]{1,0:T(8,128)(2,1)S(1)}, bf16[64,64]{1,0:T(8,128)(2,1)}, u32[]{:S(2)}) copy-start(bf16[64,64]{1,0:T(8,128)(2,1)} %w_ref.3) | copy-start | bytes 24580
  29.8 7.3 %copy-start.7 = (f32[64]{0:T(128)S(1)}, f32[64]{0:T(128)}, u32[]{:S(2)}) copy-start(f32[64]{0:T(128)} %param.16) | copy-start | bytes 772
  37.0 21.4 %copy-start.2 = (bf16[2,128,128]{2,1,0:T(8,128)(2,1)S(1)}, bf16[2,128,128]{2,1,0:T(8,128)(2,1)}, u32[]{:S(2)}) copy-start(bf16[2,128,128]{2,1,0:T(8,128)(2,1)} %constant.18.clone.gather_ref) | copy-start | bytes 196612
  37.0 21.4 %copy-start.6 = (bf16[64,128]{1,0:T(8,128)(2,1)S(1)}, bf16[64,128]{1,0:T(8,128)(2,1)}, u32[]{:S(2)}) copy-start(bf16[64,128]{1,0:T(8,128)(2,1)} %constant.15.clone.fo_ref) | copy-start | bytes 49156
  37.0 32.4 %copy-start.4 = (bf16[128,64]{1,0:T(8,128)(2,1)S(1)}, bf16[128,64]{1,0:T(8,128)(2,1)}, u32[]{:S(2)}) copy-start(bf16[128,64]{1,0:T(8,128)(2,1)} %constant.17.clone.ia_ref) | copy-start | bytes 49156
  59.6 20.1 %all-to-all-start.3 = ((bf16[16,8,640]{2,1,0:T(8,128)(2,1)}), bf16[16,8,640]{2,1,0:T(8,128)(2,1)S(1)}, u32[]{:S(2)}, u32[]{:S(2)}) async-start(bf16[16,8,640]{2,1,0:T(8,128)(2,1)} %bitcast.8), calls=%async_computation.3 | async-start | bytes 327680 | tf_op jit(solution)/shard_map/all_to_all | solution.py:561
  69.4 16.4 %copy-start.3 = (bf16[6,32,128]{2,1,0:T(8,128)(2,1)S(1)}, bf16[6,32,128]{2,1,0:T(8,128)(2,1)}, u32[]{:S(2)}) copy-start(bf16[6,32,128]{2,1,0:T(8,128)(2,1)} %constant.19.clone.pick_ref) | copy-start | bytes 147460
  80.5 12.9 %all-to-all-start.4 = ((bf16[16,8,1152]{2,1,0:T(8,128)(2,1)}), bf16[16,8,1152]{2,1,0:T(8,128)(2,1)S(1)}, u32[]{:S(2)}, u32[]{:S(2)}) async-start(bf16[16,8,1152]{2,1,0:T(8,128)(2,1)} %bitcast.10), calls=%async_computation.4 | async-start | bytes 589824 | tf_op jit(solution)/shard_map/all_to_all | solution.py:561

commit v2 on v1

--- a/solution.py
+++ b/solution.py
@@ -39,8 +39,8 @@
 
 def phase_tables():
     f = np.float32
-    k = np.repeat(waves(S, N), 2)[:, None]
-    part = np.tile([0.0, np.pi / 2], S)[:, None]
+    k = np.tile(waves(S, N), 2)[:, None]
+    part = np.repeat([0.0, np.pi / 2], S)[:, None]
     unit = 2.0 * np.pi / N
     ang = unit * (k * (np.arange(128) // N)[None, :]) + part
     turn = unit * np.broadcast_to(2 * k, (2 * S, 128))
@@ -116,27 +116,36 @@
     return pltpu.roll(v, 64, 1)
 
 
-def pack_spectra(acc, perm, order, z_ref):
+def pack_spectra(acc, perm, z_ref, out_ref):
     s = mm(acc.astype(BF16), perm)
     low = low_half((32, 128))
+
+    def put(x, u, v):
+        z_ref[u, pl.ds(2 * x, S, stride=8), :] = v[:S]
+        z_ref[u, pl.ds(2 * x + 1, S, stride=8), :] = v[S:]
+
     for u in range(L // 2):
         for t in range(2):
             a = s[u * 64 : u * 64 + 32, t * 128 : t * 128 + 128]
             b = s[u * 64 + 32 : u * 64 + 64, t * 128 : t * 128 + 128]
-            even = jnp.where(low, a, half_turn(b))
-            odd = jnp.where(low, half_turn(a), b)
-            z_ref[t * 64 : t * 64 + 32, u * 128 : u * 128 + 128] = even.astype(BF16)
-            z_ref[t * 64 + 32 : t * 64 + 64, u * 128 : u * 128 + 128] = odd.astype(BF16)
-    return mm(order, z_ref[...]).astype(BF16)
-
-
-def unpack_back(arrived, perm, order_t, b_ref, doubled):
-    z = mm(order_t, arrived)
+            put(2 * t, u, jnp.where(low, a, half_turn(b)))
+            put(2 * t + 1, u, jnp.where(low, half_turn(a), b))
+    for u in range(L // 2):
+        out_ref[:, u * 128 : u * 128 + 128] = z_ref[u].astype(BF16)
+
+
+def unpack_back(arrived, perm, z_ref, b_ref, doubled):
+    for u in range(L // 2):
+        z_ref[u] = arrived[:, u * 128 : u * 128 + 128].astype(F32)
     low = low_half((32, 128))
+
+    def take(x, u):
+        parts = [z_ref[u, pl.ds(2 * x + p, S, stride=8), :] for p in range(2)]
+        return jnp.concatenate(parts, axis=0)
+
     for u in range(L // 2):
         for t in range(2):
-            a = z[t * 64 : t * 64 + 32, u * 128 : u * 128 + 128]
-            b = z[t * 64 + 32 : t * 64 + 64, u * 128 : u * 128 + 128]
+            a, b = take(2 * t, u), take(2 * t + 1, u)
             first = jnp.where(low, a, half_turn(b))
             second = jnp.where(low, half_turn(a), b)
             if doubled:
@@ -147,9 +156,13 @@
     return nt(perm, b_ref[...]).astype(BF16)
 
 
+def halves_of(v):
+    hi = v.astype(BF16)
+    return hi, (v - hi.astype(F32)).astype(BF16)
+
+
 def split(v):
-    hi = v.astype(BF16)
-    lo = (v - hi.astype(F32)).astype(BF16)
+    hi, lo = halves_of(v)
     return jnp.where(low_half(v.shape), hi.astype(F32), lo.astype(F32)).astype(BF16)
 
 
@@ -168,10 +181,6 @@
 def lane_order():
     r, k = subl((ROWS, ROWS)), lanes((ROWS, ROWS))
     return onehot(((r >> 2) == (k & 63)) & ((r & 3) == (k >> 6)))
-
-
-def row_order(r, k):
-    return onehot(((r >> 3) == ((k >> 1) & 15)) & (((r >> 1) & 3) == (k >> 5)) & ((r & 1) == (k & 1)))
 
 
 def ext_order(r, k):
@@ -190,6 +199,8 @@
 
 
 def at(step):
+    if isinstance(step, int):
+        return slice(step * CHUNK, step * CHUNK + CHUNK)
     return pl.ds(pl.multiple_of(step * CHUNK, CHUNK), CHUNK)
 
 
@@ -217,57 +228,59 @@
 
 def spectra_kernel(
     f_hbm, phase_hbm,
-    out_ref, t_hbm, flat_hbm,
-    f_ref, t_ref, flat_ref, ta_ref, tb_ref, acc_ref, pack_ref, phase_ref, f_sem, t_sem, p_sem, flat_sem,
+    out_ref, t_hbm,
+    f_ref, t_ref, ta_ref, tb_ref, acc_ref, z_ref, phase_ref, f_sem, t_sem, p_sem,
 ):
     phases = pltpu.make_async_copy(phase_hbm, phase_ref, p_sem.at[0])
     phases.start()
     start_all(planes, f_hbm, f_ref, f_sem)
     acc_ref[...] = jnp.zeros_like(acc_ref)
+    perm = lane_order()
     phases.wait()
     cr, sr = phase_ref[64:96, :], phase_ref[96:128, :]
 
-    def make(n, ca, sa, buf_ref):
-        for g in range(CHUNK // 128):
+    def make(n, ca, sa, buf_ref, tiles):
+        for g in tiles:
             cols = pl.ds(pl.multiple_of(n * CHUNK + g * 128, 128), 128)
             for l in range(L):
-                v = (ca * phase_ref[128 + l : 129 + l, :] - sa * phase_ref[144 + l : 145 + l, :]).astype(BF16)
+                cb, sb = phase_ref[128 + l : 129 + l, :], phase_ref[144 + l : 145 + l, :]
+                v = (ca * cb - sa * sb).astype(BF16)
                 buf_ref[l * 32 : l * 32 + 32, g * 128 : g * 128 + 128] = v
                 t_ref[l * 32 : l * 32 + 32, cols] = v
             ca, sa = ca * cr - sa * sr, sa * cr + ca * sr
         return ca, sa
 
-    def add(n, buf_ref):
-        flat = f_ref[:, :, at(n)].reshape(ROWS, CHUNK)
-        flat_ref[:, at(n)] = flat
-        acc_ref[...] += nt(buf_ref[...], flat)
-        columns(flat_ref, flat_hbm, flat_sem, n).start()
-
-    ca, sa = make(0, phase_ref[:32, :], phase_ref[32:64, :], ta_ref)
+    def add(n, buf_ref, first):
+        acc_ref[first : first + 256, :] += nt(
+            buf_ref[first : first + 256, :], f_ref[:, :, at(n)].reshape(ROWS, CHUNK)
+        )
+
+    def weave(n, ca, sa, own_ref, next_ref):
+        add(n, own_ref, 0)
+        ca, sa = make(n + 1, ca, sa, next_ref, (0, 1))
+        add(n, own_ref, 256)
+        ca, sa = make(n + 1, ca, sa, next_ref, (2, 3))
+        columns(t_ref, t_hbm, t_sem, n + 1).start()
+        return ca, sa
+
+    ca, sa = make(0, phase_ref[:32, :], phase_ref[32:64, :], ta_ref, range(4))
     columns(t_ref, t_hbm, t_sem, 0).start()
 
     def step(m, carry):
         n = 2 * m
         planes(f_hbm, f_ref, f_sem, n).wait()
         planes(f_hbm, f_ref, f_sem, n + 1).wait()
-        add(n, ta_ref)
-        carry = make(n + 1, *carry, tb_ref)
-        columns(t_ref, t_hbm, t_sem, n + 1).start()
-        add(n + 1, tb_ref)
-        carry = make(n + 2, *carry, ta_ref)
-        columns(t_ref, t_hbm, t_sem, n + 2).start()
-        return carry
+        carry = weave(n, *carry, ta_ref, tb_ref)
+        return weave(n + 1, *carry, tb_ref, ta_ref)
 
     ca, sa = lax.fori_loop(0, STEPS // 2 - 1, step, (ca, sa))
     planes(f_hbm, f_ref, f_sem, STEPS - 2).wait()
     planes(f_hbm, f_ref, f_sem, STEPS - 1).wait()
-    add(STEPS - 2, ta_ref)
-    make(STEPS - 1, ca, sa, tb_ref)
-    columns(t_ref, t_hbm, t_sem, STEPS - 1).start()
-    add(STEPS - 1, tb_ref)
-    out_ref[...] = pack_spectra(acc_ref[...], lane_order(), row_order(subl(SQUARE), lanes(SQUARE)), pack_ref)
+    weave(STEPS - 2, ca, sa, ta_ref, tb_ref)
+    add(STEPS - 1, tb_ref, 0)
+    add(STEPS - 1, tb_ref, 256)
+    pack_spectra(acc_ref[...], perm, z_ref, out_ref)
     wait_all(columns, t_ref, t_hbm, t_sem)
-    wait_all(columns, flat_ref, flat_hbm, flat_sem)
 
 
 def mix_kernel(r_ref, w_hbm, fx_ref, iv_ref, out_ref, m_ref, w_ref, mask_ref, v_ref, w_sem):
@@ -325,40 +338,33 @@
 def delta_kernel(
     r_ref, f_hbm, ct_hbm, t_hbm, w_ref, bias_ref,
     out_ref, d_hbm,
-    f_ref, ct_ref, t_ref, d_ref, b_ref, lw_ref, shift_ref, pa_ref, pb_ref, da_ref, db_ref,
-    s_ref, g_ref, bt_ref, z_ref, f_sem, ct_sem, t_sem, d_sem,
+    ct_ref, tf_ref, d_ref, bl_ref, shift_ref, pa_ref, pb_ref, da_ref, db_ref,
+    sg_ref, bt_ref, z_ref, f_sem, ct_sem, t_sem, d_sem,
 ):
+    table, flat = tf_ref.at[:Q], tf_ref.at[Q : Q + ROWS]
     for n in range(STEPS):
-        columns(t_hbm, t_ref.at[:Q], t_sem, n).start()
-        columns(f_hbm, f_ref, f_sem, n).start()
+        columns(t_hbm, table, t_sem, n).start()
+        columns(f_hbm, flat, f_sem, n).start()
         columns(ct_hbm, ct_ref, ct_sem, n).start()
-    t_ref[Q:, :] = jnp.ones((16, CELLS), BF16)
-    b_ref[...] = unpack_back(
-        r_ref[...], lane_order(), row_order(lanes(SQUARE), subl(SQUARE)), bt_ref, True
-    )
-    lw_ref[...] = spread_weight(w_ref[...])
+    tf_ref[Q + ROWS :, :] = jnp.ones((16, CELLS), BF16)
+    bl_ref[:, :Q] = unpack_back(r_ref[...], lane_order(), z_ref, bt_ref, True)
+    bl_ref[:, Q:] = spread_weight(w_ref[...])
     e = (subl((ROWS, C)) // XL == lanes((ROWS, C))).astype(F32)
     shift_ref[...] = EXACT(e, jnp.broadcast_to(bias_ref[...], (128, C)), NT)
-    s_ref[...] = jnp.zeros_like(s_ref)
-    g_ref[...] = jnp.zeros_like(g_ref)
+    sg_ref[...] = jnp.zeros_like(sg_ref)
     db_ref[...] = jnp.zeros_like(db_ref)
 
     def arrive(n):
-        columns(t_hbm, t_ref.at[:Q], t_sem, n).wait()
-        columns(f_hbm, f_ref, f_sem, n).wait()
+        columns(t_hbm, table, t_sem, n).wait()
+        columns(f_hbm, flat, f_sem, n).wait()
 
     def before(n, p_ref, halves=(0, 1)):
         for h in halves:
             cols = pl.ds(pl.multiple_of(n * CHUNK + h * 256, 256), 256)
-            p_ref[:, h * 256 : h * 256 + 256] = mm(b_ref[...], t_ref[:Q, cols]) + mm(
-                lw_ref[...], f_ref[:, cols]
-            )
-
-    def add_spectra(n, own_ref, first, last):
-        s_ref[first:last, :] += nt(t_ref[first:last, at(n)], own_ref[...])
-
-    def add_point(n, own_ref):
-        g_ref[...] += nt(own_ref[...], f_ref[:, at(n)])
+            p_ref[:, h * 256 : h * 256 + 256] = mm(bl_ref[...], tf_ref[: Q + ROWS, cols])
+
+    def add(n, own_ref, first, last):
+        sg_ref[first:last, :] += nt(tf_ref[first:last, at(n)], own_ref[...])
 
     def bend(n, p_ref, own_ref, blocks):
         for r in blocks:
@@ -370,11 +376,11 @@
 
     def weave(n, p_ref, next_ref, own_ref, past_ref):
         past, later = jnp.maximum(n - 1, 0), jnp.minimum(n + 1, STEPS - 1)
-        add_spectra(past, past_ref, 0, 256)
+        add(past, past_ref, 0, 256)
         bend(n, p_ref, own_ref, range(0, 3))
-        add_spectra(past, past_ref, 256, Q + 16)
+        add(past, past_ref, 256, 512)
         bend(n, p_ref, own_ref, range(3, 6))
-        add_point(past, past_ref)
+        add(past, past_ref, 512, 784)
         bend(n, p_ref, own_ref, range(6, 9))
         before(later, next_ref, (0,))
         bend(n, p_ref, own_ref, range(9, 12))
@@ -400,19 +406,18 @@
         return carry
 
     lax.fori_loop(0, STEPS // 2, step, 0)
-    add_spectra(STEPS - 1, db_ref, 0, Q + 16)
-    add_point(STEPS - 1, db_ref)
+    add(STEPS - 1, db_ref, 0, 784)
     doubled = jnp.where(subl((Q, ROWS)) < 32, 1.0, 2.0)
-    out_ref[:, :1024] = pack_spectra(
-        s_ref[:Q, :] * doubled, lane_order(), row_order(subl(SQUARE), lanes(SQUARE)), z_ref
-    )
+    pack_spectra(sg_ref[:Q, :] * doubled, lane_order(), z_ref, out_ref)
     same = (subl((ROWS, ROWS)) & 3) == (lanes((ROWS, ROWS)) & 3)
-    g = jnp.where(same, g_ref[...], 0.0)
-    e = (subl((C, ROWS)) == lanes((C, ROWS)) // XL).astype(F32)
-    e2 = ((subl((ROWS, 128)) // XL) == (lanes((ROWS, 128)) & 63)).astype(F32)
-    wg = EXACT(EXACT(e, g, NN), e2, NN)
-    bg = EXACT(e, jnp.broadcast_to(s_ref[Q : Q + 1, :], (128, ROWS)), NT)
-    both = jnp.concatenate([wg, bg], axis=0)
+    g = jnp.where(same, sg_ref[Q : Q + ROWS, :], 0.0)
+    e = onehot(subl((C, ROWS)) == lanes((C, ROWS)) // XL)
+    e2 = onehot((subl((ROWS, 128)) // XL) == (lanes((ROWS, 128)) & 63))
+    wg = [nt(e, half) for half in halves_of(g)]
+    wg = [mm(half, e2) for half in halves_of(wg[0] + wg[1])]
+    sums = jnp.broadcast_to(sg_ref[Q + ROWS : Q + ROWS + 1, :], (128, ROWS))
+    bg = [nt(e, half) for half in halves_of(sums)]
+    both = jnp.concatenate([wg[0] + wg[1], bg[0] + bg[1]], axis=0)
     out_ref[:, 1024:] = mm(ext_order(subl(SQUARE), lanes(SQUARE)), split(both)).astype(BF16)
     wait_all(columns, d_ref, d_hbm, d_sem)
 
@@ -499,15 +504,14 @@
 def input_grad_kernel(
     r_ref, d_hbm, t_hbm, w_ref,
     out_hbm, pg_hbm, bg_hbm,
-    d_ref, t_ref, o_ref, b_ref, lw_ref, bt_ref, pg_ref, bg_ref, d_sem, t_sem, o_sem, g_sem,
+    td_ref, o_ref, bl_ref, bt_ref, z_ref, pg_ref, bg_ref, d_sem, t_sem, o_sem, g_sem,
 ):
+    table, delta = td_ref.at[:Q], td_ref.at[Q:]
     for n in range(STEPS):
-        columns(t_hbm, t_ref, t_sem, n).start()
-        columns(d_hbm, d_ref, d_sem, n).start()
-    b_ref[...] = unpack_back(
-        r_ref[:, :1024], lane_order(), row_order(lanes(SQUARE), subl(SQUARE)), bt_ref, False
-    )
-    lw_ref[...] = spread_weight(w_ref[...]).astype(F32).T.astype(BF16)
+        columns(t_hbm, table, t_sem, n).start()
+        columns(d_hbm, delta, d_sem, n).start()
+    bl_ref[:, :Q] = unpack_back(r_ref[:, :1024], lane_order(), z_ref, bt_ref, False)
+    bl_ref[:, Q:] = spread_weight(w_ref[...]).astype(F32).T.astype(BF16)
     v = mm(ext_order(lanes(SQUARE), subl(SQUARE)), r_ref[:, 1024:])
     v = (v + half_turn(v)) * (1.0 / 2048.0)
     pg_ref[...] = v[:C, :C]
@@ -519,16 +523,15 @@
     ]
     for copy in small:
         copy.start()
-
-    def step(n, carry):
-        columns(t_hbm, t_ref, t_sem, n).wait()
-        columns(d_hbm, d_ref, d_sem, n).wait()
-        out = mm(b_ref[...], t_ref[:, at(n)]) + mm(lw_ref[...], d_ref[:, at(n)])
-        o_ref[:, :, at(n)] = out.astype(BF16).reshape(C, XL, CHUNK)
-        planes(o_ref, out_hbm, o_sem, n).start()
-        return carry
-
-    lax.fori_loop(0, STEPS, step, 0)
+    for p in range(STEPS // 2):
+        for n in (2 * p, 2 * p + 1):
+            columns(t_hbm, table, t_sem, n).wait()
+            columns(d_hbm, delta, d_sem, n).wait()
+        for n in (2 * p, 2 * p + 1):
+            out = mm(bl_ref[...], td_ref[:, at(n)])
+            o_ref[:, :, at(n)] = out.astype(BF16).reshape(C, XL, CHUNK)
+        for n in (2 * p, 2 * p + 1):
+            planes(o_ref, out_hbm, o_sem, n).start()
     wait_all(planes, o_ref, out_hbm, o_sem)
     for copy in small:
         copy.wait()
@@ -565,21 +568,22 @@
 def body(field, cotangent, spectral_weight, point_weight, bias):
     k = constants()
     field3 = field.reshape(C, XL, CELLS)
+    flat = field.reshape(ROWS, CELLS)
     cot2 = cotangent.reshape(ROWS, CELLS)
     planes_shape = ((C, XL, CELLS), BF16)
     cells_shape = ((ROWS, CELLS), BF16)
     weight_shape = (spectral_weight.shape, BF16)
 
-    spectra, table, flat = call(
+    spectra, table = call(
         spectra_kernel,
         "spectra",
-        [((128, 1024), BF16), ((Q, CELLS), BF16), cells_shape],
-        [planes_shape, ((Q, CELLS), BF16), cells_shape, ((Q, CHUNK), BF16), ((Q, CHUNK), BF16),
-         ((Q, ROWS), F32), ((128, 1024), BF16), ((160, 128), F32)],
+        [((128, 1024), BF16), ((Q, CELLS), BF16)],
+        [planes_shape, ((Q, CELLS), BF16), ((Q, CHUNK), BF16), ((Q, CHUNK), BF16), ((Q, ROWS), F32), ((L // 2, 128, 128), F32),
+         ((160, 128), F32)],
         [field3, jnp.asarray(phase_tables())],
-        big=(0, 1), big_outs=(1, 2), sems=4,
-    )
-    arrived = exchange(spectra, "slab")
+        big=(0, 1), big_outs=(1,), sems=3,
+    )
+    arrived, flat = lax.optimization_barrier((exchange(spectra, "slab"), flat))
     back, modes = call(
         mix_kernel,
         "mix",
@@ -594,10 +598,10 @@
         "delta",
         [((128, 1152), BF16), cells_shape],
         [
-            cells_shape, cells_shape, ((Q + 16, CELLS), BF16), cells_shape,
-            ((ROWS, Q), BF16), ((ROWS, ROWS), BF16), ((ROWS, 128), F32),
+            cells_shape, ((Q + ROWS + 16, CELLS), BF16), cells_shape,
+            ((ROWS, Q + ROWS), BF16), ((ROWS, 128), F32),
             ((ROWS, CHUNK), F32), ((ROWS, CHUNK), F32), ((ROWS, CHUNK), BF16), ((ROWS, CHUNK), BF16),
-            ((Q + 16, ROWS), F32), ((ROWS, ROWS), F32), ((Q, ROWS), BF16), ((128, 1024), BF16),
+            ((Q + ROWS + 16, ROWS), F32), ((Q, ROWS), BF16), ((L // 2, 128, 128), F32),
         ],
         [arrived, flat, cot2, table, point_weight, bias.reshape(1, C)],
         big=(1, 2, 3), big_outs=(1,), sems=4,
@@ -628,8 +632,8 @@
         input_grad_kernel,
         "input_grad",
         [planes_shape, ((C, C), F32), ((1, C), F32)],
-        [cells_shape, ((Q, CELLS), BF16), planes_shape,
-         ((ROWS, Q), BF16), ((ROWS, ROWS), BF16), ((Q, ROWS), BF16), ((C, C), F32), ((1, C), F32)],
+        [((Q + ROWS, CELLS), BF16), planes_shape, ((ROWS, Q + ROWS), BF16), ((Q, ROWS), BF16),
+         ((L // 2, 128, 128), F32), ((C, C), F32), ((1, C), F32)],
         [arrived, delta, table, point_weight],
         big=(1, 2), big_outs=(0, 1, 2), sems=4,
     )

time: 99.4 us -> 99.3 us (level)
  blocking collectives: 25.2 us -> 10.9 us
  starting transfers between devices: 19.5 us -> 26.8 us
  waiting for transfers between devices: 17.9 us -> 23 us
  local copies, waits for them, and re-layouts: 2.95 us -> 4.98 us
    all_to_all x2 -> x1, blocking collectives: 25.2 us -> 10.9 us  [exchange(): lax.all_to_all(v.reshape(S, 8, width), axis, split_axis=0, concat_axis=0,...]
    all_to_all x3 -> x4, starting transfers between devices: 19.5 us -> 26.8 us  [exchange(): lax.all_to_all(v.reshape(S, 8, width), axis, split_axis=0, concat_axis=0,...]
    all_to_all x3 -> x4, waiting for transfers between devices: 17.9 us -> 23 us  [exchange(): lax.all_to_all(v.reshape(S, 8, width), axis, split_axis=0, concat_axis=0,...]
    reshape x0 -> x1, local copies, waits for them, and re-layouts: none -> 2.02 us  [body(): flat = field.reshape(ROWS, CELLS)]
  transfers between devices with their start and end apart: 3 -> 4, of which waited for: 3 -> 4; matrix products, arithmetic and copies ran while one was open for 3% -> 5% of each run, Pallas kernels for 4% -> 4%
where the time goes in v2:
time: 99.3 us; the launch traced here: 98.8 us
  Pallas kernels  32.4 us (33%)
  starting transfers between devices  26.8 us (27%)
  waiting for transfers between devices  23 us (23%)
  blocking collectives  10.9 us (11%)
  local copies, waits for them, and re-layouts  4.98 us (5%)
    pallas_call x8, Pallas kernels, call(): pl.pallas_call(kernel, in_specs=[place(n, big) for n in range(len(args))]...  32.4 us
    all_to_all x4, starting transfers between devices, exchange(): lax.all_to_all(v.reshape(S, 8, width), axis, split_axis=0, concat_axis=0,...  26.8 us
    all_to_all x4, waiting for transfers between devices, exchange(): lax.all_to_all(v.reshape(S, 8, width), axis, split_axis=0, concat_axis=0,...  23 us
    all_to_all x1, blocking collectives, exchange(): lax.all_to_all(v.reshape(S, 8, width), axis, split_axis=0, concat_axis=0,...  10.9 us
    reshape x1, local copies, waits for them, and re-layouts, body(): cot2 = cotangent.reshape(ROWS, CELLS)  2.11 us
    reshape x1, local copies, waits for them, and re-layouts, body(): flat = field.reshape(ROWS, CELLS)  2.02 us
  transfers between devices with their start and end apart: 4, of which 4 were waited for; matrix products, arithmetic and copies ran while one was open for 5% of the time, Pallas kernels for 4%

profile of v2, /device:TPU:1, one launch (start us, length us, event | category | flops | bytes accessed | tf_op | source)
XLA Modules:
  0.0 98.8 jit_solution(5931694145289021935)
XLA Ops:
  0.6 6.3 %spectra.1 = (bf16[128,1024]{1,0:T(8,128)(2,1)}, bf16[512,4096]{1,0:T(8,128)(2,1)}) custom-call(bf16[64,4,4096]{2,1,0:T(4,128)(2,1)} %bitcast.24, f32[160,128]{1,0:T(8,128)} %constant.20.clone.phase_hbm), custom_call_target="tpu_custom_call" | custom-call | tf_op jit(solution)/shard_map/spectra/pallas_call | solution.py:542
  7.0 7.4 %all-to-all-start = ((bf16[16,8,1024]{2,1,0:T(8,128)(2,1)}), bf16[16,8,1024]{2,1,0:T(8,128)(2,1)S(1)}, u32[]{:S(2)}, u32[]{:S(2)}) async-start(bf16[16,8,1024]{2,1,0:T(8,128)(2,1)} %bitcast.1), calls=%async_computation | async-start | bytes 524288 | tf_op jit(solution)/shard_map/all_to_all | solution.py:564
  14.3 0.0 copy-start.1
  14.3 0.0 copy-start.5
  14.4 2.0 %reshape.59.f_hbm = bf16[256,4096]{1,0:T(8,128)(2,1)} reshape(bf16[1,64,4,4096]{3,2,1,0:T(4,128)(2,1)S(1)} %copy-done.8) | data formatting | bytes 4194304 | tf_op jit(solution)/shard_map/reshape | solution.py:571
  16.4 5.1 %all-to-all-done = bf16[16,8,1024]{2,1,0:T(8,128)(2,1)S(1)} async-done(((bf16[16,8,1024]{2,1,0:T(8,128)(2,1)}), bf16[16,8,1024]{2,1,0:T(8,128)(2,1)S(1)}, u32[]{:S(2)}, u32[]{:S(2)}) %all-to-all-start) | async-done | bytes 262176 | tf_op jit(solution)/shard_map/all_to_all | solution.py:564
  21.5 4.3 %mix.1 = (bf16[128,1024]{1,0:T(8,128)(2,1)}, bf16[64,1024]{1,0:T(8,128)(2,1)S(1)}) custom-call(bf16[128,1024]{1,0:T(8,128)(2,1)S(1)} %bitcast.21, bf16[16,16,64,128]{3,2,1,0:T(8,128)(2,1)} %w_hbm.3, bf16[64,128]{1,0:T(8,128)(2,1)S(1)} %copy-done.1, bf16[128,64]{1,0:T(8,128)(2,1)S(1)} %copy-done.5), custom_call_target="tpu_custom_call" | custom-call | tf_op jit(solution)/shard_map/mix/pallas_call | solution.py:542
  25.8 4.3 %all-to-all-start.1 = ((bf16[16,8,1024]{2,1,0:T(8,128)(2,1)}), bf16[16,8,1024]{2,1,0:T(8,128)(2,1)S(1)}, u32[]{:S(2)}, u32[]{:S(2)}) async-start(bf16[16,8,1024]{2,1,0:T(8,128)(2,1)} %bitcast.3), calls=%async_computation.1 | async-start | bytes 524288 | tf_op jit(solution)/shard_map/all_to_all | solution.py:564
  30.1 2.1 %reshape.62.ct_hbm = bf16[256,4096]{1,0:T(8,128)(2,1)} reshape(bf16[1,64,4,4096]{3,2,1,0:T(4,128)(2,1)S(1)} %copy-done.9) | data formatting | bytes 4194304 | tf_op jit(solution)/shard_map/reshape | solution.py:572
  32.2 5.1 %all-to-all-done.1 = bf16[16,8,1024]{2,1,0:T(8,128)(2,1)S(1)} async-done(((bf16[16,8,1024]{2,1,0:T(8,128)(2,1)}), bf16[16,8,1024]{2,1,0:T(8,128)(2,1)S(1)}, u32[]{:S(2)}, u32[]{:S(2)}) %all-to-all-start.1) | async-done | bytes 262176 | tf_op jit(solution)/shard_map/all_to_all | solution.py:564
  37.3 0.0 copy-start.4
  37.3 10.5 %delta.1 = (bf16[128,1152]{1,0:T(8,128)(2,1)S(1)}, bf16[256,4096]{1,0:T(8,128)(2,1)}) custom-call(bf16[128,1024]{1,0:T(8,128)(2,1)S(1)} %bitcast.20, bf16[256,4096]{1,0:T(8,128)(2,1)} %reshape.59.f_hbm, bf16[256,4096]{1,0:T(8,128)(2,1)} %reshape.62.ct_hbm, bf16[512,4096]{1,0:T(8,128)(2,1)} %get-tuple-element.21.t_hbm, bf16[64,64]{1,0:T(8,128)(2,1)S(1)} %copy-done, ...), custom_call_target="tpu_custom_call" | custom-call | tf_op jit(solution)/shard_map/delta/pallas_call | solution.py:542
  47.9 10.9 %all_to_all.25 = bf16[16,8,1152]{2,1,0:T(8,128)(2,1)S(1)} all-to-all(bf16[16,8,1152]{2,1,0:T(8,128)(2,1)S(1)} %bitcast.22), channel_id=1, replica_groups=mesh['dp'=16,'slab'=16] {'slab'}, dimensions={0} | all-to-all | bytes 589824 | tf_op jit(solution)/shard_map/all_to_all | solution.py:564
  58.8 1.1 %grad_modes.1 = (bf16[64,1024]{1,0:T(8,128)(2,1)S(1)}, bf16[128,640]{1,0:T(8,128)(2,1)}) custom-call(bf16[128,1152]{1,0:T(8,128)(2,1)S(1)} %bitcast.19, bf16[64,1024]{1,0:T(8,128)(2,1)S(1)} %get-tuple-element.23.m_ref, bf16[64,128]{1,0:T(8,128)(2,1)S(1)} %copy-done.1, bf16[64,128]{1,0:T(8,128)(2,1)S(1)} %copy-done.6, bf16[2,128,128]{2,1,0:T(8,128)(2,1)S(1)} %copy-done.2), custom_call_target="tpu_custom_call" | custom-call | tf_op jit(solution)/shard_map/grad_modes/pallas_call | solution.py:542
  59.9 9.8 %all-to-all-start.3 = ((bf16[16,8,640]{2,1,0:T(8,128)(2,1)}), bf16[16,8,640]{2,1,0:T(8,128)(2,1)S(1)}, u32[]{:S(2)}, u32[]{:S(2)}) async-start(bf16[16,8,640]{2,1,0:T(8,128)(2,1)} %bitcast.8), calls=%async_computation.3 | async-start | bytes 327680 | tf_op jit(solution)/shard_map/all_to_all | solution.py:564
  69.8 0.0 copy-start.3
  69.8 3.4 %adjoint.1.v_ref = bf16[128,1024]{1,0:T(8,128)(2,1)S(1)} custom-call(bf16[64,1024]{1,0:T(8,128)(2,1)S(1)} %get-tuple-element.24.left_ref, bf16[16,16,64,128]{3,2,1,0:T(8,128)(2,1)} %w_hbm.3, bf16[128,64]{1,0:T(8,128)(2,1)S(1)} %copy-done.4), custom_call_target="tpu_custom_call" | custom-call | tf_op jit(solution)/shard_map/adjoint/pallas_call | solution.py:542
  73.2 6.8 %all-to-all-done.3 = bf16[16,8,640]{2,1,0:T(8,128)(2,1)S(1)} async-done(((bf16[16,8,640]{2,1,0:T(8,128)(2,1)}), bf16[16,8,640]{2,1,0:T(8,128)(2,1)S(1)}, u32[]{:S(2)}, u32[]{:S(2)}) %all-to-all-start.3) | async-done | bytes 163872 | tf_op jit(solution)/shard_map/all_to_all | solution.py:564
  80.0 0.9 join.1
  80.9 5.3 %all-to-all-start.4 = ((bf16[16,8,1152]{2,1,0:T(8,128)(2,1)}), bf16[16,8,1152]{2,1,0:T(8,128)(2,1)S(1)}, u32[]{:S(2)}, u32[]{:S(2)}) async-start(bf16[16,8,1152]{2,1,0:T(8,128)(2,1)} %bitcast.10), calls=%async_computation.4 | async-start | bytes 589824 | tf_op jit(solution)/shard_map/all_to_all | solution.py:564
  86.2 0.8 weight_grad.1
  87.0 0.8 copy.16
  87.8 5.9 %all-to-all-done.4 = bf16[16,8,1152]{2,1,0:T(8,128)(2,1)S(1)} async-done(((bf16[16,8,1152]{2,1,0:T(8,128)(2,1)}), bf16[16,8,1152]{2,1,0:T(8,128)(2,1)S(1)}, u32[]{:S(2)}, u32[]{:S(2)}) %all-to-all-start.4) | async-done | bytes 294944 | tf_op jit(solution)/shard_map/all_to_all | solution.py:564
  93.7 5.1 %input_grad.1 = (bf16[64,4,4096]{2,1,0:T(4,128)(2,1)}, f32[64,64]{1,0:T(8,128)}, f32[1,64]{1,0:T(1,128)}) custom-call(bf16[128,1152]{1,0:T(8,128)(2,1)S(1)} %bitcast.18, bf16[256,4096]{1,0:T(8,128)(2,1)} %get-tuple-element.26.d_hbm, bf16[512,4096]{1,0:T(8,128)(2,1)} %get-tuple-element.21.t_hbm, bf16[64,64]{1,0:T(8,128)(2,1)S(1)} %copy-done), custom_call_target="tpu_custom_call" | custom-call | tf_op jit(solution)/shard_map/input_grad/pallas_call | solution.py:542
  (16 shorter events, 0.0 us)
Async XLA Ops:
  0.6 13.7 %copy-start.8 = (bf16[1,64,4,4096]{3,2,1,0:T(4,128)(2,1)S(1)}, bf16[1,64,4,4096]{3,2,1,0:T(4,128)(2,1)}, u32[]{:S(2)}) copy-start(bf16[1,64,4,4096]{3,2,1,0:T(4,128)(2,1)} %param.12) | copy-start | bytes 6291460
  7.0 14.6 %all-to-all-start = ((bf16[16,8,1024]{2,1,0:T(8,128)(2,1)}), bf16[16,8,1024]{2,1,0:T(8,128)(2,1)S(1)}, u32[]{:S(2)}, u32[]{:S(2)}) async-start(bf16[16,8,1024]{2,1,0:T(8,128)(2,1)} %bitcast.1), calls=%async_computation | async-start | bytes 524288 | tf_op jit(solution)/shard_map/all_to_all | solution.py:564
  14.3 7.2 %copy-start.1 = (bf16[64,128]{1,0:T(8,128)(2,1)S(1)}, bf16[64,128]{1,0:T(8,128)(2,1)}, u32[]{:S(2)}) copy-start(bf16[64,128]{1,0:T(8,128)(2,1)} %constant.14.clone.fx_ref) | copy-start | bytes 49156
  14.3 7.2 %copy-start.5 = (bf16[128,64]{1,0:T(8,128)(2,1)S(1)}, bf16[128,64]{1,0:T(8,128)(2,1)}, u32[]{:S(2)}) copy-start(bf16[128,64]{1,0:T(8,128)(2,1)} %constant.16.clone.iv_ref) | copy-start | bytes 49156
  21.5 8.5 %copy-start.9 = (bf16[1,64,4,4096]{3,2,1,0:T(4,128)(2,1)S(1)}, bf16[1,64,4,4096]{3,2,1,0:T(4,128)(2,1)}, u32[]{:S(2)}) copy-start(bf16[1,64,4,4096]{3,2,1,0:T(4,128)(2,1)} %param.13) | copy-start | bytes 6291460
  25.8 11.5 %all-to-all-start.1 = ((bf16[16,8,1024]{2,1,0:T(8,128)(2,1)}), bf16[16,8,1024]{2,1,0:T(8,128)(2,1)S(1)}, u32[]{:S(2)}, u32[]{:S(2)}) async-start(bf16[16,8,1024]{2,1,0:T(8,128)(2,1)} %bitcast.3), calls=%async_computation.1 | async-start | bytes 524288 | tf_op jit(solution)/shard_map/all_to_all | solution.py:564
  30.0 7.3 %copy-start = (bf16[64,64]{1,0:T(8,128)(2,1)S(1)}, bf16[64,64]{1,0:T(8,128)(2,1)}, u32[]{:S(2)}) copy-start(bf16[64,64]{1,0:T(8,128)(2,1)} %w_ref.3) | copy-start | bytes 24580
  30.1 7.3 %copy-start.7 = (f32[64]{0:T(128)S(1)}, f32[64]{0:T(128)}, u32[]{:S(2)}) copy-start(f32[64]{0:T(128)} %param.16) | copy-start | bytes 772
  37.3 21.4 %copy-start.2 = (bf16[2,128,128]{2,1,0:T(8,128)(2,1)S(1)}, bf16[2,128,128]{2,1,0:T(8,128)(2,1)}, u32[]{:S(2)}) copy-start(bf16[2,128,128]{2,1,0:T(8,128)(2,1)} %constant.18.clone.gather_ref) | copy-start | bytes 196612
  37.3 21.4 %copy-start.6 = (bf16[64,128]{1,0:T(8,128)(2,1)S(1)}, bf16[64,128]{1,0:T(8,128)(2,1)}, u32[]{:S(2)}) copy-start(bf16[64,128]{1,0:T(8,128)(2,1)} %constant.15.clone.fo_ref) | copy-start | bytes 49156
  37.3 32.4 %copy-start.4 = (bf16[128,64]{1,0:T(8,128)(2,1)S(1)}, bf16[128,64]{1,0:T(8,128)(2,1)}, u32[]{:S(2)}) copy-start(bf16[128,64]{1,0:T(8,128)(2,1)} %constant.17.clone.ia_ref) | copy-start | bytes 49156
  59.9 20.1 %all-to-all-start.3 = ((bf16[16,8,640]{2,1,0:T(8,128)(2,1)}), bf16[16,8,640]{2,1,0:T(8,128)(2,1)S(1)}, u32[]{:S(2)}, u32[]{:S(2)}) async-start(bf16[16,8,640]{2,1,0:T(8,128)(2,1)} %bitcast.8), calls=%async_computation.3 | async-start | bytes 327680 | tf_op jit(solution)/shard_map/all_to_all | solution.py:564
  69.8 16.4 %copy-start.3 = (bf16[6,32,128]{2,1,0:T(8,128)(2,1)S(1)}, bf16[6,32,128]{2,1,0:T(8,128)(2,1)}, u32[]{:S(2)}) copy-start(bf16[6,32,128]{2,1,0:T(8,128)(2,1)} %constant.19.clone.pick_ref) | copy-start | bytes 147460
  80.9 12.9 %all-to-all-start.4 = ((bf16[16,8,1152]{2,1,0:T(8,128)(2,1)}), bf16[16,8,1152]{2,1,0:T(8,128)(2,1)S(1)}, u32[]{:S(2)}, u32[]{:S(2)}) async-start(bf16[16,8,1152]{2,1,0:T(8,128)(2,1)} %bitcast.10), calls=%async_computation.4 | async-start | bytes 589824 | tf_op jit(solution)/shard_map/all_to_all | solution.py:564

commit v3 on v2

--- a/solution.py
+++ b/solution.py
@@ -190,6 +190,7 @@
 SQUARE = (128, 128)
 
 STEPS = 8
+AHEAD = 3
 CHUNK = CELLS // STEPS
 EXACT = functools.partial(
     lax.dot_general, precision=lax.Precision.HIGHEST, preferred_element_type=F32
@@ -284,7 +285,8 @@
 
 
 def mix_kernel(r_ref, w_hbm, fx_ref, iv_ref, out_ref, m_ref, w_ref, mask_ref, v_ref, w_sem):
-    start_all(modes_pair, w_hbm, w_ref, w_sem)
+    for n in range(AHEAD):
+        modes_pair(w_hbm, w_ref, w_sem, n).start()
     m = mm(fx_ref[...], r_ref[...])
     m_ref[...] = m.astype(BF16)
     shape = m.shape
@@ -300,6 +302,11 @@
         cols = pl.ds(pl.multiple_of(u * 128, 128), 128)
         pair = pl.ds(2 * u, 2)
         modes_pair(w_hbm, w_ref, w_sem, u).wait()
+
+        @pl.when(u < L // 2 - AHEAD)
+        def _():
+            modes_pair(w_hbm, w_ref, w_sem, u + AHEAD).start()
+
         for t in range(8):
             left = mask_ref[8 * t : 8 * t + 8, cols].astype(BF16)
             right = jnp.concatenate(
@@ -342,10 +349,14 @@
     sg_ref, bt_ref, z_ref, f_sem, ct_sem, t_sem, d_sem,
 ):
     table, flat = tf_ref.at[:Q], tf_ref.at[Q : Q + ROWS]
-    for n in range(STEPS):
+
+    def send(n):
         columns(t_hbm, table, t_sem, n).start()
         columns(f_hbm, flat, f_sem, n).start()
         columns(ct_hbm, ct_ref, ct_sem, n).start()
+
+    send(0)
+    send(1)
     tf_ref[Q + ROWS :, :] = jnp.ones((16, CELLS), BF16)
     bl_ref[:, :Q] = unpack_back(r_ref[...], lane_order(), z_ref, bt_ref, True)
     bl_ref[:, Q:] = spread_weight(w_ref[...])
@@ -388,6 +399,7 @@
         bend(n, p_ref, own_ref, range(12, 16))
         columns(d_ref, d_hbm, d_sem, n).start()
 
+    send(2)
     arrive(0)
     before(0, pa_ref)
 
@@ -400,6 +412,11 @@
         @pl.when(m < STEPS // 2 - 1)
         def _():
             arrive(n + 2)
+            send(n + 3)
+
+        @pl.when(m < STEPS // 2 - 2)
+        def _():
+            send(n + 4)
 
         weave(n, pa_ref, pb_ref, da_ref, db_ref)
         weave(n + 1, pb_ref, pa_ref, db_ref, da_ref)
@@ -454,7 +471,8 @@
 
 
 def adjoint_kernel(left_ref, w_hbm, ia_ref, out_ref, w_ref, v_ref, w_sem):
-    start_all(modes_pair, w_hbm, w_ref, w_sem)
+    for n in range(AHEAD):
+        modes_pair(w_hbm, w_ref, w_sem, n).start()
     row, lane = subl((8, 128)), lanes((8, 128))
     top = row < 4
     keep = (lane >> 6) == ((row >> 1) & 1)
@@ -463,6 +481,11 @@
         cols = pl.ds(pl.multiple_of(u * 128, 128), 128)
         pair = pl.ds(2 * u, 2)
         modes_pair(w_hbm, w_ref, w_sem, u).wait()
+
+        @pl.when(u < L // 2 - AHEAD)
+        def _():
+            modes_pair(w_hbm, w_ref, w_sem, u + AHEAD).start()
+
         for t in range(8):
             right = jnp.concatenate(
                 [w_ref[2 * t, pair].reshape(128, 128), w_ref[2 * t + 1, pair].reshape(128, 128)],
@@ -507,9 +530,13 @@
     td_ref, o_ref, bl_ref, bt_ref, z_ref, pg_ref, bg_ref, d_sem, t_sem, o_sem, g_sem,
 ):
     table, delta = td_ref.at[:Q], td_ref.at[Q:]
-    for n in range(STEPS):
-        columns(t_hbm, table, t_sem, n).start()
-        columns(d_hbm, delta, d_sem, n).start()
+
+    def send(p):
+        for n in (2 * p, 2 * p + 1):
+            columns(t_hbm, table, t_sem, n).start()
+            columns(d_hbm, delta, d_sem, n).start()
+
+    send(0)
     bl_ref[:, :Q] = unpack_back(r_ref[:, :1024], lane_order(), z_ref, bt_ref, False)
     bl_ref[:, Q:] = spread_weight(w_ref[...]).astype(F32).T.astype(BF16)
     v = mm(ext_order(lanes(SQUARE), subl(SQUARE)), r_ref[:, 1024:])
@@ -523,10 +550,13 @@
     ]
     for copy in small:
         copy.start()
+    send(1)
     for p in range(STEPS // 2):
         for n in (2 * p, 2 * p + 1):
             columns(t_hbm, table, t_sem, n).wait()
             columns(d_hbm, delta, d_sem, n).wait()
+        if p + 2 < STEPS // 2:
+            send(p + 2)
         for n in (2 * p, 2 * p + 1):
             out = mm(bl_ref[...], td_ref[:, at(n)])
             o_ref[:, :, at(n)] = out.astype(BF16).reshape(C, XL, CHUNK)

time: 99.3 us -> 100 us (level)
  Pallas kernels: 32.4 us -> 34 us
    pallas_call x8, Pallas kernels: 32.4 us -> 34 us  [call(): pl.pallas_call(kernel, in_specs=[place(n, big) for n in range(len(args))]...]
  transfers between devices with their start and end apart: 4 -> 4, of which waited for: 4 -> 4; matrix products, arithmetic and copies ran while one was open for 5% -> 5% of each run, Pallas kernels for 4% -> 5%
where the time goes in v3:
time: 100 us; the launch traced here: 99.8 us
  Pallas kernels  34 us (34%)
  starting transfers between devices  26.8 us (27%)
  waiting for transfers between devices  22.3 us (22%)
  blocking collectives  10.9 us (11%)
  local copies, waits for them, and re-layouts  4.98 us (5%)
    pallas_call x8, Pallas kernels, call(): pl.pallas_call(kernel, in_specs=[place(n, big) for n in range(len(args))]...  34 us
    all_to_all x4, starting transfers between devices, exchange(): lax.all_to_all(v.reshape(S, 8, width), axis, split_axis=0, concat_axis=0,...  26.8 us
    all_to_all x4, waiting for transfers between devices, exchange(): lax.all_to_all(v.reshape(S, 8, width), axis, split_axis=0, concat_axis=0,...  22.3 us
    all_to_all x1, blocking collectives, exchange(): lax.all_to_all(v.reshape(S, 8, width), axis, split_axis=0, concat_axis=0,...  10.9 us
    reshape x1, local copies, waits for them, and re-layouts, body(): cot2 = cotangent.reshape(ROWS, CELLS)  2.11 us
    reshape x1, local copies, waits for them, and re-layouts, body(): flat = field.reshape(ROWS, CELLS)  2.02 us
  transfers between devices with their start and end apart: 4, of which 4 were waited for; matrix products, arithmetic and copies ran while one was open for 5% of the time, Pallas kernels for 5%

profile of v3, /device:TPU:1, one launch (start us, length us, event | category | flops | bytes accessed | tf_op | source)
XLA Modules:
  0.0 99.8 jit_solution(11987790876889537954)
XLA Ops:
  0.6 6.3 %spectra.1 = (bf16[128,1024]{1,0:T(8,128)(2,1)}, bf16[512,4096]{1,0:T(8,128)(2,1)}) custom-call(bf16[64,4,4096]{2,1,0:T(4,128)(2,1)} %bitcast.24, f32[160,128]{1,0:T(8,128)} %constant.20.clone.phase_hbm), custom_call_target="tpu_custom_call" | custom-call | tf_op jit(solution)/shard_map/spectra/pallas_call | solution.py:572
  7.0 7.4 %all-to-all-start = ((bf16[16,8,1024]{2,1,0:T(8,128)(2,1)}), bf16[16,8,1024]{2,1,0:T(8,128)(2,1)S(1)}, u32[]{:S(2)}, u32[]{:S(2)}) async-start(bf16[16,8,1024]{2,1,0:T(8,128)(2,1)} %bitcast.1), calls=%async_computation | async-start | bytes 524288 | tf_op jit(solution)/shard_map/all_to_all | solution.py:594
  14.3 0.0 copy-start.1
  14.3 0.0 copy-start.5
  14.4 2.0 %reshape.59.f_hbm = bf16[256,4096]{1,0:T(8,128)(2,1)} reshape(bf16[1,64,4,4096]{3,2,1,0:T(4,128)(2,1)S(1)} %copy-done.8) | data formatting | bytes 4194304 | tf_op jit(solution)/shard_map/reshape | solution.py:601
  16.4 5.1 %all-to-all-done = bf16[16,8,1024]{2,1,0:T(8,128)(2,1)S(1)} async-done(((bf16[16,8,1024]{2,1,0:T(8,128)(2,1)}), bf16[16,8,1024]{2,1,0:T(8,128)(2,1)S(1)}, u32[]{:S(2)}, u32[]{:S(2)}) %all-to-all-start) | async-done | bytes 262176 | tf_op jit(solution)/shard_map/all_to_all | solution.py:594
  21.5 4.9 %mix.1 = (bf16[128,1024]{1,0:T(8,128)(2,1)}, bf16[64,1024]{1,0:T(8,128)(2,1)S(1)}) custom-call(bf16[128,1024]{1,0:T(8,128)(2,1)S(1)} %bitcast.21, bf16[16,16,64,128]{3,2,1,0:T(8,128)(2,1)} %w_hbm.3, bf16[64,128]{1,0:T(8,128)(2,1)S(1)} %copy-done.1, bf16[128,64]{1,0:T(8,128)(2,1)S(1)} %copy-done.5), custom_call_target="tpu_custom_call" | custom-call | tf_op jit(solution)/shard_map/mix/pallas_call | solution.py:572
  26.5 4.3 %all-to-all-start.1 = ((bf16[16,8,1024]{2,1,0:T(8,128)(2,1)}), bf16[16,8,1024]{2,1,0:T(8,128)(2,1)S(1)}, u32[]{:S(2)}, u32[]{:S(2)}) async-start(bf16[16,8,1024]{2,1,0:T(8,128)(2,1)} %bitcast.3), calls=%async_computation.1 | async-start | bytes 524288 | tf_op jit(solution)/shard_map/all_to_all | solution.py:594
  30.8 2.1 %reshape.62.ct_hbm = bf16[256,4096]{1,0:T(8,128)(2,1)} reshape(bf16[1,64,4,4096]{3,2,1,0:T(4,128)(2,1)S(1)} %copy-done.9) | data formatting | bytes 4194304 | tf_op jit(solution)/shard_map/reshape | solution.py:602
  32.9 5.1 %all-to-all-done.1 = bf16[16,8,1024]{2,1,0:T(8,128)(2,1)S(1)} async-done(((bf16[16,8,1024]{2,1,0:T(8,128)(2,1)}), bf16[16,8,1024]{2,1,0:T(8,128)(2,1)S(1)}, u32[]{:S(2)}, u32[]{:S(2)}) %all-to-all-start.1) | async-done | bytes 262176 | tf_op jit(solution)/shard_map/all_to_all | solution.py:594
  38.0 0.0 copy-start.4
  38.0 10.1 %delta.1 = (bf16[128,1152]{1,0:T(8,128)(2,1)S(1)}, bf16[256,4096]{1,0:T(8,128)(2,1)}) custom-call(bf16[128,1024]{1,0:T(8,128)(2,1)S(1)} %bitcast.20, bf16[256,4096]{1,0:T(8,128)(2,1)} %reshape.59.f_hbm, bf16[256,4096]{1,0:T(8,128)(2,1)} %reshape.62.ct_hbm, bf16[512,4096]{1,0:T(8,128)(2,1)} %get-tuple-element.21.t_hbm, bf16[64,64]{1,0:T(8,128)(2,1)S(1)} %copy-done, ...), custom_call_target="tpu_custom_call" | custom-call | tf_op jit(solution)/shard_map/delta/pallas_call | solution.py:572
  48.2 10.9 %all_to_all.25 = bf16[16,8,1152]{2,1,0:T(8,128)(2,1)S(1)} all-to-all(bf16[16,8,1152]{2,1,0:T(8,128)(2,1)S(1)} %bitcast.22), channel_id=1, replica_groups=mesh['dp'=16,'slab'=16] {'slab'}, dimensions={0} | all-to-all | bytes 589824 | tf_op jit(solution)/shard_map/all_to_all | solution.py:594
  59.1 1.1 %grad_modes.1 = (bf16[64,1024]{1,0:T(8,128)(2,1)S(1)}, bf16[128,640]{1,0:T(8,128)(2,1)}) custom-call(bf16[128,1152]{1,0:T(8,128)(2,1)S(1)} %bitcast.19, bf16[64,1024]{1,0:T(8,128)(2,1)S(1)} %get-tuple-element.23.m_ref, bf16[64,128]{1,0:T(8,128)(2,1)S(1)} %copy-done.1, bf16[64,128]{1,0:T(8,128)(2,1)S(1)} %copy-done.6, bf16[2,128,128]{2,1,0:T(8,128)(2,1)S(1)} %copy-done.2), custom_call_target="tpu_custom_call" | custom-call | tf_op jit(solution)/shard_map/grad_modes/pallas_call | solution.py:572
  60.2 9.8 %all-to-all-start.3 = ((bf16[16,8,640]{2,1,0:T(8,128)(2,1)}), bf16[16,8,640]{2,1,0:T(8,128)(2,1)S(1)}, u32[]{:S(2)}, u32[]{:S(2)}) async-start(bf16[16,8,640]{2,1,0:T(8,128)(2,1)} %bitcast.8), calls=%async_computation.3 | async-start | bytes 327680 | tf_op jit(solution)/shard_map/all_to_all | solution.py:594
  70.1 0.0 copy-start.3
  70.1 4.1 %adjoint.1.v_ref = bf16[128,1024]{1,0:T(8,128)(2,1)S(1)} custom-call(bf16[64,1024]{1,0:T(8,128)(2,1)S(1)} %get-tuple-element.24.left_ref, bf16[16,16,64,128]{3,2,1,0:T(8,128)(2,1)} %w_hbm.3, bf16[128,64]{1,0:T(8,128)(2,1)S(1)} %copy-done.4), custom_call_target="tpu_custom_call" | custom-call | tf_op jit(solution)/shard_map/adjoint/pallas_call | solution.py:572
  74.2 6.1 %all-to-all-done.3 = bf16[16,8,640]{2,1,0:T(8,128)(2,1)S(1)} async-done(((bf16[16,8,640]{2,1,0:T(8,128)(2,1)}), bf16[16,8,640]{2,1,0:T(8,128)(2,1)S(1)}, u32[]{:S(2)}, u32[]{:S(2)}) %all-to-all-start.3) | async-done | bytes 163872 | tf_op jit(solution)/shard_map/all_to_all | solution.py:594
  80.3 0.9 join.1
  81.2 5.3 %all-to-all-start.4 = ((bf16[16,8,1152]{2,1,0:T(8,128)(2,1)}), bf16[16,8,1152]{2,1,0:T(8,128)(2,1)S(1)}, u32[]{:S(2)}, u32[]{:S(2)}) async-start(bf16[16,8,1152]{2,1,0:T(8,128)(2,1)} %bitcast.10), calls=%async_computation.4 | async-start | bytes 589824 | tf_op jit(solution)/shard_map/all_to_all | solution.py:594
  86.5 0.8 weight_grad.1
  87.3 0.8 copy.16
  88.1 5.9 %all-to-all-done.4 = bf16[16,8,1152]{2,1,0:T(8,128)(2,1)S(1)} async-done(((bf16[16,8,1152]{2,1,0:T(8,128)(2,1)}), bf16[16,8,1152]{2,1,0:T(8,128)(2,1)S(1)}, u32[]{:S(2)}, u32[]{:S(2)}) %all-to-all-start.4) | async-done | bytes 294944 | tf_op jit(solution)/shard_map/all_to_all | solution.py:594
  94.0 5.7 %input_grad.1 = (bf16[64,4,4096]{2,1,0:T(4,128)(2,1)}, f32[64,64]{1,0:T(8,128)}, f32[1,64]{1,0:T(1,128)}) custom-call(bf16[128,1152]{1,0:T(8,128)(2,1)S(1)} %bitcast.18, bf16[256,4096]{1,0:T(8,128)(2,1)} %get-tuple-element.26.d_hbm, bf16[512,4096]{1,0:T(8,128)(2,1)} %get-tuple-element.21.t_hbm, bf16[64,64]{1,0:T(8,128)(2,1)S(1)} %copy-done), custom_call_target="tpu_custom_call" | custom-call | tf_op jit(solution)/shard_map/input_grad/pallas_call | solution.py:572
  (16 shorter events, 0.0 us)
Async XLA Ops:
  0.6 13.7 %copy-start.8 = (bf16[1,64,4,4096]{3,2,1,0:T(4,128)(2,1)S(1)}, bf16[1,64,4,4096]{3,2,1,0:T(4,128)(2,1)}, u32[]{:S(2)}) copy-start(bf16[1,64,4,4096]{3,2,1,0:T(4,128)(2,1)} %param.12) | copy-start | bytes 6291460
  7.0 14.6 %all-to-all-start = ((bf16[16,8,1024]{2,1,0:T(8,128)(2,1)}), bf16[16,8,1024]{2,1,0:T(8,128)(2,1)S(1)}, u32[]{:S(2)}, u32[]{:S(2)}) async-start(bf16[16,8,1024]{2,1,0:T(8,128)(2,1)} %bitcast.1), calls=%async_computation | async-start | bytes 524288 | tf_op jit(solution)/shard_map/all_to_all | solution.py:594
  14.3 7.2 %copy-start.1 = (bf16[64,128]{1,0:T(8,128)(2,1)S(1)}, bf16[64,128]{1,0:T(8,128)(2,1)}, u32[]{:S(2)}) copy-start(bf16[64,128]{1,0:T(8,128)(2,1)} %constant.14.clone.fx_ref) | copy-start | bytes 49156
  14.3 7.2 %copy-start.5 = (bf16[128,64]{1,0:T(8,128)(2,1)S(1)}, bf16[128,64]{1,0:T(8,128)(2,1)}, u32[]{:S(2)}) copy-start(bf16[128,64]{1,0:T(8,128)(2,1)} %constant.16.clone.iv_ref) | copy-start | bytes 49156
  21.5 9.2 %copy-start.9 = (bf16[1,64,4,4096]{3,2,1,0:T(4,128)(2,1)S(1)}, bf16[1,64,4,4096]{3,2,1,0:T(4,128)(2,1)}, u32[]{:S(2)}) copy-start(bf16[1,64,4,4096]{3,2,1,0:T(4,128)(2,1)} %param.13) | copy-start | bytes 6291460
  26.5 11.5 %all-to-all-start.1 = ((bf16[16,8,1024]{2,1,0:T(8,128)(2,1)}), bf16[16,8,1024]{2,1,0:T(8,128)(2,1)S(1)}, u32[]{:S(2)}, u32[]{:S(2)}) async-start(bf16[16,8,1024]{2,1,0:T(8,128)(2,1)} %bitcast.3), calls=%async_computation.1 | async-start | bytes 524288 | tf_op jit(solution)/shard_map/all_to_all | solution.py:594
  30.7 7.3 %copy-start = (bf16[64,64]{1,0:T(8,128)(2,1)S(1)}, bf16[64,64]{1,0:T(8,128)(2,1)}, u32[]{:S(2)}) copy-start(bf16[64,64]{1,0:T(8,128)(2,1)} %w_ref.3) | copy-start | bytes 24580
  30.8 7.3 %copy-start.7 = (f32[64]{0:T(128)S(1)}, f32[64]{0:T(128)}, u32[]{:S(2)}) copy-start(f32[64]{0:T(128)} %param.16) | copy-start | bytes 772
  38.0 21.1 %copy-start.2 = (bf16[2,128,128]{2,1,0:T(8,128)(2,1)S(1)}, bf16[2,128,128]{2,1,0:T(8,128)(2,1)}, u32[]{:S(2)}) copy-start(bf16[2,128,128]{2,1,0:T(8,128)(2,1)} %constant.18.clone.gather_ref) | copy-start | bytes 196612
  38.0 21.1 %copy-start.6 = (bf16[64,128]{1,0:T(8,128)(2,1)S(1)}, bf16[64,128]{1,0:T(8,128)(2,1)}, u32[]{:S(2)}) copy-start(bf16[64,128]{1,0:T(8,128)(2,1)} %constant.15.clone.fo_ref) | copy-start | bytes 49156
  38.0 32.0 %copy-start.4 = (bf16[128,64]{1,0:T(8,128)(2,1)S(1)}, bf16[128,64]{1,0:T(8,128)(2,1)}, u32[]{:S(2)}) copy-start(bf16[128,64]{1,0:T(8,128)(2,1)} %constant.17.clone.ia_ref) | copy-start | bytes 49156
  60.2 20.0 %all-to-all-start.3 = ((bf16[16,8,640]{2,1,0:T(8,128)(2,1)}), bf16[16,8,640]{2,1,0:T(8,128)(2,1)S(1)}, u32[]{:S(2)}, u32[]{:S(2)}) async-start(bf16[16,8,640]{2,1,0:T(8,128)(2,1)} %bitcast.8), calls=%async_computation.3 | async-start | bytes 327680 | tf_op jit(solution)/shard_map/all_to_all | solution.py:594
  70.1 16.4 %copy-start.3 = (bf16[6,32,128]{2,1,0:T(8,128)(2,1)S(1)}, bf16[6,32,128]{2,1,0:T(8,128)(2,1)}, u32[]{:S(2)}) copy-start(bf16[6,32,128]{2,1,0:T(8,128)(2,1)} %constant.19.clone.pick_ref) | copy-start | bytes 147460
  81.2 12.9 %all-to-all-start.4 = ((bf16[16,8,1152]{2,1,0:T(8,128)(2,1)}), bf16[16,8,1152]{2,1,0:T(8,128)(2,1)S(1)}, u32[]{:S(2)}, u32[]{:S(2)}) async-start(bf16[16,8,1152]{2,1,0:T(8,128)(2,1)} %bitcast.10), calls=%async_computation.4 | async-start | bytes 589824 | tf_op jit(solution)/shard_map/all_to_all | solution.py:594

commit v4 on v2

--- a/solution.py
+++ b/solution.py
@@ -226,61 +226,58 @@
         copy(src, dst, sems, n).wait()
 
 
+def make_table(phase_ref, ca, sa, refs, tiles):
+    cr, sr = phase_ref[64:96, :], phase_ref[96:128, :]
+    for g in tiles:
+        for l in range(L):
+            cb, sb = phase_ref[128 + l : 129 + l, :], phase_ref[144 + l : 145 + l, :]
+            v = (ca * cb - sa * sb).astype(BF16)
+            for ref, start in refs:
+                ref[l * 32 : l * 32 + 32, pl.ds(start + g * 128, 128)] = v
+        ca, sa = ca * cr - sa * sr, sa * cr + ca * sr
+    return ca, sa
+
+
 def spectra_kernel(
     f_hbm, phase_hbm,
-    out_ref, t_hbm,
-    f_ref, t_ref, ta_ref, tb_ref, acc_ref, z_ref, phase_ref, f_sem, t_sem, p_sem,
+    out_ref, tf_ref,
+    f_ref, ta_ref, tb_ref, acc_ref, z_ref, phase_ref, f_sem, p_sem,
 ):
     phases = pltpu.make_async_copy(phase_hbm, phase_ref, p_sem.at[0])
     phases.start()
     start_all(planes, f_hbm, f_ref, f_sem)
     acc_ref[...] = jnp.zeros_like(acc_ref)
+    tf_ref[Q + ROWS :, :] = jnp.ones((16, CELLS), BF16)
     perm = lane_order()
     phases.wait()
-    cr, sr = phase_ref[64:96, :], phase_ref[96:128, :]
-
-    def make(n, ca, sa, buf_ref, tiles):
-        for g in tiles:
-            cols = pl.ds(pl.multiple_of(n * CHUNK + g * 128, 128), 128)
-            for l in range(L):
-                cb, sb = phase_ref[128 + l : 129 + l, :], phase_ref[144 + l : 145 + l, :]
-                v = (ca * cb - sa * sb).astype(BF16)
-                buf_ref[l * 32 : l * 32 + 32, g * 128 : g * 128 + 128] = v
-                t_ref[l * 32 : l * 32 + 32, cols] = v
-            ca, sa = ca * cr - sa * sr, sa * cr + ca * sr
-        return ca, sa
-
-    def add(n, buf_ref, first):
-        acc_ref[first : first + 256, :] += nt(
-            buf_ref[first : first + 256, :], f_ref[:, :, at(n)].reshape(ROWS, CHUNK)
-        )
-
-    def weave(n, ca, sa, own_ref, next_ref):
-        add(n, own_ref, 0)
-        ca, sa = make(n + 1, ca, sa, next_ref, (0, 1))
-        add(n, own_ref, 256)
-        ca, sa = make(n + 1, ca, sa, next_ref, (2, 3))
-        columns(t_ref, t_hbm, t_sem, n + 1).start()
-        return ca, sa
-
-    ca, sa = make(0, phase_ref[:32, :], phase_ref[32:64, :], ta_ref, range(4))
-    columns(t_ref, t_hbm, t_sem, 0).start()
+
+    def make(n, ca, sa, buf_ref):
+        start = n * CHUNK if isinstance(n, int) else pl.multiple_of(n * CHUNK, CHUNK)
+        return make_table(phase_ref, ca, sa, ((buf_ref, 0), (tf_ref, start)), range(4))
+
+    def add(n, buf_ref):
+        flat = f_ref[:, :, at(n)].reshape(ROWS, CHUNK)
+        tf_ref[Q : Q + ROWS, at(n)] = flat
+        acc_ref[...] += nt(buf_ref[...], flat)
+
+    ca, sa = make(0, phase_ref[:32, :], phase_ref[32:64, :], ta_ref)
 
     def step(m, carry):
         n = 2 * m
         planes(f_hbm, f_ref, f_sem, n).wait()
         planes(f_hbm, f_ref, f_sem, n + 1).wait()
-        carry = weave(n, *carry, ta_ref, tb_ref)
-        return weave(n + 1, *carry, tb_ref, ta_ref)
+        add(n, ta_ref)
+        carry = make(n + 1, *carry, tb_ref)
+        add(n + 1, tb_ref)
+        return make(n + 2, *carry, ta_ref)
 
     ca, sa = lax.fori_loop(0, STEPS // 2 - 1, step, (ca, sa))
     planes(f_hbm, f_ref, f_sem, STEPS - 2).wait()
     planes(f_hbm, f_ref, f_sem, STEPS - 1).wait()
-    weave(STEPS - 2, ca, sa, ta_ref, tb_ref)
-    add(STEPS - 1, tb_ref, 0)
-    add(STEPS - 1, tb_ref, 256)
+    add(STEPS - 2, ta_ref)
+    make(STEPS - 1, ca, sa, tb_ref)
+    add(STEPS - 1, tb_ref)
     pack_spectra(acc_ref[...], perm, z_ref, out_ref)
-    wait_all(columns, t_ref, t_hbm, t_sem)
 
 
 def mix_kernel(r_ref, w_hbm, fx_ref, iv_ref, out_ref, m_ref, w_ref, mask_ref, v_ref, w_sem):
@@ -336,17 +333,12 @@
 
 
 def delta_kernel(
-    r_ref, f_hbm, ct_hbm, t_hbm, w_ref, bias_ref,
+    r_ref, tf_ref, ct_hbm, w_ref, bias_ref,
     out_ref, d_hbm,
-    ct_ref, tf_ref, d_ref, bl_ref, shift_ref, pa_ref, pb_ref, da_ref, db_ref,
-    sg_ref, bt_ref, z_ref, f_sem, ct_sem, t_sem, d_sem,
+    ct_ref, d_ref, bl_ref, shift_ref, pa_ref, pb_ref, da_ref, db_ref,
+    sg_ref, bt_ref, z_ref, ct_sem, d_sem,
 ):
-    table, flat = tf_ref.at[:Q], tf_ref.at[Q : Q + ROWS]
-    for n in range(STEPS):
-        columns(t_hbm, table, t_sem, n).start()
-        columns(f_hbm, flat, f_sem, n).start()
-        columns(ct_hbm, ct_ref, ct_sem, n).start()
-    tf_ref[Q + ROWS :, :] = jnp.ones((16, CELLS), BF16)
+    start_all(planes, ct_hbm, ct_ref, ct_sem)
     bl_ref[:, :Q] = unpack_back(r_ref[...], lane_order(), z_ref, bt_ref, True)
     bl_ref[:, Q:] = spread_weight(w_ref[...])
     e = (subl((ROWS, C)) // XL == lanes((ROWS, C))).astype(F32)
@@ -354,10 +346,6 @@
     sg_ref[...] = jnp.zeros_like(sg_ref)
     db_ref[...] = jnp.zeros_like(db_ref)
 
-    def arrive(n):
-        columns(t_hbm, table, t_sem, n).wait()
-        columns(f_hbm, flat, f_sem, n).wait()
-
     def before(n, p_ref, halves=(0, 1)):
         for h in halves:
             cols = pl.ds(pl.multiple_of(n * CHUNK + h * 256, 256), 256)
@@ -370,7 +358,8 @@
         for r in blocks:
             rows = slice(r * 16, r * 16 + 16)
             v = p_ref[rows, :] + jnp.concatenate([shift_ref[rows, :]] * (CHUNK // 128), axis=1)
-            d = (ct_ref[rows, at(n)].astype(F32) * slope(v)).astype(BF16)
+            ct = ct_ref[r * 4 : r * 4 + 4, :, at(n)].reshape(16, CHUNK)
+            d = (ct.astype(F32) * slope(v)).astype(BF16)
             own_ref[rows, :] = d
             d_ref[rows, at(n)] = d
 
@@ -388,19 +377,12 @@
         bend(n, p_ref, own_ref, range(12, 16))
         columns(d_ref, d_hbm, d_sem, n).start()
 
-    arrive(0)
     before(0, pa_ref)
 
     def step(m, carry):
         n = 2 * m
-        columns(ct_hbm, ct_ref, ct_sem, n).wait()
-        columns(ct_hbm, ct_ref, ct_sem, n + 1).wait()
-        arrive(n + 1)
-
-        @pl.when(m < STEPS // 2 - 1)
-        def _():
-            arrive(n + 2)
-
+        planes(ct_hbm, ct_ref, ct_sem, n).wait()
+        planes(ct_hbm, ct_ref, ct_sem, n + 1).wait()
         weave(n, pa_ref, pb_ref, da_ref, db_ref)
         weave(n + 1, pb_ref, pa_ref, db_ref, da_ref)
         return carry
@@ -502,14 +484,11 @@
 
 
 def input_grad_kernel(
-    r_ref, d_hbm, t_hbm, w_ref,
+    r_ref, d_hbm, w_ref, phase_ref,
     out_hbm, pg_hbm, bg_hbm,
-    td_ref, o_ref, bl_ref, bt_ref, z_ref, pg_ref, bg_ref, d_sem, t_sem, o_sem, g_sem,
+    d_ref, ta_ref, tb_ref, o_ref, bl_ref, bt_ref, z_ref, pg_ref, bg_ref, d_sem, o_sem, g_sem,
 ):
-    table, delta = td_ref.at[:Q], td_ref.at[Q:]
-    for n in range(STEPS):
-        columns(t_hbm, table, t_sem, n).start()
-        columns(d_hbm, delta, d_sem, n).start()
+    start_all(columns, d_hbm, d_ref, d_sem)
     bl_ref[:, :Q] = unpack_back(r_ref[:, :1024], lane_order(), z_ref, bt_ref, False)
     bl_ref[:, Q:] = spread_weight(w_ref[...]).astype(F32).T.astype(BF16)
     v = mm(ext_order(lanes(SQUARE), subl(SQUARE)), r_ref[:, 1024:])
@@ -523,21 +502,41 @@
     ]
     for copy in small:
         copy.start()
-    for p in range(STEPS // 2):
-        for n in (2 * p, 2 * p + 1):
-            columns(t_hbm, table, t_sem, n).wait()
-            columns(d_hbm, delta, d_sem, n).wait()
-        for n in (2 * p, 2 * p + 1):
-            out = mm(bl_ref[...], td_ref[:, at(n)])
-            o_ref[:, :, at(n)] = out.astype(BF16).reshape(C, XL, CHUNK)
-        for n in (2 * p, 2 * p + 1):
-            planes(o_ref, out_hbm, o_sem, n).start()
+
+    def finish(n, own_ref):
+        out = mm(bl_ref[:, :Q], own_ref[...]) + mm(bl_ref[:, Q:], d_ref[:, at(n)])
+        o_ref[:, :, at(n)] = out.astype(BF16).reshape(C, XL, CHUNK)
+
+    def make(carry, next_ref):
+        return make_table(phase_ref, *carry, ((next_ref, 0),), range(4))
+
+    def step(m, carry):
+        n = 2 * m
+        columns(d_hbm, d_ref, d_sem, n).wait()
+        columns(d_hbm, d_ref, d_sem, n + 1).wait()
+        finish(n, ta_ref)
+        carry = make(carry, tb_ref)
+        finish(n + 1, tb_ref)
+        carry = make(carry, ta_ref)
+        planes(o_ref, out_hbm, o_sem, n).start()
+        planes(o_ref, out_hbm, o_sem, n + 1).start()
+        return carry
+
+    carry = make((phase_ref[:32, :], phase_ref[32:64, :]), ta_ref)
+    carry = lax.fori_loop(0, STEPS // 2 - 1, step, carry)
+    columns(d_hbm, d_ref, d_sem, STEPS - 2).wait()
+    columns(d_hbm, d_ref, d_sem, STEPS - 1).wait()
+    finish(STEPS - 2, ta_ref)
+    planes(o_ref, out_hbm, o_sem, STEPS - 2).start()
+    make(carry, tb_ref)
+    finish(STEPS - 1, tb_ref)
+    planes(o_ref, out_hbm, o_sem, STEPS - 1).start()
     wait_all(planes, o_ref, out_hbm, o_sem)
     for copy in small:
         copy.wait()
 
 
-def call(kernel, name, outs, scratch, args, big=(), big_outs=(), sems=0):
+def call(kernel, name, outs, scratch, args, big=(), big_outs=(), sems=0, room=8):
     place = lambda n, far: pl.BlockSpec(memory_space=pltpu.HBM if n in far else pltpu.VMEM)
     return pl.pallas_call(
         kernel,
@@ -549,7 +548,7 @@
         ],
         scratch_shapes=[pltpu.VMEM(shape, dtype) for shape, dtype in scratch]
         + [pltpu.SemaphoreType.DMA((STEPS,))] * sems,
-        compiler_params=pltpu.CompilerParams(vmem_limit_bytes=40 << 20),
+        compiler_params=pltpu.CompilerParams(vmem_limit_bytes=room << 20),
         name=name,
     )(
         *[
@@ -568,22 +567,22 @@
 def body(field, cotangent, spectral_weight, point_weight, bias):
     k = constants()
     field3 = field.reshape(C, XL, CELLS)
-    flat = field.reshape(ROWS, CELLS)
-    cot2 = cotangent.reshape(ROWS, CELLS)
+    cot3 = cotangent.reshape(C, XL, CELLS)
     planes_shape = ((C, XL, CELLS), BF16)
     cells_shape = ((ROWS, CELLS), BF16)
     weight_shape = (spectral_weight.shape, BF16)
 
-    spectra, table = call(
+    phases = jnp.asarray(phase_tables())
+    spectra, rows = call(
         spectra_kernel,
         "spectra",
-        [((128, 1024), BF16), ((Q, CELLS), BF16)],
-        [planes_shape, ((Q, CELLS), BF16), ((Q, CHUNK), BF16), ((Q, CHUNK), BF16), ((Q, ROWS), F32), ((L // 2, 128, 128), F32),
-         ((160, 128), F32)],
-        [field3, jnp.asarray(phase_tables())],
-        big=(0, 1), big_outs=(1,), sems=3,
-    )
-    arrived, flat = lax.optimization_barrier((exchange(spectra, "slab"), flat))
+        [((128, 1024), BF16), ((Q + ROWS + 16, CELLS), BF16)],
+        [planes_shape, ((Q, CHUNK), BF16), ((Q, CHUNK), BF16), ((Q, ROWS), F32),
+         ((L // 2, 128, 128), F32), ((160, 128), F32)],
+        [field3, phases],
+        big=(0, 1), sems=2,
+    )
+    arrived = exchange(spectra, "slab")
     back, modes = call(
         mix_kernel,
         "mix",
@@ -598,13 +597,13 @@
         "delta",
         [((128, 1152), BF16), cells_shape],
         [
-            cells_shape, ((Q + ROWS + 16, CELLS), BF16), cells_shape,
+            planes_shape, cells_shape,
             ((ROWS, Q + ROWS), BF16), ((ROWS, 128), F32),
             ((ROWS, CHUNK), F32), ((ROWS, CHUNK), F32), ((ROWS, CHUNK), BF16), ((ROWS, CHUNK), BF16),
             ((Q + ROWS + 16, ROWS), F32), ((Q, ROWS), BF16), ((L // 2, 128, 128), F32),
         ],
-        [arrived, flat, cot2, table, point_weight, bias.reshape(1, C)],
-        big=(1, 2, 3), big_outs=(1,), sems=4,
+        [arrived, rows, cot3, point_weight, bias.reshape(1, C)],
+        big=(2,), big_outs=(1,), sems=2, room=16,
     )
     arrived = exchange(grad_spectra, "slab")
     left, shared = call(
@@ -632,10 +631,11 @@
         input_grad_kernel,
         "input_grad",
         [planes_shape, ((C, C), F32), ((1, C), F32)],
-        [((Q + ROWS, CELLS), BF16), planes_shape, ((ROWS, Q + ROWS), BF16), ((Q, ROWS), BF16),
-         ((L // 2, 128, 128), F32), ((C, C), F32), ((1, C), F32)],
-        [arrived, delta, table, point_weight],
-        big=(1, 2), big_outs=(0, 1, 2), sems=4,
+        [cells_shape, ((Q, CHUNK), BF16), ((Q, CHUNK), BF16), planes_shape,
+         ((ROWS, Q + ROWS), BF16), ((Q, ROWS), BF16), ((L // 2, 128, 128), F32), ((C, C), F32),
+         ((1, C), F32)],
+        [arrived, delta, point_weight, phases],
+        big=(1,), big_outs=(0, 1, 2), sems=3, room=16,
     )
     return (
         input_grad.reshape(field.shape),

time: 99.3 us -> 95.5 us (0.962)
  blocking collectives: 10.9 us -> 35.8 us
  starting transfers between devices: 26.8 us -> 15.2 us
  waiting for transfers between devices: 23 us -> 12.7 us
  local copies, waits for them, and re-layouts: 4.98 us -> 0.84 us
  Pallas kernels: 32.4 us -> 29.8 us
    all_to_all x1 -> x3, blocking collectives: 10.9 us -> 35.8 us  [exchange(): lax.all_to_all(v.reshape(S, 8, width), axis, split_axis=0, concat_axis=0,...]
    all_to_all x4 -> x2, starting transfers between devices: 26.8 us -> 15.2 us  [exchange(): lax.all_to_all(v.reshape(S, 8, width), axis, split_axis=0, concat_axis=0,...]
    all_to_all x4 -> x2, waiting for transfers between devices: 23 us -> 12.7 us  [exchange(): lax.all_to_all(v.reshape(S, 8, width), axis, split_axis=0, concat_axis=0,...]
    reshape x2 -> x0, local copies, waits for them, and re-layouts: 4.13 us -> none  [the longest x1 2.11 us: body(): cot2 = cotangent.reshape(ROWS, CELLS)]
    pallas_call x8, Pallas kernels: 32.4 us -> 29.8 us  [call(): pl.pallas_call(kernel, in_specs=[place(n, big) for n in range(len(args))]...]
  transfers between devices with their start and end apart: 4 -> 2, of which waited for: 4 -> 2; matrix products, arithmetic and copies ran while one was open for 5% -> 1% of each run, Pallas kernels for 4% -> 4%
where the time goes in v4:
time: 95.5 us; the launch traced here: 95.1 us
  blocking collectives  35.8 us (37%)
  Pallas kernels  29.8 us (31%)
  starting transfers between devices  15.2 us (16%)
  waiting for transfers between devices  12.7 us (13%)
    all_to_all x3, blocking collectives, exchange(): lax.all_to_all(v.reshape(S, 8, width), axis, split_axis=0, concat_axis=0,...  35.8 us
    pallas_call x8, Pallas kernels, call(): pl.pallas_call(kernel, in_specs=[place(n, big) for n in range(len(args))]...  29.8 us
    all_to_all x2, starting transfers between devices, exchange(): lax.all_to_all(v.reshape(S, 8, width), axis, split_axis=0, concat_axis=0,...  15.2 us
    all_to_all x2, waiting for transfers between devices, exchange(): lax.all_to_all(v.reshape(S, 8, width), axis, split_axis=0, concat_axis=0,...  12.7 us
  transfers between devices with their start and end apart: 2, of which 2 were waited for; matrix products, arithmetic and copies ran while one was open for 1% of the time, Pallas kernels for 4%

profile of v4, /device:TPU:1, one launch (start us, length us, event | category | flops | bytes accessed | tf_op | source)
XLA Modules:
  0.0 95.1 jit_solution(15497024062402755947)
XLA Ops:
  0.6 0.0 copy-start.2
  0.6 0.0 copy-start.6
  0.7 5.6 %spectra.1 = (bf16[128,1024]{1,0:T(8,128)(2,1)S(1)}, bf16[784,4096]{1,0:T(8,128)(2,1)S(1)}) custom-call(bf16[64,4,4096]{2,1,0:T(4,128)(2,1)} %bitcast.28, f32[160,128]{1,0:T(8,128)} %constant.20.clone.phase_hbm.phase_ref), custom_call_target="tpu_custom_call" | custom-call | tf_op jit(solution)/shard_map/spectra/pallas_call | solution.py:541
  6.2 14.3 %all_to_all.25 = bf16[16,8,1024]{2,1,0:T(8,128)(2,1)S(1)} all-to-all(bf16[16,8,1024]{2,1,0:T(8,128)(2,1)S(1)} %bitcast.25), channel_id=1, replica_groups=mesh['dp'=16,'slab'=16] {'slab'}, dimensions={0} | all-to-all | bytes 524288 | tf_op jit(solution)/shard_map/all_to_all | solution.py:563
  20.6 3.4 %mix.1 = (bf16[128,1024]{1,0:T(8,128)(2,1)S(1)}, bf16[64,1024]{1,0:T(8,128)(2,1)S(1)}) custom-call(bf16[128,1024]{1,0:T(8,128)(2,1)S(1)} %bitcast.22, bf16[16,16,64,128]{3,2,1,0:T(8,128)(2,1)} %w_hbm.3, bf16[64,128]{1,0:T(8,128)(2,1)S(1)} %copy-done.2, bf16[128,64]{1,0:T(8,128)(2,1)S(1)} %copy-done.6), custom_call_target="tpu_custom_call" | custom-call | tf_op jit(solution)/shard_map/mix/pallas_call | solution.py:541
  24.0 10.6 %all_to_all.26 = bf16[16,8,1024]{2,1,0:T(8,128)(2,1)S(1)} all-to-all(bf16[16,8,1024]{2,1,0:T(8,128)(2,1)S(1)} %bitcast.24), channel_id=1, replica_groups=mesh['dp'=16,'slab'=16] {'slab'}, dimensions={0} | all-to-all | bytes 524288 | tf_op jit(solution)/shard_map/all_to_all | solution.py:563
  34.6 0.0 copy-done.8
  34.6 0.0 copy-start.5
  34.6 9.4 %delta.1 = (bf16[128,1152]{1,0:T(8,128)(2,1)S(1)}, bf16[256,4096]{1,0:T(8,128)(2,1)}) custom-call(bf16[128,1024]{1,0:T(8,128)(2,1)S(1)} %bitcast.21, bf16[784,4096]{1,0:T(8,128)(2,1)S(1)} %get-tuple-element.17.tf_ref, bf16[64,4,4096]{2,1,0:T(4,128)(2,1)} %bitcast.27, bf16[64,64]{1,0:T(8,128)(2,1)S(1)} %copy-done.1, f32[1,64]{1,0:T(1,128)S(1)} %bitcast.26), custom_call_target="tpu_custom_call" | custom-call | tf_op jit(solution)/shard_map/delta/pallas_call | solution.py:541
  44.0 10.9 %all_to_all.27 = bf16[16,8,1152]{2,1,0:T(8,128)(2,1)S(1)} all-to-all(bf16[16,8,1152]{2,1,0:T(8,128)(2,1)S(1)} %bitcast.23), channel_id=1, replica_groups=mesh['dp'=16,'slab'=16] {'slab'}, dimensions={0} | all-to-all | bytes 589824 | tf_op jit(solution)/shard_map/all_to_all | solution.py:563
  54.9 0.0 copy-done.3
  54.9 1.1 %grad_modes.1 = (bf16[64,1024]{1,0:T(8,128)(2,1)S(1)}, bf16[128,640]{1,0:T(8,128)(2,1)}) custom-call(bf16[128,1152]{1,0:T(8,128)(2,1)S(1)} %bitcast.20, bf16[64,1024]{1,0:T(8,128)(2,1)S(1)} %get-tuple-element.19.m_ref, bf16[64,128]{1,0:T(8,128)(2,1)S(1)} %copy-done.2, bf16[64,128]{1,0:T(8,128)(2,1)S(1)} %copy-done.7, bf16[2,128,128]{2,1,0:T(8,128)(2,1)S(1)} %copy-done.3), custom_call_target="tpu_custom_call" | custom-call | tf_op jit(solution)/shard_map/grad_modes/pallas_call | solution.py:541
  56.1 9.8 %all-to-all-start.3 = ((bf16[16,8,640]{2,1,0:T(8,128)(2,1)}), bf16[16,8,640]{2,1,0:T(8,128)(2,1)S(1)}, u32[]{:S(2)}, u32[]{:S(2)}) async-start(bf16[16,8,640]{2,1,0:T(8,128)(2,1)} %bitcast.9), calls=%async_computation.3 | async-start | bytes 327680 | tf_op jit(solution)/shard_map/all_to_all | solution.py:563
  65.9 0.0 copy-start.4
  65.9 3.4 %adjoint.1.v_ref = bf16[128,1024]{1,0:T(8,128)(2,1)S(1)} custom-call(bf16[64,1024]{1,0:T(8,128)(2,1)S(1)} %get-tuple-element.20.left_ref, bf16[16,16,64,128]{3,2,1,0:T(8,128)(2,1)} %w_hbm.3, bf16[128,64]{1,0:T(8,128)(2,1)S(1)} %copy-done.5), custom_call_target="tpu_custom_call" | custom-call | tf_op jit(solution)/shard_map/adjoint/pallas_call | solution.py:541
  69.3 0.0 copy-start
  69.3 6.8 %all-to-all-done.3 = bf16[16,8,640]{2,1,0:T(8,128)(2,1)S(1)} async-done(((bf16[16,8,640]{2,1,0:T(8,128)(2,1)}), bf16[16,8,640]{2,1,0:T(8,128)(2,1)S(1)}, u32[]{:S(2)}, u32[]{:S(2)}) %all-to-all-start.3) | async-done | bytes 163872 | tf_op jit(solution)/shard_map/all_to_all | solution.py:563
  76.1 0.9 join.1
  77.0 5.3 %all-to-all-start.4 = ((bf16[16,8,1152]{2,1,0:T(8,128)(2,1)}), bf16[16,8,1152]{2,1,0:T(8,128)(2,1)S(1)}, u32[]{:S(2)}, u32[]{:S(2)}) async-start(bf16[16,8,1152]{2,1,0:T(8,128)(2,1)} %bitcast.11), calls=%async_computation.4 | async-start | bytes 589824 | tf_op jit(solution)/shard_map/all_to_all | solution.py:563
  82.4 0.8 weight_grad.1
  83.1 0.8 copy.16
  83.9 5.9 %all-to-all-done.4 = bf16[16,8,1152]{2,1,0:T(8,128)(2,1)S(1)} async-done(((bf16[16,8,1152]{2,1,0:T(8,128)(2,1)}), bf16[16,8,1152]{2,1,0:T(8,128)(2,1)S(1)}, u32[]{:S(2)}, u32[]{:S(2)}) %all-to-all-start.4) | async-done | bytes 294944 | tf_op jit(solution)/shard_map/all_to_all | solution.py:563
  89.9 0.0 copy-done
  89.9 5.2 %input_grad.1 = (bf16[64,4,4096]{2,1,0:T(4,128)(2,1)}, f32[64,64]{1,0:T(8,128)}, f32[1,64]{1,0:T(1,128)}) custom-call(bf16[128,1152]{1,0:T(8,128)(2,1)S(1)} %bitcast.19, bf16[256,4096]{1,0:T(8,128)(2,1)} %get-tuple-element.22.d_hbm, bf16[64,64]{1,0:T(8,128)(2,1)S(1)} %copy-done.1, f32[160,128]{1,0:T(8,128)S(1)} %copy-done), custom_call_target="tpu_custom_call" | custom-call | tf_op jit(solution)/shard_map/input_grad/pallas_call | solution.py:541
  (10 shorter events, 0.0 us)
Async XLA Ops:
  0.6 19.9 %copy-start.2 = (bf16[64,128]{1,0:T(8,128)(2,1)S(1)}, bf16[64,128]{1,0:T(8,128)(2,1)}, u32[]{:S(2)}) copy-start(bf16[64,128]{1,0:T(8,128)(2,1)} %constant.14.clone.fx_ref) | copy-start | bytes 49156
  0.6 19.9 %copy-start.6 = (bf16[128,64]{1,0:T(8,128)(2,1)S(1)}, bf16[128,64]{1,0:T(8,128)(2,1)}, u32[]{:S(2)}) copy-start(bf16[128,64]{1,0:T(8,128)(2,1)} %constant.16.clone.iv_ref) | copy-start | bytes 49156
  20.6 14.0 %copy-start.1 = (bf16[64,64]{1,0:T(8,128)(2,1)S(1)}, bf16[64,64]{1,0:T(8,128)(2,1)}, u32[]{:S(2)}) copy-start(bf16[64,64]{1,0:T(8,128)(2,1)} %w_ref.3) | copy-start | bytes 24580
  20.6 14.0 %copy-start.8 = (f32[64]{0:T(128)S(1)}, f32[64]{0:T(128)}, u32[]{:S(2)}) copy-start(f32[64]{0:T(128)} %param.16) | copy-start | bytes 772
  34.6 20.3 %copy-start.3 = (bf16[2,128,128]{2,1,0:T(8,128)(2,1)S(1)}, bf16[2,128,128]{2,1,0:T(8,128)(2,1)}, u32[]{:S(2)}) copy-start(bf16[2,128,128]{2,1,0:T(8,128)(2,1)} %constant.18.clone.gather_ref) | copy-start | bytes 196612
  34.6 20.3 %copy-start.7 = (bf16[64,128]{1,0:T(8,128)(2,1)S(1)}, bf16[64,128]{1,0:T(8,128)(2,1)}, u32[]{:S(2)}) copy-start(bf16[64,128]{1,0:T(8,128)(2,1)} %constant.15.clone.fo_ref) | copy-start | bytes 49156
  34.6 31.3 %copy-start.5 = (bf16[128,64]{1,0:T(8,128)(2,1)S(1)}, bf16[128,64]{1,0:T(8,128)(2,1)}, u32[]{:S(2)}) copy-start(bf16[128,64]{1,0:T(8,128)(2,1)} %constant.17.clone.ia_ref) | copy-start | bytes 49156
  56.1 20.1 %all-to-all-start.3 = ((bf16[16,8,640]{2,1,0:T(8,128)(2,1)}), bf16[16,8,640]{2,1,0:T(8,128)(2,1)S(1)}, u32[]{:S(2)}, u32[]{:S(2)}) async-start(bf16[16,8,640]{2,1,0:T(8,128)(2,1)} %bitcast.9), calls=%async_computation.3 | async-start | bytes 327680 | tf_op jit(solution)/shard_map/all_to_all | solution.py:563
  65.9 16.4 %copy-start.4 = (bf16[6,32,128]{2,1,0:T(8,128)(2,1)S(1)}, bf16[6,32,128]{2,1,0:T(8,128)(2,1)}, u32[]{:S(2)}) copy-start(bf16[6,32,128]{2,1,0:T(8,128)(2,1)} %constant.19.clone.pick_ref) | copy-start | bytes 147460
  69.3 20.6 %copy-start = (f32[160,128]{1,0:T(8,128)S(1)}, f32[160,128]{1,0:T(8,128)}, u32[]{:S(2)}) copy-start(f32[160,128]{1,0:T(8,128)} %constant.20.clone.phase_hbm.phase_ref) | copy-start | bytes 245764
  77.0 12.9 %all-to-all-start.4 = ((bf16[16,8,1152]{2,1,0:T(8,128)(2,1)}), bf16[16,8,1152]{2,1,0:T(8,128)(2,1)S(1)}, u32[]{:S(2)}, u32[]{:S(2)}) async-start(bf16[16,8,1152]{2,1,0:T(8,128)(2,1)} %bitcast.11), calls=%async_computation.4 | async-start | bytes 589824 | tf_op jit(solution)/shard_map/all_to_all | solution.py:563

commit v5 on v4

--- a/solution.py
+++ b/solution.py
@@ -239,13 +239,14 @@
 
 
 def spectra_kernel(
-    f_hbm, phase_hbm,
-    out_ref, tf_ref,
+    f_hbm, phase_hbm, w_hbm,
+    out_ref, tf_ref, w_ref,
     f_ref, ta_ref, tb_ref, acc_ref, z_ref, phase_ref, f_sem, p_sem,
 ):
     phases = pltpu.make_async_copy(phase_hbm, phase_ref, p_sem.at[0])
     phases.start()
     start_all(planes, f_hbm, f_ref, f_sem)
+    weights = pltpu.make_async_copy(w_hbm, w_ref, p_sem.at[1])
     acc_ref[...] = jnp.zeros_like(acc_ref)
     tf_ref[Q + ROWS :, :] = jnp.ones((16, CELLS), BF16)
     perm = lane_order()
@@ -261,6 +262,7 @@
         acc_ref[...] += nt(buf_ref[...], flat)
 
     ca, sa = make(0, phase_ref[:32, :], phase_ref[32:64, :], ta_ref)
+    weights.start()
 
     def step(m, carry):
         n = 2 * m
@@ -278,10 +280,10 @@
     make(STEPS - 1, ca, sa, tb_ref)
     add(STEPS - 1, tb_ref)
     pack_spectra(acc_ref[...], perm, z_ref, out_ref)
-
-
-def mix_kernel(r_ref, w_hbm, fx_ref, iv_ref, out_ref, m_ref, w_ref, mask_ref, v_ref, w_sem):
-    start_all(modes_pair, w_hbm, w_ref, w_sem)
+    weights.wait()
+
+
+def mix_kernel(r_ref, w_ref, fx_ref, iv_ref, out_ref, m_ref, mask_ref, v_ref):
     m = mm(fx_ref[...], r_ref[...])
     m_ref[...] = m.astype(BF16)
     shape = m.shape
@@ -296,7 +298,6 @@
     def step(u, carry):
         cols = pl.ds(pl.multiple_of(u * 128, 128), 128)
         pair = pl.ds(2 * u, 2)
-        modes_pair(w_hbm, w_ref, w_sem, u).wait()
         for t in range(8):
             left = mask_ref[8 * t : 8 * t + 8, cols].astype(BF16)
             right = jnp.concatenate(
@@ -415,7 +416,7 @@
     return jnp.concatenate([split(v).astype(F32)] * S, axis=0).astype(BF16)
 
 
-def grad_modes_kernel(r_ref, m_ref, fx_ref, fo_ref, gather_ref, left_ref, dp_ref):
+def grad_modes_kernel(r_ref, m_ref, fx_ref, fo_ref, gather_ref, left_ref, dp_ref, ext_ref):
     r = r_ref[:, :1024]
     a = mm(fx_ref[...], r)
     b = mm(fo_ref[...], r)
@@ -429,13 +430,11 @@
             first, jnp.where(low, au, half_turn(bu)), jnp.where(low, half_turn(au), bu)
         ).astype(BF16)
     both = jnp.concatenate([m_ref[...], a.astype(BF16)], axis=0)
-    dp_ref[:, :512] = (
-        mm(gather_ref[0], both[:, :512]) + mm(gather_ref[1], both[:, 512:])
-    ).astype(BF16)
-    dp_ref[:, 512:] = spread_total(total_of(r_ref[:, 1024:]))
-
-
-def adjoint_kernel(left_ref, w_hbm, ia_ref, out_ref, w_ref, v_ref, w_sem):
+    dp_ref[...] = (mm(gather_ref[0], both[:, :512]) + mm(gather_ref[1], both[:, 512:])).astype(BF16)
+    ext_ref[...] = spread_total(total_of(r_ref[:, 1024:]))
+
+
+def adjoint_kernel(left_ref, w_hbm, ia_ref, ext_ref, out_ref, w_ref, v_ref, w_sem):
     start_all(modes_pair, w_hbm, w_ref, w_sem)
     row, lane = subl((8, 128)), lanes((8, 128))
     top = row < 4
@@ -456,15 +455,41 @@
         return carry
 
     lax.fori_loop(0, L // 2, step, 0)
-    out_ref[...] = mm(ia_ref[...], v_ref[...].astype(BF16)).astype(BF16)
-
-
-def join_kernel(v_ref, dp_ref, out_ref):
-    out_ref[:, :1024] = v_ref[...]
-    out_ref[:, 1024:] = spread_total(total_of(dp_ref[:, 512:]))
-
-
-def weight_grad_kernel(dp_ref, pick_ref, out_ref):
+    out_ref[:, :1024] = mm(ia_ref[...], v_ref[...].astype(BF16)).astype(BF16)
+    out_ref[:, 1024:] = ext_ref[...]
+
+
+def assemble_kernel(r_ref, part_ref, out_ref):
+    out_ref[:, :512] = part_ref[...]
+    v = mm(ext_order(lanes(SQUARE), subl(SQUARE)), r_ref[:, 1024:])
+    v = v + half_turn(v)
+    low = low_half((8, 128))
+    tiles = [jnp.where(low, v[p : p + 8], v[p + 8 : p + 16]) for p in range(0, C, 16)]
+    diag = subl((C, 128)) == lanes((C, 128))
+    hi, lo = halves_of(jnp.sum(jnp.where(diag, v[C:], 0.0), axis=0, keepdims=True))
+    row = subl((8, 128))
+    bias = jnp.where(row == 0, hi.astype(F32), jnp.where(row == 1, lo.astype(F32), 0.0))
+    sums = jnp.concatenate(tiles + [bias], axis=1)
+    out_ref[:, 512:] = jnp.concatenate([sums] * S, axis=0).astype(BF16)
+
+
+def weight_grad_kernel(
+    dp_ref, pick_ref, out_hbm, pg_hbm, bg_hbm, out_ref, pg_ref, bg_ref, o_sem, g_sem
+):
+    shape = (8, 128)
+    which = onehot((lanes(shape) & 7) == subl(shape))
+    sums = mm(which, dp_ref[:, 512:]) * (1.0 / 2048.0)
+    for p in range(4):
+        tile = sums[:, p * 128 : p * 128 + 128]
+        pg_ref[p * 16 : p * 16 + 8, :] = tile[:, :C]
+        pg_ref[p * 16 + 8 : p * 16 + 16, :] = half_turn(tile)[:, :C]
+    bg_ref[...] = sums[0:1, 512 : 512 + C] + sums[1:2, 512 : 512 + C]
+    copies = [
+        pltpu.make_async_copy(pg_ref, pg_hbm, g_sem.at[0]),
+        pltpu.make_async_copy(bg_ref, bg_hbm, g_sem.at[1]),
+    ]
+    for copy in copies:
+        copy.start()
     low = low_half((32, 128))
     data = dp_ref[:, :512]
     for h in range(2):
@@ -481,27 +506,21 @@
             l = h * 8 + v * 2
             out_ref[l] = o[:64, :128]
             out_ref[l + 1] = o[64:, 128:]
+        part = pl.ds(h * 8, 8)
+        copies.append(pltpu.make_async_copy(out_ref.at[part], out_hbm.at[part], o_sem.at[h]))
+        copies[-1].start()
+    for copy in copies:
+        copy.wait()
 
 
 def input_grad_kernel(
     r_ref, d_hbm, w_ref, phase_ref,
-    out_hbm, pg_hbm, bg_hbm,
-    d_ref, ta_ref, tb_ref, o_ref, bl_ref, bt_ref, z_ref, pg_ref, bg_ref, d_sem, o_sem, g_sem,
+    out_hbm,
+    d_ref, ta_ref, tb_ref, o_ref, bl_ref, bt_ref, z_ref, d_sem, o_sem,
 ):
     start_all(columns, d_hbm, d_ref, d_sem)
     bl_ref[:, :Q] = unpack_back(r_ref[:, :1024], lane_order(), z_ref, bt_ref, False)
     bl_ref[:, Q:] = spread_weight(w_ref[...]).astype(F32).T.astype(BF16)
-    v = mm(ext_order(lanes(SQUARE), subl(SQUARE)), r_ref[:, 1024:])
-    v = (v + half_turn(v)) * (1.0 / 2048.0)
-    pg_ref[...] = v[:C, :C]
-    diag = subl((C, C)) == lanes((C, C))
-    bg_ref[...] = jnp.sum(jnp.where(diag, v[C:, :C], 0.0), axis=0, keepdims=True)
-    small = [
-        pltpu.make_async_copy(pg_ref, pg_hbm, g_sem.at[0]),
-        pltpu.make_async_copy(bg_ref, bg_hbm, g_sem.at[1]),
-    ]
-    for copy in small:
-        copy.start()
 
     def finish(n, own_ref):
         out = mm(bl_ref[:, :Q], own_ref[...]) + mm(bl_ref[:, Q:], d_ref[:, at(n)])
@@ -532,8 +551,6 @@
     finish(STEPS - 1, tb_ref)
     planes(o_ref, out_hbm, o_sem, STEPS - 1).start()
     wait_all(planes, o_ref, out_hbm, o_sem)
-    for copy in small:
-        copy.wait()
 
 
 def call(kernel, name, outs, scratch, args, big=(), big_outs=(), sems=0, room=8):
@@ -573,23 +590,22 @@
     weight_shape = (spectral_weight.shape, BF16)
 
     phases = jnp.asarray(phase_tables())
-    spectra, rows = call(
+    spectra, rows, weights = call(
         spectra_kernel,
         "spectra",
-        [((128, 1024), BF16), ((Q + ROWS + 16, CELLS), BF16)],
+        [((128, 1024), BF16), ((Q + ROWS + 16, CELLS), BF16), weight_shape],
         [planes_shape, ((Q, CHUNK), BF16), ((Q, CHUNK), BF16), ((Q, ROWS), F32),
          ((L // 2, 128, 128), F32), ((160, 128), F32)],
-        [field3, phases],
-        big=(0, 1), sems=2,
+        [field3, phases, spectral_weight],
+        big=(0, 1, 2), sems=2,
     )
     arrived = exchange(spectra, "slab")
     back, modes = call(
         mix_kernel,
         "mix",
         [((128, 1024), BF16), ((64, 1024), BF16)],
-        [weight_shape, ((64, 1024), F32), ((64, 1024), F32)],
-        [arrived, spectral_weight, k["fx"], k["iv"]],
-        big=(1,), sems=1,
+        [((64, 1024), F32), ((64, 1024), F32)],
+        [arrived, weights, k["fx"], k["iv"]],
     )
     arrived = exchange(back, "slab")
     grad_spectra, delta = call(
@@ -606,36 +622,40 @@
         big=(2,), big_outs=(1,), sems=2, room=16,
     )
     arrived = exchange(grad_spectra, "slab")
-    left, shared = call(
+    left, part, sums = call(
         grad_modes_kernel,
         "grad_modes",
-        [((64, 1024), BF16), ((128, 640), BF16)],
+        [((64, 1024), BF16), ((128, 512), BF16), (SQUARE, BF16)],
         [],
         [arrived, modes, k["fx"], k["fo"], k["gather"]],
     )
-    shared = exchange(shared, "dp")
     (adjoint,) = call(
         adjoint_kernel,
         "adjoint",
-        [((128, 1024), BF16)],
+        [((128, 1152), BF16)],
         [weight_shape, ((64, 1024), F32)],
-        [left, spectral_weight, k["ia"]],
+        [left, spectral_weight, k["ia"], sums],
         big=(1,), sems=1,
     )
-    (joined,) = call(join_kernel, "join", [((128, 1152), BF16)], [], [adjoint, shared])
-    arrived = exchange(joined, "slab")
-    (spectral_grad,) = call(
-        weight_grad_kernel, "weight_grad", [((L, C, 128), F32)], [], [shared, k["pick"]]
-    )
-    input_grad, point_grad, bias_grad = call(
+    arrived = exchange(adjoint, "slab")
+    (shared,) = call(assemble_kernel, "assemble", [((128, 1152), BF16)], [], [arrived, part])
+    shared = exchange(shared, "dp")
+    (input_grad,) = call(
         input_grad_kernel,
         "input_grad",
-        [planes_shape, ((C, C), F32), ((1, C), F32)],
+        [planes_shape],
         [cells_shape, ((Q, CHUNK), BF16), ((Q, CHUNK), BF16), planes_shape,
-         ((ROWS, Q + ROWS), BF16), ((Q, ROWS), BF16), ((L // 2, 128, 128), F32), ((C, C), F32),
-         ((1, C), F32)],
+         ((ROWS, Q + ROWS), BF16), ((Q, ROWS), BF16), ((L // 2, 128, 128), F32)],
         [arrived, delta, point_weight, phases],
-        big=(1,), big_outs=(0, 1, 2), sems=3, room=16,
+        big=(1,), big_outs=(0,), sems=2, room=16,
+    )
+    spectral_grad, point_grad, bias_grad = call(
+        weight_grad_kernel,
+        "weight_grad",
+        [((L, C, 128), F32), ((C, C), F32), ((1, C), F32)],
+        [((L, C, 128), F32), ((C, C), F32), ((1, C), F32)],
+        [shared, k["pick"]],
+        big_outs=(0, 1, 2), sems=2,
     )
     return (
         input_grad.reshape(field.shape),

time: 95.5 us -> 94 us (0.984)
  blocking collectives: 35.8 us -> 46.8 us
  starting transfers between devices: 15.2 us -> 9.86 us
  waiting for transfers between devices: 12.7 us -> 7.78 us
  Pallas kernels: 29.8 us -> 28.2 us
    all_to_all x3 -> x4, blocking collectives: 35.8 us -> 46.8 us  [exchange(): lax.all_to_all(v.reshape(S, 8, width), axis, split_axis=0, concat_axis=0,...]
    all_to_all x2 -> x1, starting transfers between devices: 15.2 us -> 9.86 us  [exchange(): lax.all_to_all(v.reshape(S, 8, width), axis, split_axis=0, concat_axis=0,...]
    all_to_all x2 -> x1, waiting for transfers between devices: 12.7 us -> 7.78 us  [exchange(): lax.all_to_all(v.reshape(S, 8, width), axis, split_axis=0, concat_axis=0,...]
    pallas_call x8, Pallas kernels: 29.8 us -> 28.2 us  [call(): pl.pallas_call(kernel, in_specs=[place(n, big) for n in range(len(args))]...]
  transfers between devices with their start and end apart: 2 -> 1, of which waited for: 2 -> 1; matrix products, arithmetic and copies ran while one was open for 1% -> 0% of each run, Pallas kernels for 4% -> 5%
where the time goes in v5:
time: 94 us; the launch traced here: 93.4 us
  blocking collectives  46.8 us (50%)
  Pallas kernels  28.2 us (30%)
  starting transfers between devices  9.86 us (10%)
  waiting for transfers between devices  7.78 us (8%)
    all_to_all x4, blocking collectives, exchange(): lax.all_to_all(v.reshape(S, 8, width), axis, split_axis=0, concat_axis=0,...  46.8 us
    pallas_call x8, Pallas kernels, call(): pl.pallas_call(kernel, in_specs=[place(n, big) for n in range(len(args))]...  28.2 us
    all_to_all x1, starting transfers between devices, exchange(): lax.all_to_all(v.reshape(S, 8, width), axis, split_axis=0, concat_axis=0,...  9.86 us
    all_to_all x1, waiting for transfers between devices, exchange(): lax.all_to_all(v.reshape(S, 8, width), axis, split_axis=0, concat_axis=0,...  7.78 us
  transfers between devices with their start and end apart: 1, of which 1 were waited for; matrix products, arithmetic and copies ran while one was open for 0% of the time, Pallas kernels for 5%

profile of v5, /device:TPU:1, one launch (start us, length us, event | category | flops | bytes accessed | tf_op | source)
XLA Modules:
  0.0 93.4 jit_solution(6468905142103100110)
XLA Ops:
  0.6 0.0 copy-start.2
  0.6 0.0 copy-start.6
  0.7 5.3 %spectra.1 = (bf16[128,1024]{1,0:T(8,128)(2,1)S(1)}, bf16[784,4096]{1,0:T(8,128)(2,1)S(1)}, bf16[16,16,64,128]{3,2,1,0:T(8,128)(2,1)S(1)}) custom-call(bf16[64,4,4096]{2,1,0:T(4,128)(2,1)} %bitcast.27, f32[160,128]{1,0:T(8,128)} %constant.20.clone.phase_hbm.phase_ref, bf16[16,16,64,128]{3,2,1,0:T(8,128)(2,1)} %w_hbm.3), custom_call_target="tpu_custom_call" | custom-call | tf_op jit(solution)/shard_map/spectra/pallas_call | solution.py:558
  6.0 14.3 %all_to_all.25 = bf16[16,8,1024]{2,1,0:T(8,128)(2,1)S(1)} all-to-all(bf16[16,8,1024]{2,1,0:T(8,128)(2,1)S(1)} %bitcast.25), channel_id=1, replica_groups=mesh['dp'=16,'slab'=16] {'slab'}, dimensions={0} | all-to-all | bytes 524288 | tf_op jit(solution)/shard_map/all_to_all | solution.py:580
  20.3 0.0 copy-done.2
  20.3 0.0 copy-done.6
  20.3 2.4 %mix.1 = (bf16[128,1024]{1,0:T(8,128)(2,1)S(1)}, bf16[64,1024]{1,0:T(8,128)(2,1)S(1)}) custom-call(bf16[128,1024]{1,0:T(8,128)(2,1)S(1)} %bitcast.21, bf16[16,16,64,128]{3,2,1,0:T(8,128)(2,1)S(1)} %get-tuple-element.18.w_ref, bf16[64,128]{1,0:T(8,128)(2,1)S(1)} %copy-done.2, bf16[128,64]{1,0:T(8,128)(2,1)S(1)} %copy-done.6), custom_call_target="tpu_custom_call" | custom-call | tf_op jit(solution)/shard_map/mix/pallas_call | solution.py:558
  22.8 10.6 %all_to_all.26 = bf16[16,8,1024]{2,1,0:T(8,128)(2,1)S(1)} all-to-all(bf16[16,8,1024]{2,1,0:T(8,128)(2,1)S(1)} %bitcast.24), channel_id=1, replica_groups=mesh['dp'=16,'slab'=16] {'slab'}, dimensions={0} | all-to-all | bytes 524288 | tf_op jit(solution)/shard_map/all_to_all | solution.py:580
  33.4 0.0 copy-done.8
  33.4 0.0 copy-start.5
  33.4 9.4 %delta.1 = (bf16[128,1152]{1,0:T(8,128)(2,1)S(1)}, bf16[256,4096]{1,0:T(8,128)(2,1)}) custom-call(bf16[128,1024]{1,0:T(8,128)(2,1)S(1)} %bitcast.22, bf16[784,4096]{1,0:T(8,128)(2,1)S(1)} %get-tuple-element.20.tf_ref, bf16[64,4,4096]{2,1,0:T(4,128)(2,1)} %bitcast.28, bf16[64,64]{1,0:T(8,128)(2,1)S(1)} %copy-done.1, f32[1,64]{1,0:T(1,128)S(1)} %bitcast.26), custom_call_target="tpu_custom_call" | custom-call | tf_op jit(solution)/shard_map/delta/pallas_call | solution.py:558
  42.9 10.9 %all_to_all.27 = bf16[16,8,1152]{2,1,0:T(8,128)(2,1)S(1)} all-to-all(bf16[16,8,1152]{2,1,0:T(8,128)(2,1)S(1)} %bitcast.23), channel_id=1, replica_groups=mesh['dp'=16,'slab'=16] {'slab'}, dimensions={0} | all-to-all | bytes 589824 | tf_op jit(solution)/shard_map/all_to_all | solution.py:580
  53.8 0.0 copy-done.7
  53.8 0.5 grad_modes.1
  54.2 0.0 copy-done.5
  54.2 0.0 copy-start
  54.3 3.4 %adjoint.1 = bf16[128,1152]{1,0:T(8,128)(2,1)S(1)} custom-call(bf16[64,1024]{1,0:T(8,128)(2,1)S(1)} %get-tuple-element.23.left_ref, bf16[16,16,64,128]{3,2,1,0:T(8,128)(2,1)} %w_hbm.3, bf16[128,64]{1,0:T(8,128)(2,1)S(1)} %copy-done.5, bf16[128,128]{1,0:T(8,128)(2,1)S(1)} %get-tuple-element.24.ext_ref), custom_call_target="tpu_custom_call" | custom-call | tf_op jit(solution)/shard_map/adjoint/pallas_call | solution.py:558
  57.7 11.0 %all_to_all.28 = bf16[16,8,1152]{2,1,0:T(8,128)(2,1)S(1)} all-to-all(bf16[16,8,1152]{2,1,0:T(8,128)(2,1)S(1)} %bitcast.18), channel_id=1, replica_groups=mesh['dp'=16,'slab'=16] {'slab'}, dimensions={0} | all-to-all | bytes 589824 | tf_op jit(solution)/shard_map/all_to_all | solution.py:580
  68.6 0.9 %assemble.1 = bf16[128,1152]{1,0:T(8,128)(2,1)} custom-call(bf16[128,1152]{1,0:T(8,128)(2,1)S(1)} %bitcast.16, bf16[128,512]{1,0:T(8,128)(2,1)S(1)} %get-tuple-element.26.part_ref), custom_call_target="tpu_custom_call" | custom-call | tf_op jit(solution)/shard_map/assemble/pallas_call | solution.py:558
  69.6 9.9 %all-to-all-start.4 = ((bf16[16,8,1152]{2,1,0:T(8,128)(2,1)}), bf16[16,8,1152]{2,1,0:T(8,128)(2,1)S(1)}, u32[]{:S(2)}, u32[]{:S(2)}) async-start(bf16[16,8,1152]{2,1,0:T(8,128)(2,1)} %bitcast.12), calls=%async_computation.4 | async-start | bytes 589824 | tf_op jit(solution)/shard_map/all_to_all | solution.py:580
  79.4 0.0 copy-start.4
  79.5 4.5 %input_grad.1 = bf16[64,4,4096]{2,1,0:T(4,128)(2,1)} custom-call(bf16[128,1152]{1,0:T(8,128)(2,1)S(1)} %bitcast.17, bf16[256,4096]{1,0:T(8,128)(2,1)} %get-tuple-element.25.d_hbm, bf16[64,64]{1,0:T(8,128)(2,1)S(1)} %copy-done.1, f32[160,128]{1,0:T(8,128)S(1)} %copy-done), custom_call_target="tpu_custom_call" | custom-call | tf_op jit(solution)/shard_map/input_grad/pallas_call | solution.py:558
  84.0 7.8 %all-to-all-done.4 = bf16[16,8,1152]{2,1,0:T(8,128)(2,1)S(1)} async-done(((bf16[16,8,1152]{2,1,0:T(8,128)(2,1)}), bf16[16,8,1152]{2,1,0:T(8,128)(2,1)S(1)}, u32[]{:S(2)}, u32[]{:S(2)}) %all-to-all-start.4) | async-done | bytes 294944 | tf_op jit(solution)/shard_map/all_to_all | solution.py:580
  91.8 1.6 %weight_grad.1 = (f32[16,64,128]{2,1,0:T(8,128)}, f32[64,64]{1,0:T(8,128)}, f32[1,64]{1,0:T(1,128)}) custom-call(bf16[128,1152]{1,0:T(8,128)(2,1)S(1)} %bitcast.19, bf16[6,32,128]{2,1,0:T(8,128)(2,1)S(1)} %copy-done.4), custom_call_target="tpu_custom_call" | custom-call | tf_op jit(solution)/shard_map/weight_grad/pallas_call | solution.py:558
  (8 shorter events, 0.0 us)
Async XLA Ops:
  0.6 19.7 %copy-start.2 = (bf16[64,128]{1,0:T(8,128)(2,1)S(1)}, bf16[64,128]{1,0:T(8,128)(2,1)}, u32[]{:S(2)}) copy-start(bf16[64,128]{1,0:T(8,128)(2,1)} %constant.14.clone.fx_ref) | copy-start | bytes 49156
  0.6 19.7 %copy-start.6 = (bf16[128,64]{1,0:T(8,128)(2,1)S(1)}, bf16[128,64]{1,0:T(8,128)(2,1)}, u32[]{:S(2)}) copy-start(bf16[128,64]{1,0:T(8,128)(2,1)} %constant.16.clone.iv_ref) | copy-start | bytes 49156
  20.3 13.1 %copy-start.1 = (bf16[64,64]{1,0:T(8,128)(2,1)S(1)}, bf16[64,64]{1,0:T(8,128)(2,1)}, u32[]{:S(2)}) copy-start(bf16[64,64]{1,0:T(8,128)(2,1)} %w_ref.3) | copy-start | bytes 24580
  20.3 13.1 %copy-start.8 = (f32[64]{0:T(128)S(1)}, f32[64]{0:T(128)}, u32[]{:S(2)}) copy-start(f32[64]{0:T(128)} %param.16) | copy-start | bytes 772
  33.4 20.4 %copy-start.3 = (bf16[2,128,128]{2,1,0:T(8,128)(2,1)S(1)}, bf16[2,128,128]{2,1,0:T(8,128)(2,1)}, u32[]{:S(2)}) copy-start(bf16[2,128,128]{2,1,0:T(8,128)(2,1)} %constant.18.clone.gather_ref) | copy-start | bytes 196612
  33.4 20.4 %copy-start.7 = (bf16[64,128]{1,0:T(8,128)(2,1)S(1)}, bf16[64,128]{1,0:T(8,128)(2,1)}, u32[]{:S(2)}) copy-start(bf16[64,128]{1,0:T(8,128)(2,1)} %constant.15.clone.fo_ref) | copy-start | bytes 49156
  33.4 20.8 %copy-start.5 = (bf16[128,64]{1,0:T(8,128)(2,1)S(1)}, bf16[128,64]{1,0:T(8,128)(2,1)}, u32[]{:S(2)}) copy-start(bf16[128,64]{1,0:T(8,128)(2,1)} %constant.17.clone.ia_ref) | copy-start | bytes 49156
  54.2 25.2 %copy-start = (f32[160,128]{1,0:T(8,128)S(1)}, f32[160,128]{1,0:T(8,128)}, u32[]{:S(2)}) copy-start(f32[160,128]{1,0:T(8,128)} %constant.20.clone.phase_hbm.phase_ref) | copy-start | bytes 245764
  69.6 22.2 %all-to-all-start.4 = ((bf16[16,8,1152]{2,1,0:T(8,128)(2,1)}), bf16[16,8,1152]{2,1,0:T(8,128)(2,1)S(1)}, u32[]{:S(2)}, u32[]{:S(2)}) async-start(bf16[16,8,1152]{2,1,0:T(8,128)(2,1)} %bitcast.12), calls=%async_computation.4 | async-start | bytes 589824 | tf_op jit(solution)/shard_map/all_to_all | solution.py:580
  79.4 12.3 %copy-start.4 = (bf16[6,32,128]{2,1,0:T(8,128)(2,1)S(1)}, bf16[6,32,128]{2,1,0:T(8,128)(2,1)}, u32[]{:S(2)}) copy-start(bf16[6,32,128]{2,1,0:T(8,128)(2,1)} %constant.19.clone.pick_ref) | copy-start | bytes 147460

commit v6 on v5

--- a/solution.py
+++ b/solution.py
@@ -212,10 +212,6 @@
     return pltpu.make_async_copy(src.at[:, at(step)], dst.at[:, at(step)], sems.at[step])
 
 
-def modes_pair(src, dst, sems, u):
-    return pltpu.make_async_copy(src.at[:, pl.ds(2 * u, 2)], dst.at[:, pl.ds(2 * u, 2)], sems.at[u])
-
-
 def start_all(copy, src, dst, sems):
     for n in range(STEPS):
         copy(src, dst, sems, n).start()
@@ -319,7 +315,7 @@
 
 def slope(v):
     a = jnp.abs(v)
-    e = jnp.exp(v * v * -0.5)
+    e = jnp.exp2(v * v * (-0.5 / math.log(2.0)))
     t = 1.0 / (1.0 + (0.3275911 / math.sqrt(2.0)) * a)
     poly = t * (
         0.5 * 0.254829592
@@ -416,7 +412,9 @@
     return jnp.concatenate([split(v).astype(F32)] * S, axis=0).astype(BF16)
 
 
-def grad_modes_kernel(r_ref, m_ref, fx_ref, fo_ref, gather_ref, left_ref, dp_ref, ext_ref):
+def adjoint_kernel(
+    r_ref, m_ref, w_ref, fx_ref, fo_ref, ia_ref, gather_ref, out_ref, dp_ref, left_ref, v_ref
+):
     r = r_ref[:, :1024]
     a = mm(fx_ref[...], r)
     b = mm(fo_ref[...], r)
@@ -431,11 +429,7 @@
         ).astype(BF16)
     both = jnp.concatenate([m_ref[...], a.astype(BF16)], axis=0)
     dp_ref[...] = (mm(gather_ref[0], both[:, :512]) + mm(gather_ref[1], both[:, 512:])).astype(BF16)
-    ext_ref[...] = spread_total(total_of(r_ref[:, 1024:]))
-
-
-def adjoint_kernel(left_ref, w_hbm, ia_ref, ext_ref, out_ref, w_ref, v_ref, w_sem):
-    start_all(modes_pair, w_hbm, w_ref, w_sem)
+    out_ref[:, 1024:] = spread_total(total_of(r_ref[:, 1024:]))
     row, lane = subl((8, 128)), lanes((8, 128))
     top = row < 4
     keep = (lane >> 6) == ((row >> 1) & 1)
@@ -443,7 +437,6 @@
     def step(u, carry):
         cols = pl.ds(pl.multiple_of(u * 128, 128), 128)
         pair = pl.ds(2 * u, 2)
-        modes_pair(w_hbm, w_ref, w_sem, u).wait()
         for t in range(8):
             right = jnp.concatenate(
                 [w_ref[2 * t, pair].reshape(128, 128), w_ref[2 * t + 1, pair].reshape(128, 128)],
@@ -456,7 +449,6 @@
 
     lax.fori_loop(0, L // 2, step, 0)
     out_ref[:, :1024] = mm(ia_ref[...], v_ref[...].astype(BF16)).astype(BF16)
-    out_ref[:, 1024:] = ext_ref[...]
 
 
 def assemble_kernel(r_ref, part_ref, out_ref):
@@ -622,20 +614,12 @@
         big=(2,), big_outs=(1,), sems=2, room=16,
     )
     arrived = exchange(grad_spectra, "slab")
-    left, part, sums = call(
-        grad_modes_kernel,
-        "grad_modes",
-        [((64, 1024), BF16), ((128, 512), BF16), (SQUARE, BF16)],
-        [],
-        [arrived, modes, k["fx"], k["fo"], k["gather"]],
-    )
-    (adjoint,) = call(
+    adjoint, part = call(
         adjoint_kernel,
         "adjoint",
-        [((128, 1152), BF16)],
-        [weight_shape, ((64, 1024), F32)],
-        [left, spectral_weight, k["ia"], sums],
-        big=(1,), sems=1,
+        [((128, 1152), BF16), ((128, 512), BF16)],
+        [((64, 1024), BF16), ((64, 1024), F32)],
+        [arrived, modes, weights, k["fx"], k["fo"], k["ia"], k["gather"]],
     )
     arrived = exchange(adjoint, "slab")
     (shared,) = call(assemble_kernel, "assemble", [((128, 1152), BF16)], [], [arrived, part])

time: 94 us -> 92.9 us (0.988)
  Pallas kernels: 28.2 us -> 27.1 us
    pallas_call x8 -> x7, Pallas kernels: 28.2 us -> 27.1 us  [call(): pl.pallas_call(kernel, in_specs=[place(n, big) for n in range(len(args))]...]
where the time goes in v6:
time: 92.9 us; the launch traced here: 92.3 us
  blocking collectives  46.8 us (50%)
  Pallas kernels  27.1 us (29%)
  starting transfers between devices  9.85 us (11%)
  waiting for transfers between devices  7.78 us (8%)
    all_to_all x4, blocking collectives, exchange(): lax.all_to_all(v.reshape(S, 8, width), axis, split_axis=0, concat_axis=0,...  46.8 us
    pallas_call x7, Pallas kernels, call(): pl.pallas_call(kernel, in_specs=[place(n, big) for n in range(len(args))]...  27.1 us
    all_to_all x1, starting transfers between devices, exchange(): lax.all_to_all(v.reshape(S, 8, width), axis, split_axis=0, concat_axis=0,...  9.85 us
    all_to_all x1, waiting for transfers between devices, exchange(): lax.all_to_all(v.reshape(S, 8, width), axis, split_axis=0, concat_axis=0,...  7.78 us
  transfers between devices with their start and end apart: 1, of which 1 were waited for; matrix products, arithmetic and copies ran while one was open for 0% of the time, Pallas kernels for 5%

profile of v6, /device:TPU:1, one launch (start us, length us, event | category | flops | bytes accessed | tf_op | source)
XLA Modules:
  0.0 92.3 jit_solution(17476003762637302048)
XLA Ops:
  0.6 0.0 copy-start.3
  0.6 0.0 copy-start.6
  0.7 5.6 %spectra.1 = (bf16[128,1024]{1,0:T(8,128)(2,1)S(1)}, bf16[784,4096]{1,0:T(8,128)(2,1)S(1)}, bf16[16,16,64,128]{3,2,1,0:T(8,128)(2,1)S(1)}) custom-call(bf16[64,4,4096]{2,1,0:T(4,128)(2,1)} %bitcast.27, f32[160,128]{1,0:T(8,128)} %constant.20.clone.phase_hbm.phase_ref, bf16[16,16,64,128]{3,2,1,0:T(8,128)(2,1)} %w_hbm.1), custom_call_target="tpu_custom_call" | custom-call | tf_op jit(solution)/shard_map/spectra/pallas_call | solution.py:550
  6.2 14.3 %all_to_all.25 = bf16[16,8,1024]{2,1,0:T(8,128)(2,1)S(1)} all-to-all(bf16[16,8,1024]{2,1,0:T(8,128)(2,1)S(1)} %bitcast.25), channel_id=1, replica_groups=mesh['dp'=16,'slab'=16] {'slab'}, dimensions={0} | all-to-all | bytes 524288 | tf_op jit(solution)/shard_map/all_to_all | solution.py:572
  20.6 0.0 copy-done.3
  20.6 0.0 copy-done.6
  20.6 2.4 %mix.1 = (bf16[128,1024]{1,0:T(8,128)(2,1)S(1)}, bf16[64,1024]{1,0:T(8,128)(2,1)S(1)}) custom-call(bf16[128,1024]{1,0:T(8,128)(2,1)S(1)} %bitcast.21, bf16[16,16,64,128]{3,2,1,0:T(8,128)(2,1)S(1)} %get-tuple-element.17.w_ref, bf16[64,128]{1,0:T(8,128)(2,1)S(1)} %copy-done.3, bf16[128,64]{1,0:T(8,128)(2,1)S(1)} %copy-done.6), custom_call_target="tpu_custom_call" | custom-call | tf_op jit(solution)/shard_map/mix/pallas_call | solution.py:550
  23.0 10.6 %all_to_all.26 = bf16[16,8,1024]{2,1,0:T(8,128)(2,1)S(1)} all-to-all(bf16[16,8,1024]{2,1,0:T(8,128)(2,1)S(1)} %bitcast.24), channel_id=1, replica_groups=mesh['dp'=16,'slab'=16] {'slab'}, dimensions={0} | all-to-all | bytes 524288 | tf_op jit(solution)/shard_map/all_to_all | solution.py:572
  33.6 0.0 copy-done.2
  33.6 0.0 copy-done.8
  33.6 0.0 copy-start.7
  33.6 9.3 %delta.1 = (bf16[128,1152]{1,0:T(8,128)(2,1)S(1)}, bf16[256,4096]{1,0:T(8,128)(2,1)}) custom-call(bf16[128,1024]{1,0:T(8,128)(2,1)S(1)} %bitcast.20, bf16[784,4096]{1,0:T(8,128)(2,1)S(1)} %get-tuple-element.19.tf_ref, bf16[64,4,4096]{2,1,0:T(4,128)(2,1)} %bitcast.28, bf16[64,64]{1,0:T(8,128)(2,1)S(1)} %copy-done.2, f32[1,64]{1,0:T(1,128)S(1)} %bitcast.26), custom_call_target="tpu_custom_call" | custom-call | tf_op jit(solution)/shard_map/delta/pallas_call | solution.py:550
  43.0 10.9 %all_to_all.27 = bf16[16,8,1152]{2,1,0:T(8,128)(2,1)S(1)} all-to-all(bf16[16,8,1152]{2,1,0:T(8,128)(2,1)S(1)} %bitcast.23), channel_id=1, replica_groups=mesh['dp'=16,'slab'=16] {'slab'}, dimensions={0} | all-to-all | bytes 589824 | tf_op jit(solution)/shard_map/all_to_all | solution.py:572
  53.8 0.0 copy-done.1
  53.8 0.0 copy-done.5
  53.8 0.0 copy-start
  53.9 2.7 %adjoint.1 = (bf16[128,1152]{1,0:T(8,128)(2,1)S(1)}, bf16[128,512]{1,0:T(8,128)(2,1)S(1)}) custom-call(bf16[128,1152]{1,0:T(8,128)(2,1)S(1)} %bitcast.18, bf16[64,1024]{1,0:T(8,128)(2,1)S(1)} %get-tuple-element.21.m_ref, bf16[16,16,64,128]{3,2,1,0:T(8,128)(2,1)S(1)} %get-tuple-element.17.w_ref, bf16[64,128]{1,0:T(8,128)(2,1)S(1)} %copy-done.3, ...), custom_call_target="tpu_custom_call" | custom-call | tf_op jit(solution)/shard_map/adjoint/pallas_call | solution.py:550
  56.6 11.0 %all_to_all.28 = bf16[16,8,1152]{2,1,0:T(8,128)(2,1)S(1)} all-to-all(bf16[16,8,1152]{2,1,0:T(8,128)(2,1)S(1)} %bitcast.22), channel_id=1, replica_groups=mesh['dp'=16,'slab'=16] {'slab'}, dimensions={0} | all-to-all | bytes 589824 | tf_op jit(solution)/shard_map/all_to_all | solution.py:572
  67.5 0.9 %assemble.1 = bf16[128,1152]{1,0:T(8,128)(2,1)} custom-call(bf16[128,1152]{1,0:T(8,128)(2,1)S(1)} %bitcast.16, bf16[128,512]{1,0:T(8,128)(2,1)S(1)} %get-tuple-element.24.part_ref), custom_call_target="tpu_custom_call" | custom-call | tf_op jit(solution)/shard_map/assemble/pallas_call | solution.py:550
  68.5 9.8 %all-to-all-start.4 = ((bf16[16,8,1152]{2,1,0:T(8,128)(2,1)}), bf16[16,8,1152]{2,1,0:T(8,128)(2,1)S(1)}, u32[]{:S(2)}, u32[]{:S(2)}) async-start(bf16[16,8,1152]{2,1,0:T(8,128)(2,1)} %bitcast.12), calls=%async_computation.4 | async-start | bytes 589824 | tf_op jit(solution)/shard_map/all_to_all | solution.py:572
  78.4 0.0 copy-start.4
  78.4 4.5 %input_grad.1 = bf16[64,4,4096]{2,1,0:T(4,128)(2,1)} custom-call(bf16[128,1152]{1,0:T(8,128)(2,1)S(1)} %bitcast.17, bf16[256,4096]{1,0:T(8,128)(2,1)} %get-tuple-element.23.d_hbm, bf16[64,64]{1,0:T(8,128)(2,1)S(1)} %copy-done.2, f32[160,128]{1,0:T(8,128)S(1)} %copy-done), custom_call_target="tpu_custom_call" | custom-call | tf_op jit(solution)/shard_map/input_grad/pallas_call | solution.py:550
  82.9 7.8 %all-to-all-done.4 = bf16[16,8,1152]{2,1,0:T(8,128)(2,1)S(1)} async-done(((bf16[16,8,1152]{2,1,0:T(8,128)(2,1)}), bf16[16,8,1152]{2,1,0:T(8,128)(2,1)S(1)}, u32[]{:S(2)}, u32[]{:S(2)}) %all-to-all-start.4) | async-done | bytes 294944 | tf_op jit(solution)/shard_map/all_to_all | solution.py:572
  90.7 1.6 %weight_grad.1 = (f32[16,64,128]{2,1,0:T(8,128)}, f32[64,64]{1,0:T(8,128)}, f32[1,64]{1,0:T(1,128)}) custom-call(bf16[128,1152]{1,0:T(8,128)(2,1)S(1)} %bitcast.19, bf16[6,32,128]{2,1,0:T(8,128)(2,1)S(1)} %copy-done.4), custom_call_target="tpu_custom_call" | custom-call | tf_op jit(solution)/shard_map/weight_grad/pallas_call | solution.py:550
  (7 shorter events, 0.0 us)
Async XLA Ops:
  0.6 19.9 %copy-start.3 = (bf16[64,128]{1,0:T(8,128)(2,1)S(1)}, bf16[64,128]{1,0:T(8,128)(2,1)}, u32[]{:S(2)}) copy-start(bf16[64,128]{1,0:T(8,128)(2,1)} %constant.14.clone.fx_ref) | copy-start | bytes 49156
  0.6 19.9 %copy-start.6 = (bf16[128,64]{1,0:T(8,128)(2,1)S(1)}, bf16[128,64]{1,0:T(8,128)(2,1)}, u32[]{:S(2)}) copy-start(bf16[128,64]{1,0:T(8,128)(2,1)} %constant.16.clone.iv_ref) | copy-start | bytes 49156
  20.6 13.1 %copy-start.2 = (bf16[64,64]{1,0:T(8,128)(2,1)S(1)}, bf16[64,64]{1,0:T(8,128)(2,1)}, u32[]{:S(2)}) copy-start(bf16[64,64]{1,0:T(8,128)(2,1)} %w_ref.3) | copy-start | bytes 24580
  20.6 13.1 %copy-start.8 = (f32[64]{0:T(128)S(1)}, f32[64]{0:T(128)}, u32[]{:S(2)}) copy-start(f32[64]{0:T(128)} %param.16) | copy-start | bytes 772
  33.6 20.2 %copy-start.1 = (bf16[2,128,128]{2,1,0:T(8,128)(2,1)S(1)}, bf16[2,128,128]{2,1,0:T(8,128)(2,1)}, u32[]{:S(2)}) copy-start(bf16[2,128,128]{2,1,0:T(8,128)(2,1)} %constant.18.clone.gather_ref) | copy-start | bytes 196612
  33.6 20.2 %copy-start.5 = (bf16[128,64]{1,0:T(8,128)(2,1)S(1)}, bf16[128,64]{1,0:T(8,128)(2,1)}, u32[]{:S(2)}) copy-start(bf16[128,64]{1,0:T(8,128)(2,1)} %constant.17.clone.ia_ref) | copy-start | bytes 49156
  33.6 20.2 %copy-start.7 = (bf16[64,128]{1,0:T(8,128)(2,1)S(1)}, bf16[64,128]{1,0:T(8,128)(2,1)}, u32[]{:S(2)}) copy-start(bf16[64,128]{1,0:T(8,128)(2,1)} %constant.15.clone.fo_ref) | copy-start | bytes 49156
  53.8 24.5 %copy-start = (f32[160,128]{1,0:T(8,128)S(1)}, f32[160,128]{1,0:T(8,128)}, u32[]{:S(2)}) copy-start(f32[160,128]{1,0:T(8,128)} %constant.20.clone.phase_hbm.phase_ref) | copy-start | bytes 245764
  68.5 22.2 %all-to-all-start.4 = ((bf16[16,8,1152]{2,1,0:T(8,128)(2,1)}), bf16[16,8,1152]{2,1,0:T(8,128)(2,1)S(1)}, u32[]{:S(2)}, u32[]{:S(2)}) async-start(bf16[16,8,1152]{2,1,0:T(8,128)(2,1)} %bitcast.12), calls=%async_computation.4 | async-start | bytes 589824 | tf_op jit(solution)/shard_map/all_to_all | solution.py:572
  78.4 12.3 %copy-start.4 = (bf16[6,32,128]{2,1,0:T(8,128)(2,1)S(1)}, bf16[6,32,128]{2,1,0:T(8,128)(2,1)}, u32[]{:S(2)}) copy-start(bf16[6,32,128]{2,1,0:T(8,128)(2,1)} %constant.19.clone.pick_ref) | copy-start | bytes 147460

commit v7 on v6

--- a/solution.py
+++ b/solution.py
@@ -269,7 +269,8 @@
         add(n + 1, tb_ref)
         return make(n + 2, *carry, ta_ref)
 
-    ca, sa = lax.fori_loop(0, STEPS // 2 - 1, step, (ca, sa))
+    for m in range(STEPS // 2 - 1):
+        ca, sa = step(m, (ca, sa))
     planes(f_hbm, f_ref, f_sem, STEPS - 2).wait()
     planes(f_hbm, f_ref, f_sem, STEPS - 1).wait()
     add(STEPS - 2, ta_ref)
@@ -291,9 +292,9 @@
     sign = jnp.where(lane < 64, -1.0, 1.0)
     keep = (lane >> 6) == ((row >> 1) & 1)
 
-    def step(u, carry):
-        cols = pl.ds(pl.multiple_of(u * 128, 128), 128)
-        pair = pl.ds(2 * u, 2)
+    def step(u):
+        cols = slice(u * 128, u * 128 + 128)
+        pair = slice(2 * u, 2 * u + 2)
         for t in range(8):
             left = mask_ref[8 * t : 8 * t + 8, cols].astype(BF16)
             right = jnp.concatenate(
@@ -307,9 +308,9 @@
             below = pltpu.roll(turned, 1, 0)
             v = jnp.where(even, res + sign * above, below - sign * res)
             v_ref[8 * t : 8 * t + 8, cols] = jnp.where(keep, v, 0.0)
-        return carry
-
-    lax.fori_loop(0, L // 2, step, 0)
+
+    for u in range(L // 2):
+        step(u)
     out_ref[...] = mm(iv_ref[...], v_ref[...].astype(BF16)).astype(BF16)
 
 
@@ -434,9 +435,9 @@
     top = row < 4
     keep = (lane >> 6) == ((row >> 1) & 1)
 
-    def step(u, carry):
-        cols = pl.ds(pl.multiple_of(u * 128, 128), 128)
-        pair = pl.ds(2 * u, 2)
+    def step(u):
+        cols = slice(u * 128, u * 128 + 128)
+        pair = slice(2 * u, 2 * u + 2)
         for t in range(8):
             right = jnp.concatenate(
                 [w_ref[2 * t, pair].reshape(128, 128), w_ref[2 * t + 1, pair].reshape(128, 128)],
@@ -445,9 +446,9 @@
             o = nt(left_ref[8 * t : 8 * t + 8, cols], right)
             res = jnp.where(top, o[:, :128], o[:, 128:])
             v_ref[8 * t : 8 * t + 8, cols] = jnp.where(keep, res, 0.0)
-        return carry
-
-    lax.fori_loop(0, L // 2, step, 0)
+
+    for u in range(L // 2):
+        step(u)
     out_ref[:, :1024] = mm(ia_ref[...], v_ref[...].astype(BF16)).astype(BF16)
 
 

time: 92.9 us -> 89.7 us (0.966)
  Pallas kernels: 27.1 us -> 23.9 us
    pallas_call x7, Pallas kernels: 27.1 us -> 23.9 us  [call(): pl.pallas_call(kernel, in_specs=[place(n, big) for n in range(len(args))]...]
where the time goes in v7:
time: 89.7 us; the launch traced here: 89.1 us
  blocking collectives  46.8 us (52%)
  Pallas kernels  23.9 us (27%)
  starting transfers between devices  9.87 us (11%)
  waiting for transfers between devices  7.78 us (9%)
    all_to_all x4, blocking collectives, exchange(): lax.all_to_all(v.reshape(S, 8, width), axis, split_axis=0, concat_axis=0,...  46.8 us
    pallas_call x7, Pallas kernels, call(): pl.pallas_call(kernel, in_specs=[place(n, big) for n in range(len(args))]...  23.9 us
    all_to_all x1, starting transfers between devices, exchange(): lax.all_to_all(v.reshape(S, 8, width), axis, split_axis=0, concat_axis=0,...  9.87 us
    all_to_all x1, waiting for transfers between devices, exchange(): lax.all_to_all(v.reshape(S, 8, width), axis, split_axis=0, concat_axis=0,...  7.78 us
  transfers between devices with their start and end apart: 1, of which 1 were waited for; matrix products, arithmetic and copies ran while one was open for 0% of the time, Pallas kernels for 5%

profile of v7, /device:TPU:1, one launch (start us, length us, event | category | flops | bytes accessed | tf_op | source)
XLA Modules:
  0.0 89.1 jit_solution(7701447100606661502)
XLA Ops:
  0.6 0.0 copy-start.3
  0.6 0.0 copy-start.6
  0.7 4.9 %spectra.1 = (bf16[128,1024]{1,0:T(8,128)(2,1)S(1)}, bf16[784,4096]{1,0:T(8,128)(2,1)S(1)}, bf16[16,16,64,128]{3,2,1,0:T(8,128)(2,1)S(1)}) custom-call(bf16[64,4,4096]{2,1,0:T(4,128)(2,1)} %bitcast.27, f32[160,128]{1,0:T(8,128)} %constant.20.clone.phase_hbm.phase_ref, bf16[16,16,64,128]{3,2,1,0:T(8,128)(2,1)} %w_hbm.1), custom_call_target="tpu_custom_call" | custom-call | tf_op jit(solution)/shard_map/spectra/pallas_call | solution.py:551
  5.5 14.3 %all_to_all.25 = bf16[16,8,1024]{2,1,0:T(8,128)(2,1)S(1)} all-to-all(bf16[16,8,1024]{2,1,0:T(8,128)(2,1)S(1)} %bitcast.25), channel_id=1, replica_groups=mesh['dp'=16,'slab'=16] {'slab'}, dimensions={0} | all-to-all | bytes 524288 | tf_op jit(solution)/shard_map/all_to_all | solution.py:573
  19.8 0.0 copy-done.3
  19.8 0.0 copy-done.6
  19.9 1.0 %mix.1 = (bf16[128,1024]{1,0:T(8,128)(2,1)S(1)}, bf16[64,1024]{1,0:T(8,128)(2,1)S(1)}) custom-call(bf16[128,1024]{1,0:T(8,128)(2,1)S(1)} %bitcast.21, bf16[16,16,64,128]{3,2,1,0:T(8,128)(2,1)S(1)} %get-tuple-element.17.w_ref, bf16[64,128]{1,0:T(8,128)(2,1)S(1)} %copy-done.3, bf16[128,64]{1,0:T(8,128)(2,1)S(1)} %copy-done.6), custom_call_target="tpu_custom_call" | custom-call | tf_op jit(solution)/shard_map/mix/pallas_call | solution.py:551
  20.9 10.6 %all_to_all.26 = bf16[16,8,1024]{2,1,0:T(8,128)(2,1)S(1)} all-to-all(bf16[16,8,1024]{2,1,0:T(8,128)(2,1)S(1)} %bitcast.24), channel_id=1, replica_groups=mesh['dp'=16,'slab'=16] {'slab'}, dimensions={0} | all-to-all | bytes 524288 | tf_op jit(solution)/shard_map/all_to_all | solution.py:573
  31.5 0.0 copy-done.2
  31.5 0.0 copy-done.8
  31.5 0.0 copy-start.7
  31.5 9.3 %delta.1 = (bf16[128,1152]{1,0:T(8,128)(2,1)S(1)}, bf16[256,4096]{1,0:T(8,128)(2,1)}) custom-call(bf16[128,1024]{1,0:T(8,128)(2,1)S(1)} %bitcast.20, bf16[784,4096]{1,0:T(8,128)(2,1)S(1)} %get-tuple-element.19.tf_ref, bf16[64,4,4096]{2,1,0:T(4,128)(2,1)} %bitcast.28, bf16[64,64]{1,0:T(8,128)(2,1)S(1)} %copy-done.2, f32[1,64]{1,0:T(1,128)S(1)} %bitcast.26), custom_call_target="tpu_custom_call" | custom-call | tf_op jit(solution)/shard_map/delta/pallas_call | solution.py:551
  40.8 10.9 %all_to_all.27 = bf16[16,8,1152]{2,1,0:T(8,128)(2,1)S(1)} all-to-all(bf16[16,8,1152]{2,1,0:T(8,128)(2,1)S(1)} %bitcast.23), channel_id=1, replica_groups=mesh['dp'=16,'slab'=16] {'slab'}, dimensions={0} | all-to-all | bytes 589824 | tf_op jit(solution)/shard_map/all_to_all | solution.py:573
  51.7 0.0 copy-done.5
  51.7 0.0 copy-start
  51.7 1.6 %adjoint.1 = (bf16[128,1152]{1,0:T(8,128)(2,1)S(1)}, bf16[128,512]{1,0:T(8,128)(2,1)S(1)}) custom-call(bf16[128,1152]{1,0:T(8,128)(2,1)S(1)} %bitcast.18, bf16[64,1024]{1,0:T(8,128)(2,1)S(1)} %get-tuple-element.21.m_ref, bf16[16,16,64,128]{3,2,1,0:T(8,128)(2,1)S(1)} %get-tuple-element.17.w_ref, bf16[64,128]{1,0:T(8,128)(2,1)S(1)} %copy-done.3, ...), custom_call_target="tpu_custom_call" | custom-call | tf_op jit(solution)/shard_map/adjoint/pallas_call | solution.py:551
  53.4 11.0 %all_to_all.28 = bf16[16,8,1152]{2,1,0:T(8,128)(2,1)S(1)} all-to-all(bf16[16,8,1152]{2,1,0:T(8,128)(2,1)S(1)} %bitcast.22), channel_id=1, replica_groups=mesh['dp'=16,'slab'=16] {'slab'}, dimensions={0} | all-to-all | bytes 589824 | tf_op jit(solution)/shard_map/all_to_all | solution.py:573
  64.3 0.9 %assemble.1 = bf16[128,1152]{1,0:T(8,128)(2,1)} custom-call(bf16[128,1152]{1,0:T(8,128)(2,1)S(1)} %bitcast.16, bf16[128,512]{1,0:T(8,128)(2,1)S(1)} %get-tuple-element.24.part_ref), custom_call_target="tpu_custom_call" | custom-call | tf_op jit(solution)/shard_map/assemble/pallas_call | solution.py:551
  65.3 9.9 %all-to-all-start.4 = ((bf16[16,8,1152]{2,1,0:T(8,128)(2,1)}), bf16[16,8,1152]{2,1,0:T(8,128)(2,1)S(1)}, u32[]{:S(2)}, u32[]{:S(2)}) async-start(bf16[16,8,1152]{2,1,0:T(8,128)(2,1)} %bitcast.12), calls=%async_computation.4 | async-start | bytes 589824 | tf_op jit(solution)/shard_map/all_to_all | solution.py:573
  75.1 0.0 copy-done
  75.2 0.0 copy-start.4
  75.2 4.5 %input_grad.1 = bf16[64,4,4096]{2,1,0:T(4,128)(2,1)} custom-call(bf16[128,1152]{1,0:T(8,128)(2,1)S(1)} %bitcast.17, bf16[256,4096]{1,0:T(8,128)(2,1)} %get-tuple-element.23.d_hbm, bf16[64,64]{1,0:T(8,128)(2,1)S(1)} %copy-done.2, f32[160,128]{1,0:T(8,128)S(1)} %copy-done), custom_call_target="tpu_custom_call" | custom-call | tf_op jit(solution)/shard_map/input_grad/pallas_call | solution.py:551
  79.7 7.8 %all-to-all-done.4 = bf16[16,8,1152]{2,1,0:T(8,128)(2,1)S(1)} async-done(((bf16[16,8,1152]{2,1,0:T(8,128)(2,1)}), bf16[16,8,1152]{2,1,0:T(8,128)(2,1)S(1)}, u32[]{:S(2)}, u32[]{:S(2)}) %all-to-all-start.4) | async-done | bytes 294944 | tf_op jit(solution)/shard_map/all_to_all | solution.py:573
  87.5 1.6 %weight_grad.1 = (f32[16,64,128]{2,1,0:T(8,128)}, f32[64,64]{1,0:T(8,128)}, f32[1,64]{1,0:T(1,128)}) custom-call(bf16[128,1152]{1,0:T(8,128)(2,1)S(1)} %bitcast.19, bf16[6,32,128]{2,1,0:T(8,128)(2,1)S(1)} %copy-done.4), custom_call_target="tpu_custom_call" | custom-call | tf_op jit(solution)/shard_map/weight_grad/pallas_call | solution.py:551
  (7 shorter events, 0.0 us)
Async XLA Ops:
  0.6 19.2 %copy-start.3 = (bf16[64,128]{1,0:T(8,128)(2,1)S(1)}, bf16[64,128]{1,0:T(8,128)(2,1)}, u32[]{:S(2)}) copy-start(bf16[64,128]{1,0:T(8,128)(2,1)} %constant.14.clone.fx_ref) | copy-start | bytes 49156
  0.6 19.2 %copy-start.6 = (bf16[128,64]{1,0:T(8,128)(2,1)S(1)}, bf16[128,64]{1,0:T(8,128)(2,1)}, u32[]{:S(2)}) copy-start(bf16[128,64]{1,0:T(8,128)(2,1)} %constant.16.clone.iv_ref) | copy-start | bytes 49156
  19.9 11.6 %copy-start.2 = (bf16[64,64]{1,0:T(8,128)(2,1)S(1)}, bf16[64,64]{1,0:T(8,128)(2,1)}, u32[]{:S(2)}) copy-start(bf16[64,64]{1,0:T(8,128)(2,1)} %w_ref.3) | copy-start | bytes 24580
  19.9 11.6 %copy-start.8 = (f32[64]{0:T(128)S(1)}, f32[64]{0:T(128)}, u32[]{:S(2)}) copy-start(f32[64]{0:T(128)} %param.16) | copy-start | bytes 772
  31.5 20.2 %copy-start.1 = (bf16[2,128,128]{2,1,0:T(8,128)(2,1)S(1)}, bf16[2,128,128]{2,1,0:T(8,128)(2,1)}, u32[]{:S(2)}) copy-start(bf16[2,128,128]{2,1,0:T(8,128)(2,1)} %constant.18.clone.gather_ref) | copy-start | bytes 196612
  31.5 20.2 %copy-start.5 = (bf16[128,64]{1,0:T(8,128)(2,1)S(1)}, bf16[128,64]{1,0:T(8,128)(2,1)}, u32[]{:S(2)}) copy-start(bf16[128,64]{1,0:T(8,128)(2,1)} %constant.17.clone.ia_ref) | copy-start | bytes 49156
  31.5 20.2 %copy-start.7 = (bf16[64,128]{1,0:T(8,128)(2,1)S(1)}, bf16[64,128]{1,0:T(8,128)(2,1)}, u32[]{:S(2)}) copy-start(bf16[64,128]{1,0:T(8,128)(2,1)} %constant.15.clone.fo_ref) | copy-start | bytes 49156
  51.7 23.4 %copy-start = (f32[160,128]{1,0:T(8,128)S(1)}, f32[160,128]{1,0:T(8,128)}, u32[]{:S(2)}) copy-start(f32[160,128]{1,0:T(8,128)} %constant.20.clone.phase_hbm.phase_ref) | copy-start | bytes 245764
  65.3 22.2 %all-to-all-start.4 = ((bf16[16,8,1152]{2,1,0:T(8,128)(2,1)}), bf16[16,8,1152]{2,1,0:T(8,128)(2,1)S(1)}, u32[]{:S(2)}, u32[]{:S(2)}) async-start(bf16[16,8,1152]{2,1,0:T(8,128)(2,1)} %bitcast.12), calls=%async_computation.4 | async-start | bytes 589824 | tf_op jit(solution)/shard_map/all_to_all | solution.py:573
  75.2 12.3 %copy-start.4 = (bf16[6,32,128]{2,1,0:T(8,128)(2,1)S(1)}, bf16[6,32,128]{2,1,0:T(8,128)(2,1)}, u32[]{:S(2)}) copy-start(bf16[6,32,128]{2,1,0:T(8,128)(2,1)} %constant.19.clone.pick_ref) | copy-start | bytes 147460

commit v8 on v7

--- a/solution.py
+++ b/solution.py
@@ -342,11 +342,10 @@
     e = (subl((ROWS, C)) // XL == lanes((ROWS, C))).astype(F32)
     shift_ref[...] = EXACT(e, jnp.broadcast_to(bias_ref[...], (128, C)), NT)
     sg_ref[...] = jnp.zeros_like(sg_ref)
-    db_ref[...] = jnp.zeros_like(db_ref)
 
     def before(n, p_ref, halves=(0, 1)):
         for h in halves:
-            cols = pl.ds(pl.multiple_of(n * CHUNK + h * 256, 256), 256)
+            cols = slice(n * CHUNK + h * 256, n * CHUNK + h * 256 + 256)
             p_ref[:, h * 256 : h * 256 + 256] = mm(bl_ref[...], tf_ref[: Q + ROWS, cols])
 
     def add(n, own_ref, first, last):
@@ -361,31 +360,23 @@
             own_ref[rows, :] = d
             d_ref[rows, at(n)] = d
 
-    def weave(n, p_ref, next_ref, own_ref, past_ref):
-        past, later = jnp.maximum(n - 1, 0), jnp.minimum(n + 1, STEPS - 1)
-        add(past, past_ref, 0, 256)
-        bend(n, p_ref, own_ref, range(0, 3))
-        add(past, past_ref, 256, 512)
-        bend(n, p_ref, own_ref, range(3, 6))
-        add(past, past_ref, 512, 784)
-        bend(n, p_ref, own_ref, range(6, 9))
-        before(later, next_ref, (0,))
-        bend(n, p_ref, own_ref, range(9, 12))
-        before(later, next_ref, (1,))
-        bend(n, p_ref, own_ref, range(12, 16))
+    before(0, pa_ref)
+    bufs = ((pa_ref, pb_ref, da_ref, db_ref), (pb_ref, pa_ref, db_ref, da_ref))
+    for n in range(STEPS):
+        p_ref, next_ref, own_ref, past_ref = bufs[n % 2]
+        if n % 2 == 0:
+            planes(ct_hbm, ct_ref, ct_sem, n).wait()
+            planes(ct_hbm, ct_ref, ct_sem, n + 1).wait()
+        ends = (0, 256, 512, 784)
+        for q in range(3):
+            if n > 0:
+                add(n - 1, past_ref, ends[q], ends[q + 1])
+            bend(n, p_ref, own_ref, range(3 * q, 3 * q + 3))
+        for h in range(2):
+            if n < STEPS - 1:
+                before(n + 1, next_ref, (h,))
+            bend(n, p_ref, own_ref, range(9 + 3 * h, 12 + 4 * h))
         columns(d_ref, d_hbm, d_sem, n).start()
-
-    before(0, pa_ref)
-
-    def step(m, carry):
-        n = 2 * m
-        planes(ct_hbm, ct_ref, ct_sem, n).wait()
-        planes(ct_hbm, ct_ref, ct_sem, n + 1).wait()
-        weave(n, pa_ref, pb_ref, da_ref, db_ref)
-        weave(n + 1, pb_ref, pa_ref, db_ref, da_ref)
-        return carry
-
-    lax.fori_loop(0, STEPS // 2, step, 0)
     add(STEPS - 1, db_ref, 0, 784)
     doubled = jnp.where(subl((Q, ROWS)) < 32, 1.0, 2.0)
     pack_spectra(sg_ref[:Q, :] * doubled, lane_order(), z_ref, out_ref)

time: 89.7 us -> 89.8 us (level)
  no operation moved by 1% of the time
where the time goes in v8:
time: 89.8 us; the launch traced here: 89.2 us
  blocking collectives  47 us (52%)
  Pallas kernels  23.6 us (26%)
  starting transfers between devices  9.85 us (11%)
  waiting for transfers between devices  7.78 us (9%)
  between operations  0.91 us (1%)
    all_to_all x4, blocking collectives, exchange(): lax.all_to_all(v.reshape(S, 8, width), axis, split_axis=0, concat_axis=0,...  47 us
    pallas_call x7, Pallas kernels, call(): pl.pallas_call(kernel, in_specs=[place(n, big) for n in range(len(args))]...  23.6 us
    all_to_all x1, starting transfers between devices, exchange(): lax.all_to_all(v.reshape(S, 8, width), axis, split_axis=0, concat_axis=0,...  9.85 us
    all_to_all x1, waiting for transfers between devices, exchange(): lax.all_to_all(v.reshape(S, 8, width), axis, split_axis=0, concat_axis=0,...  7.78 us
  transfers between devices with their start and end apart: 1, of which 1 were waited for; matrix products, arithmetic and copies ran while one was open for 0% of the time, Pallas kernels for 5%

profile of v8, /device:TPU:1, one launch (start us, length us, event | category | flops | bytes accessed | tf_op | source)
XLA Modules:
  0.0 89.2 jit_solution(6691152798395614028)
XLA Ops:
  0.6 0.0 copy-start.3
  0.6 0.0 copy-start.6
  0.7 4.9 %spectra.1 = (bf16[128,1024]{1,0:T(8,128)(2,1)S(1)}, bf16[784,4096]{1,0:T(8,128)(2,1)S(1)}, bf16[16,16,64,128]{3,2,1,0:T(8,128)(2,1)S(1)}) custom-call(bf16[64,4,4096]{2,1,0:T(4,128)(2,1)} %bitcast.27, f32[160,128]{1,0:T(8,128)} %constant.20.clone.phase_hbm.phase_ref, bf16[16,16,64,128]{3,2,1,0:T(8,128)(2,1)} %w_hbm.1), custom_call_target="tpu_custom_call" | custom-call | tf_op jit(solution)/shard_map/spectra/pallas_call | solution.py:542
  5.5 14.3 %all_to_all.25 = bf16[16,8,1024]{2,1,0:T(8,128)(2,1)S(1)} all-to-all(bf16[16,8,1024]{2,1,0:T(8,128)(2,1)S(1)} %bitcast.25), channel_id=1, replica_groups=mesh['dp'=16,'slab'=16] {'slab'}, dimensions={0} | all-to-all | bytes 524288 | tf_op jit(solution)/shard_map/all_to_all | solution.py:564
  19.8 0.0 copy-done.3
  19.9 0.0 copy-done.6
  19.9 1.0 %mix.1 = (bf16[128,1024]{1,0:T(8,128)(2,1)S(1)}, bf16[64,1024]{1,0:T(8,128)(2,1)S(1)}) custom-call(bf16[128,1024]{1,0:T(8,128)(2,1)S(1)} %bitcast.21, bf16[16,16,64,128]{3,2,1,0:T(8,128)(2,1)S(1)} %get-tuple-element.17.w_ref, bf16[64,128]{1,0:T(8,128)(2,1)S(1)} %copy-done.3, bf16[128,64]{1,0:T(8,128)(2,1)S(1)} %copy-done.6), custom_call_target="tpu_custom_call" | custom-call | tf_op jit(solution)/shard_map/mix/pallas_call | solution.py:542
  20.9 10.6 %all_to_all.26 = bf16[16,8,1024]{2,1,0:T(8,128)(2,1)S(1)} all-to-all(bf16[16,8,1024]{2,1,0:T(8,128)(2,1)S(1)} %bitcast.24), channel_id=1, replica_groups=mesh['dp'=16,'slab'=16] {'slab'}, dimensions={0} | all-to-all | bytes 524288 | tf_op jit(solution)/shard_map/all_to_all | solution.py:564
  31.5 0.0 copy-done.2
  31.5 0.0 copy-done.8
  31.5 0.0 copy-start.7
  31.5 9.0 %delta.1 = (bf16[128,1152]{1,0:T(8,128)(2,1)S(1)}, bf16[256,4096]{1,0:T(8,128)(2,1)}) custom-call(bf16[128,1024]{1,0:T(8,128)(2,1)S(1)} %bitcast.20, bf16[784,4096]{1,0:T(8,128)(2,1)S(1)} %get-tuple-element.19.tf_ref, bf16[64,4,4096]{2,1,0:T(4,128)(2,1)} %bitcast.28, bf16[64,64]{1,0:T(8,128)(2,1)S(1)} %copy-done.2, f32[1,64]{1,0:T(1,128)S(1)} %bitcast.26), custom_call_target="tpu_custom_call" | custom-call | tf_op jit(solution)/shard_map/delta/pallas_call | solution.py:542
  40.5 11.1 %all_to_all.27 = bf16[16,8,1152]{2,1,0:T(8,128)(2,1)S(1)} all-to-all(bf16[16,8,1152]{2,1,0:T(8,128)(2,1)S(1)} %bitcast.23), channel_id=1, replica_groups=mesh['dp'=16,'slab'=16] {'slab'}, dimensions={0} | all-to-all | bytes 589824 | tf_op jit(solution)/shard_map/all_to_all | solution.py:564
  51.6 0.0 copy-done.1
  51.6 0.0 copy-done.5
  51.6 0.0 copy-start
  51.6 1.6 %adjoint.1 = (bf16[128,1152]{1,0:T(8,128)(2,1)S(1)}, bf16[128,512]{1,0:T(8,128)(2,1)S(1)}) custom-call(bf16[128,1152]{1,0:T(8,128)(2,1)S(1)} %bitcast.18, bf16[64,1024]{1,0:T(8,128)(2,1)S(1)} %get-tuple-element.21.m_ref, bf16[16,16,64,128]{3,2,1,0:T(8,128)(2,1)S(1)} %get-tuple-element.17.w_ref, bf16[64,128]{1,0:T(8,128)(2,1)S(1)} %copy-done.3, ...), custom_call_target="tpu_custom_call" | custom-call | tf_op jit(solution)/shard_map/adjoint/pallas_call | solution.py:542
  53.3 11.0 %all_to_all.28 = bf16[16,8,1152]{2,1,0:T(8,128)(2,1)S(1)} all-to-all(bf16[16,8,1152]{2,1,0:T(8,128)(2,1)S(1)} %bitcast.22), channel_id=1, replica_groups=mesh['dp'=16,'slab'=16] {'slab'}, dimensions={0} | all-to-all | bytes 589824 | tf_op jit(solution)/shard_map/all_to_all | solution.py:564
  64.2 0.9 %assemble.1 = bf16[128,1152]{1,0:T(8,128)(2,1)} custom-call(bf16[128,1152]{1,0:T(8,128)(2,1)S(1)} %bitcast.16, bf16[128,512]{1,0:T(8,128)(2,1)S(1)} %get-tuple-element.24.part_ref), custom_call_target="tpu_custom_call" | custom-call | tf_op jit(solution)/shard_map/assemble/pallas_call | solution.py:542
  65.2 9.8 %all-to-all-start.4 = ((bf16[16,8,1152]{2,1,0:T(8,128)(2,1)}), bf16[16,8,1152]{2,1,0:T(8,128)(2,1)S(1)}, u32[]{:S(2)}, u32[]{:S(2)}) async-start(bf16[16,8,1152]{2,1,0:T(8,128)(2,1)} %bitcast.12), calls=%async_computation.4 | async-start | bytes 589824 | tf_op jit(solution)/shard_map/all_to_all | solution.py:564
  75.0 0.0 copy-start.4
  75.1 4.5 %input_grad.1 = bf16[64,4,4096]{2,1,0:T(4,128)(2,1)} custom-call(bf16[128,1152]{1,0:T(8,128)(2,1)S(1)} %bitcast.17, bf16[256,4096]{1,0:T(8,128)(2,1)} %get-tuple-element.23.d_hbm, bf16[64,64]{1,0:T(8,128)(2,1)S(1)} %copy-done.2, f32[160,128]{1,0:T(8,128)S(1)} %copy-done), custom_call_target="tpu_custom_call" | custom-call | tf_op jit(solution)/shard_map/input_grad/pallas_call | solution.py:542
  79.6 7.8 %all-to-all-done.4 = bf16[16,8,1152]{2,1,0:T(8,128)(2,1)S(1)} async-done(((bf16[16,8,1152]{2,1,0:T(8,128)(2,1)}), bf16[16,8,1152]{2,1,0:T(8,128)(2,1)S(1)}, u32[]{:S(2)}, u32[]{:S(2)}) %all-to-all-start.4) | async-done | bytes 294944 | tf_op jit(solution)/shard_map/all_to_all | solution.py:564
  87.4 1.6 %weight_grad.1 = (f32[16,64,128]{2,1,0:T(8,128)}, f32[64,64]{1,0:T(8,128)}, f32[1,64]{1,0:T(1,128)}) custom-call(bf16[128,1152]{1,0:T(8,128)(2,1)S(1)} %bitcast.19, bf16[6,32,128]{2,1,0:T(8,128)(2,1)S(1)} %copy-done.4), custom_call_target="tpu_custom_call" | custom-call | tf_op jit(solution)/shard_map/weight_grad/pallas_call | solution.py:542
  (7 shorter events, 0.0 us)
Async XLA Ops:
  0.6 19.2 %copy-start.3 = (bf16[64,128]{1,0:T(8,128)(2,1)S(1)}, bf16[64,128]{1,0:T(8,128)(2,1)}, u32[]{:S(2)}) copy-start(bf16[64,128]{1,0:T(8,128)(2,1)} %constant.14.clone.fx_ref) | copy-start | bytes 49156
  0.6 19.2 %copy-start.6 = (bf16[128,64]{1,0:T(8,128)(2,1)S(1)}, bf16[128,64]{1,0:T(8,128)(2,1)}, u32[]{:S(2)}) copy-start(bf16[128,64]{1,0:T(8,128)(2,1)} %constant.16.clone.iv_ref) | copy-start | bytes 49156
  19.9 11.6 %copy-start.2 = (bf16[64,64]{1,0:T(8,128)(2,1)S(1)}, bf16[64,64]{1,0:T(8,128)(2,1)}, u32[]{:S(2)}) copy-start(bf16[64,64]{1,0:T(8,128)(2,1)} %w_ref.3) | copy-start | bytes 24580
  19.9 11.6 %copy-start.8 = (f32[64]{0:T(128)S(1)}, f32[64]{0:T(128)}, u32[]{:S(2)}) copy-start(f32[64]{0:T(128)} %param.16) | copy-start | bytes 772
  31.5 20.1 %copy-start.1 = (bf16[2,128,128]{2,1,0:T(8,128)(2,1)S(1)}, bf16[2,128,128]{2,1,0:T(8,128)(2,1)}, u32[]{:S(2)}) copy-start(bf16[2,128,128]{2,1,0:T(8,128)(2,1)} %constant.18.clone.gather_ref) | copy-start | bytes 196612
  31.5 20.1 %copy-start.5 = (bf16[128,64]{1,0:T(8,128)(2,1)S(1)}, bf16[128,64]{1,0:T(8,128)(2,1)}, u32[]{:S(2)}) copy-start(bf16[128,64]{1,0:T(8,128)(2,1)} %constant.17.clone.ia_ref) | copy-start | bytes 49156
  31.5 20.1 %copy-start.7 = (bf16[64,128]{1,0:T(8,128)(2,1)S(1)}, bf16[64,128]{1,0:T(8,128)(2,1)}, u32[]{:S(2)}) copy-start(bf16[64,128]{1,0:T(8,128)(2,1)} %constant.15.clone.fo_ref) | copy-start | bytes 49156
  51.6 23.4 %copy-start = (f32[160,128]{1,0:T(8,128)S(1)}, f32[160,128]{1,0:T(8,128)}, u32[]{:S(2)}) copy-start(f32[160,128]{1,0:T(8,128)} %constant.20.clone.phase_hbm.phase_ref) | copy-start | bytes 245764
  65.2 22.2 %all-to-all-start.4 = ((bf16[16,8,1152]{2,1,0:T(8,128)(2,1)}), bf16[16,8,1152]{2,1,0:T(8,128)(2,1)S(1)}, u32[]{:S(2)}, u32[]{:S(2)}) async-start(bf16[16,8,1152]{2,1,0:T(8,128)(2,1)} %bitcast.12), calls=%async_computation.4 | async-start | bytes 589824 | tf_op jit(solution)/shard_map/all_to_all | solution.py:564
  75.0 12.3 %copy-start.4 = (bf16[6,32,128]{2,1,0:T(8,128)(2,1)S(1)}, bf16[6,32,128]{2,1,0:T(8,128)(2,1)}, u32[]{:S(2)}) copy-start(bf16[6,32,128]{2,1,0:T(8,128)(2,1)} %constant.19.clone.pick_ref) | copy-start | bytes 147460

commit v9 on v8

--- a/solution.py
+++ b/solution.py
@@ -367,15 +367,15 @@
         if n % 2 == 0:
             planes(ct_hbm, ct_ref, ct_sem, n).wait()
             planes(ct_hbm, ct_ref, ct_sem, n + 1).wait()
-        ends = (0, 256, 512, 784)
-        for q in range(3):
+        ends = (0, 400, 784)
+        for q in range(2):
             if n > 0:
                 add(n - 1, past_ref, ends[q], ends[q + 1])
-            bend(n, p_ref, own_ref, range(3 * q, 3 * q + 3))
+            bend(n, p_ref, own_ref, range(4 * q, 4 * q + 4))
         for h in range(2):
             if n < STEPS - 1:
                 before(n + 1, next_ref, (h,))
-            bend(n, p_ref, own_ref, range(9 + 3 * h, 12 + 4 * h))
+            bend(n, p_ref, own_ref, range(8 + 4 * h, 12 + 4 * h))
         columns(d_ref, d_hbm, d_sem, n).start()
     add(STEPS - 1, db_ref, 0, 784)
     doubled = jnp.where(subl((Q, ROWS)) < 32, 1.0, 2.0)

time: 89.8 us -> 89.4 us (level)
  no operation moved by 1% of the time
where the time goes in v9:
time: 89.4 us; the launch traced here: 88.8 us
  blocking collectives  46.8 us (52%)
  Pallas kernels  23.5 us (26%)
  starting transfers between devices  9.85 us (11%)
  waiting for transfers between devices  7.78 us (9%)
  between operations  0.91 us (1%)
    all_to_all x4, blocking collectives, exchange(): lax.all_to_all(v.reshape(S, 8, width), axis, split_axis=0, concat_axis=0,...  46.8 us
    pallas_call x7, Pallas kernels, call(): pl.pallas_call(kernel, in_specs=[place(n, big) for n in range(len(args))]...  23.5 us
    all_to_all x1, starting transfers between devices, exchange(): lax.all_to_all(v.reshape(S, 8, width), axis, split_axis=0, concat_axis=0,...  9.85 us
    all_to_all x1, waiting for transfers between devices, exchange(): lax.all_to_all(v.reshape(S, 8, width), axis, split_axis=0, concat_axis=0,...  7.78 us
  transfers between devices with their start and end apart: 1, of which 1 were waited for; matrix products, arithmetic and copies ran while one was open for 0% of the time, Pallas kernels for 5%

profile of v9, /device:TPU:1, one launch (start us, length us, event | category | flops | bytes accessed | tf_op | source)
XLA Modules:
  0.0 88.8 jit_solution(4528971634537405519)
XLA Ops:
  0.6 0.0 copy-start.3
  0.6 0.0 copy-start.6
  0.7 4.9 %spectra.1 = (bf16[128,1024]{1,0:T(8,128)(2,1)S(1)}, bf16[784,4096]{1,0:T(8,128)(2,1)S(1)}, bf16[16,16,64,128]{3,2,1,0:T(8,128)(2,1)S(1)}) custom-call(bf16[64,4,4096]{2,1,0:T(4,128)(2,1)} %bitcast.27, f32[160,128]{1,0:T(8,128)} %constant.20.clone.phase_hbm.phase_ref, bf16[16,16,64,128]{3,2,1,0:T(8,128)(2,1)} %w_hbm.1), custom_call_target="tpu_custom_call" | custom-call | tf_op jit(solution)/shard_map/spectra/pallas_call | solution.py:542
  5.5 14.3 %all_to_all.25 = bf16[16,8,1024]{2,1,0:T(8,128)(2,1)S(1)} all-to-all(bf16[16,8,1024]{2,1,0:T(8,128)(2,1)S(1)} %bitcast.25), channel_id=1, replica_groups=mesh['dp'=16,'slab'=16] {'slab'}, dimensions={0} | all-to-all | bytes 524288 | tf_op jit(solution)/shard_map/all_to_all | solution.py:564
  19.8 0.0 copy-done.3
  19.9 0.0 copy-done.6
  19.9 1.0 %mix.1 = (bf16[128,1024]{1,0:T(8,128)(2,1)S(1)}, bf16[64,1024]{1,0:T(8,128)(2,1)S(1)}) custom-call(bf16[128,1024]{1,0:T(8,128)(2,1)S(1)} %bitcast.21, bf16[16,16,64,128]{3,2,1,0:T(8,128)(2,1)S(1)} %get-tuple-element.17.w_ref, bf16[64,128]{1,0:T(8,128)(2,1)S(1)} %copy-done.3, bf16[128,64]{1,0:T(8,128)(2,1)S(1)} %copy-done.6), custom_call_target="tpu_custom_call" | custom-call | tf_op jit(solution)/shard_map/mix/pallas_call | solution.py:542
  20.9 10.6 %all_to_all.26 = bf16[16,8,1024]{2,1,0:T(8,128)(2,1)S(1)} all-to-all(bf16[16,8,1024]{2,1,0:T(8,128)(2,1)S(1)} %bitcast.24), channel_id=1, replica_groups=mesh['dp'=16,'slab'=16] {'slab'}, dimensions={0} | all-to-all | bytes 524288 | tf_op jit(solution)/shard_map/all_to_all | solution.py:564
  31.5 0.0 copy-done.2
  31.5 0.0 copy-done.8
  31.5 0.0 copy-start.7
  31.5 8.8 %delta.1 = (bf16[128,1152]{1,0:T(8,128)(2,1)S(1)}, bf16[256,4096]{1,0:T(8,128)(2,1)}) custom-call(bf16[128,1024]{1,0:T(8,128)(2,1)S(1)} %bitcast.20, bf16[784,4096]{1,0:T(8,128)(2,1)S(1)} %get-tuple-element.19.tf_ref, bf16[64,4,4096]{2,1,0:T(4,128)(2,1)} %bitcast.28, bf16[64,64]{1,0:T(8,128)(2,1)S(1)} %copy-done.2, f32[1,64]{1,0:T(1,128)S(1)} %bitcast.26), custom_call_target="tpu_custom_call" | custom-call | tf_op jit(solution)/shard_map/delta/pallas_call | solution.py:542
  40.4 10.9 %all_to_all.27 = bf16[16,8,1152]{2,1,0:T(8,128)(2,1)S(1)} all-to-all(bf16[16,8,1152]{2,1,0:T(8,128)(2,1)S(1)} %bitcast.23), channel_id=1, replica_groups=mesh['dp'=16,'slab'=16] {'slab'}, dimensions={0} | all-to-all | bytes 589824 | tf_op jit(solution)/shard_map/all_to_all | solution.py:564
  51.3 0.0 copy-done.1
  51.3 0.0 copy-done.5
  51.3 0.0 copy-start
  51.3 1.6 %adjoint.1 = (bf16[128,1152]{1,0:T(8,128)(2,1)S(1)}, bf16[128,512]{1,0:T(8,128)(2,1)S(1)}) custom-call(bf16[128,1152]{1,0:T(8,128)(2,1)S(1)} %bitcast.18, bf16[64,1024]{1,0:T(8,128)(2,1)S(1)} %get-tuple-element.21.m_ref, bf16[16,16,64,128]{3,2,1,0:T(8,128)(2,1)S(1)} %get-tuple-element.17.w_ref, bf16[64,128]{1,0:T(8,128)(2,1)S(1)} %copy-done.3, ...), custom_call_target="tpu_custom_call" | custom-call | tf_op jit(solution)/shard_map/adjoint/pallas_call | solution.py:542
  52.9 11.0 %all_to_all.28 = bf16[16,8,1152]{2,1,0:T(8,128)(2,1)S(1)} all-to-all(bf16[16,8,1152]{2,1,0:T(8,128)(2,1)S(1)} %bitcast.22), channel_id=1, replica_groups=mesh['dp'=16,'slab'=16] {'slab'}, dimensions={0} | all-to-all | bytes 589824 | tf_op jit(solution)/shard_map/all_to_all | solution.py:564
  63.9 0.9 %assemble.1 = bf16[128,1152]{1,0:T(8,128)(2,1)} custom-call(bf16[128,1152]{1,0:T(8,128)(2,1)S(1)} %bitcast.16, bf16[128,512]{1,0:T(8,128)(2,1)S(1)} %get-tuple-element.24.part_ref), custom_call_target="tpu_custom_call" | custom-call | tf_op jit(solution)/shard_map/assemble/pallas_call | solution.py:542
  64.8 9.8 %all-to-all-start.4 = ((bf16[16,8,1152]{2,1,0:T(8,128)(2,1)}), bf16[16,8,1152]{2,1,0:T(8,128)(2,1)S(1)}, u32[]{:S(2)}, u32[]{:S(2)}) async-start(bf16[16,8,1152]{2,1,0:T(8,128)(2,1)} %bitcast.12), calls=%async_computation.4 | async-start | bytes 589824 | tf_op jit(solution)/shard_map/all_to_all | solution.py:564
  74.7 0.0 copy-start.4
  74.7 4.5 %input_grad.1 = bf16[64,4,4096]{2,1,0:T(4,128)(2,1)} custom-call(bf16[128,1152]{1,0:T(8,128)(2,1)S(1)} %bitcast.17, bf16[256,4096]{1,0:T(8,128)(2,1)} %get-tuple-element.23.d_hbm, bf16[64,64]{1,0:T(8,128)(2,1)S(1)} %copy-done.2, f32[160,128]{1,0:T(8,128)S(1)} %copy-done), custom_call_target="tpu_custom_call" | custom-call | tf_op jit(solution)/shard_map/input_grad/pallas_call | solution.py:542
  79.2 7.8 %all-to-all-done.4 = bf16[16,8,1152]{2,1,0:T(8,128)(2,1)S(1)} async-done(((bf16[16,8,1152]{2,1,0:T(8,128)(2,1)}), bf16[16,8,1152]{2,1,0:T(8,128)(2,1)S(1)}, u32[]{:S(2)}, u32[]{:S(2)}) %all-to-all-start.4) | async-done | bytes 294944 | tf_op jit(solution)/shard_map/all_to_all | solution.py:564
  87.0 1.6 %weight_grad.1 = (f32[16,64,128]{2,1,0:T(8,128)}, f32[64,64]{1,0:T(8,128)}, f32[1,64]{1,0:T(1,128)}) custom-call(bf16[128,1152]{1,0:T(8,128)(2,1)S(1)} %bitcast.19, bf16[6,32,128]{2,1,0:T(8,128)(2,1)S(1)} %copy-done.4), custom_call_target="tpu_custom_call" | custom-call | tf_op jit(solution)/shard_map/weight_grad/pallas_call | solution.py:542
  (7 shorter events, 0.0 us)
Async XLA Ops:
  0.6 19.2 %copy-start.3 = (bf16[64,128]{1,0:T(8,128)(2,1)S(1)}, bf16[64,128]{1,0:T(8,128)(2,1)}, u32[]{:S(2)}) copy-start(bf16[64,128]{1,0:T(8,128)(2,1)} %constant.14.clone.fx_ref) | copy-start | bytes 49156
  0.6 19.2 %copy-start.6 = (bf16[128,64]{1,0:T(8,128)(2,1)S(1)}, bf16[128,64]{1,0:T(8,128)(2,1)}, u32[]{:S(2)}) copy-start(bf16[128,64]{1,0:T(8,128)(2,1)} %constant.16.clone.iv_ref) | copy-start | bytes 49156
  19.9 11.6 %copy-start.2 = (bf16[64,64]{1,0:T(8,128)(2,1)S(1)}, bf16[64,64]{1,0:T(8,128)(2,1)}, u32[]{:S(2)}) copy-start(bf16[64,64]{1,0:T(8,128)(2,1)} %w_ref.3) | copy-start | bytes 24580
  19.9 11.6 %copy-start.8 = (f32[64]{0:T(128)S(1)}, f32[64]{0:T(128)}, u32[]{:S(2)}) copy-start(f32[64]{0:T(128)} %param.16) | copy-start | bytes 772
  31.5 19.8 %copy-start.1 = (bf16[2,128,128]{2,1,0:T(8,128)(2,1)S(1)}, bf16[2,128,128]{2,1,0:T(8,128)(2,1)}, u32[]{:S(2)}) copy-start(bf16[2,128,128]{2,1,0:T(8,128)(2,1)} %constant.18.clone.gather_ref) | copy-start | bytes 196612
  31.5 19.8 %copy-start.5 = (bf16[128,64]{1,0:T(8,128)(2,1)S(1)}, bf16[128,64]{1,0:T(8,128)(2,1)}, u32[]{:S(2)}) copy-start(bf16[128,64]{1,0:T(8,128)(2,1)} %constant.17.clone.ia_ref) | copy-start | bytes 49156
  31.5 19.8 %copy-start.7 = (bf16[64,128]{1,0:T(8,128)(2,1)S(1)}, bf16[64,128]{1,0:T(8,128)(2,1)}, u32[]{:S(2)}) copy-start(bf16[64,128]{1,0:T(8,128)(2,1)} %constant.15.clone.fo_ref) | copy-start | bytes 49156
  51.3 23.4 %copy-start = (f32[160,128]{1,0:T(8,128)S(1)}, f32[160,128]{1,0:T(8,128)}, u32[]{:S(2)}) copy-start(f32[160,128]{1,0:T(8,128)} %constant.20.clone.phase_hbm.phase_ref) | copy-start | bytes 245764
  64.8 22.2 %all-to-all-start.4 = ((bf16[16,8,1152]{2,1,0:T(8,128)(2,1)}), bf16[16,8,1152]{2,1,0:T(8,128)(2,1)S(1)}, u32[]{:S(2)}, u32[]{:S(2)}) async-start(bf16[16,8,1152]{2,1,0:T(8,128)(2,1)} %bitcast.12), calls=%async_computation.4 | async-start | bytes 589824 | tf_op jit(solution)/shard_map/all_to_all | solution.py:564
  74.7 12.3 %copy-start.4 = (bf16[6,32,128]{2,1,0:T(8,128)(2,1)S(1)}, bf16[6,32,128]{2,1,0:T(8,128)(2,1)}, u32[]{:S(2)}) copy-start(bf16[6,32,128]{2,1,0:T(8,128)(2,1)} %constant.19.clone.pick_ref) | copy-start | bytes 147460
